TPU v7x, 256 devices: a whole 4x4x8 slice. The times are simulated.
256 devices in a mesh: role: 2 (over core), dev: 64 (over x_hi, y, z), head: 2 (over x_lo).
Axes of the slice: x: 4 (x_hi: 2, x_lo: 2; x = x_hi * 2 + x_lo), y: 4, z: 8, core: 2. Of those that a mesh axis runs over, the one named last changes fastest.
Arguments:
- hidden: bfloat16 [2048, 4096], P(('role', 'dev', 'head')), may hold values from -6 to 6
- queries: bfloat16 [2048, 64, 128], P(('role', 'dev'), 'head'), as said below
- cache_keys: bfloat16 [2048, 128, 4, 128], P(('role', 'dev'), None, 'head'), as said below
- cache_values: bfloat16 [2048, 128, 4, 128], P(('role', 'dev'), None, 'head'), may hold values from -6 to 6
- new_keys: bfloat16 [2048, 4, 128], P(('role', 'dev'), 'head'), may hold values from -6 to 6
- new_values: bfloat16 [2048, 4, 128], P(('role', 'dev'), 'head'), may hold values from -6 to 6
- lengths: int32 [2048], P(('role', 'dev')), may hold values from 32 to 128, as said below
- out_proj: bfloat16 [8192, 4096], P('head', 'dev'), may hold values from -0.5 to 0.5
- norm_gain: float32 [4096], replicated, may hold values from 0.1 to 1.9
- expert_gate: bfloat16 [128, 4096, 768], P(('role', 'dev'), None, 'head'), may hold values from -0.09375 to 0.09375
- expert_up: bfloat16 [128, 4096, 768], P(('role', 'dev'), None, 'head'), may hold values from -0.09375 to 0.09375
- expert_down: bfloat16 [128, 768, 4096], P(('role', 'dev'), 'head'), may hold values from -0.21875 to 0.21875
- expert_ids: int32 [2048, 8], P(('role', 'dev', 'head')), may hold values from 0 to 127, all different within a row; in each aligned block of 8 rows (0 to 7, 8 to 15, ...) at most 2 rows name the same one
- gate_levels: int32 [2048, 8], P(('role', 'dev', 'head')), may hold values from 1 to 255
Outputs:
- layer_out: bfloat16 [2048, 4096], P(('role', 'dev', 'head'))
Inputs may be any that keep to these rules, and one draw needn't show every extreme that they name: `queries`: query vectors of the new tokens. `cache_keys`: cached keys of the requests. `lengths`: the first request of each block of 16 rows holds 128 positions and the second holds 32. `expert_ids`: each row names 8 different experts; among the 8 rows of one device no expert is named more than 2 times, a bound that some block reaches.
All inputs are finite; a program needn't handle non-finite values.
Results may differ from a plain program's by a relative error of at most 0.0065.
Values may be sent and summed in bfloat16 or wider, within the bound.
No kernel may reach another device: no remote copies, remote signals or barrier semaphores. Data moves between devices by JAX's collectives and lax.ppermute only.
A program may use at most 64 MiB of HBM per device.

v0:
```python
import math

import jax
import jax.numpy as jnp
from jax import lax
from jax.sharding import PartitionSpec as P


def attend_block(query_rows, key_rows, value_rows, key_new, value_new, valid_len):
    row_count = query_rows.shape[0]
    kv_heads = key_rows.shape[2]
    group_size = query_rows.shape[1] // kv_heads
    head_dim = query_rows.shape[2]
    scaling = 1.0 / math.sqrt(head_dim)
    query_f = query_rows.astype(jnp.float32).reshape(row_count, kv_heads, group_size, head_dim)
    scores = jnp.einsum("bhgd,bthd->bhgt", query_f, key_rows.astype(jnp.float32)) * scaling
    scores_new = jnp.einsum("bhgd,bhd->bhg", query_f, key_new.astype(jnp.float32)) * scaling
    positions = jnp.arange(key_rows.shape[1], dtype=jnp.int32)
    usable = (positions[None, :] < valid_len[:, None])[:, None, None, :]
    masked = jnp.where(usable, scores, -1e30)
    highest = jnp.maximum(jnp.max(masked, axis=-1), scores_new)
    exp_terms = jnp.exp(masked - highest[..., None])
    exp_new = jnp.exp(scores_new - highest)
    totals = jnp.sum(exp_terms, axis=-1) + exp_new
    weights = (exp_terms / totals[..., None]).astype(jnp.bfloat16)
    weight_new = (exp_new / totals).astype(jnp.bfloat16)
    blended = jnp.einsum("bhgt,bthd->bhgd", weights, value_rows, preferred_element_type=jnp.float32)
    blended = (
        blended
        + weight_new.astype(jnp.float32)[..., None] * value_new.astype(jnp.float32)[:, :, None, :]
    )
    return blended.astype(jnp.bfloat16).reshape(row_count, kv_heads * group_size * head_dim)


def expert_rows(rows_in, gate_w, up_w, down_w):
    gate_part = jnp.dot(rows_in, gate_w, preferred_element_type=jnp.float32)
    up_part = jnp.dot(rows_in, up_w, preferred_element_type=jnp.float32)
    active = (jax.nn.silu(gate_part) * up_part).astype(jnp.bfloat16)
    return jnp.dot(active, down_w, preferred_element_type=jnp.float32)


def slot_ranks(flat_ids, experts):
    one_hot = (flat_ids[:, None] == jnp.arange(experts, dtype=jnp.int32)[None, :]).astype(jnp.int32)
    return jnp.sum(jnp.cumsum(one_hot, axis=0) * one_hot, axis=1) - 1


def on_device(
    hidden,
    queries,
    cache_keys,
    cache_values,
    new_keys,
    new_values,
    lengths,
    out_proj,
    norm_gain,
    expert_gate,
    expert_up,
    expert_down,
    expert_ids,
    gate_levels,
):
    attended = attend_block(queries, cache_keys, cache_values, new_keys, new_values, lengths)
    columns = jnp.dot(
        lax.all_gather(attended, "dev", axis=0, tiled=True),
        out_proj,
        preferred_element_type=jnp.float32,
    )
    dev_count = lax.axis_size("dev")
    head_count = lax.axis_size("head")
    experts = lax.axis_size("role") * dev_count
    col_width = out_proj.shape[1]
    width = dev_count * col_width
    projected = lax.all_to_all(columns, ("dev", "head"), split_axis=0, concat_axis=1, tiled=True)
    tokens = projected.shape[0]
    summed = jnp.sum(projected.reshape(tokens, dev_count, head_count, col_width), axis=2).reshape(
        tokens, width
    )
    residual = hidden.astype(jnp.float32) + summed
    normed = (
        residual
        * lax.rsqrt(jnp.mean(residual * residual, axis=-1, keepdims=True) + 1e-06)
        * norm_gain
    ).astype(jnp.bfloat16)
    top_k = expert_ids.shape[1]
    capacity = max(2, 2 * tokens * top_k // experts)
    own_ids = expert_ids.reshape(-1)
    own_ranks = slot_ranks(own_ids, experts)
    pair_rows, pair_ids = (
        lax.all_gather(normed, "head", axis=0, tiled=True),
        lax.all_gather(expert_ids, "head", axis=0, tiled=True),
    )
    pair_flat = pair_ids.reshape(head_count, tokens * top_k)
    pair_ranks = jax.vmap(lambda id_row: slot_ranks(id_row, experts))(pair_flat)
    pair_ranks = pair_ranks + capacity * jnp.arange(head_count, dtype=jnp.int32)[:, None]
    rows_from = jnp.arange(head_count * tokens * top_k, dtype=jnp.int32) // top_k
    outgoing = (
        jnp.zeros((experts, head_count * capacity, width), jnp.bfloat16)
        .at[pair_flat.reshape(-1), pair_ranks.reshape(-1)]
        .set(pair_rows[rows_from])
    )
    incoming = lax.all_to_all(outgoing, ("role", "dev"), split_axis=0, concat_axis=0, tiled=True)
    sources = incoming.shape[0]
    slot_total = incoming.shape[1]
    partial_value = expert_rows(
        incoming.reshape(sources * slot_total, width), expert_gate[0], expert_up[0], expert_down[0]
    )
    partial_value = partial_value.reshape(sources, slot_total, width).astype(jnp.bfloat16)
    arrived = lax.all_to_all(
        partial_value, ("role", "dev"), split_axis=0, concat_axis=0, tiled=True
    )
    arrived = (
        lax.psum_scatter(arrived, "head", scatter_dimension=1, tiled=True)
        .astype(jnp.float32)
        .astype(jnp.bfloat16)
    )
    picked = arrived[own_ids, own_ranks].astype(jnp.float32).reshape(tokens, top_k, width)
    levels = gate_levels.astype(jnp.float32)
    shares = levels / jnp.sum(levels, axis=1, keepdims=True)
    return (residual + jnp.sum(shares[..., None] * picked, axis=1)).astype(jnp.bfloat16)


def solution(mesh):
    placed = (
        P(("role", "dev", "head"), None),
        P(("role", "dev"), "head", None),
        P(("role", "dev"), None, "head", None),
        P(("role", "dev"), None, "head", None),
        P(("role", "dev"), "head", None),
        P(("role", "dev"), "head", None),
        P(("role", "dev")),
        P("head", "dev"),
        P(),
        P(("role", "dev"), None, "head"),
        P(("role", "dev"), None, "head"),
        P(("role", "dev"), "head", None),
        P(("role", "dev", "head"), None),
        P(("role", "dev", "head"), None),
    )
    return jax.shard_map(
        on_device,
        mesh=mesh,
        in_specs=placed,
        out_specs=P(("role", "dev", "head"), None),
        check_vma=False,
    )
```

profile of v0, /device:TPU:1, one launch (start us, length us, event | category | flops | bytes accessed | tf_op | source)
XLA Modules:
  0.0 561.0 jit_solution(16563779175409254275)
XLA Ops:
  8.6 2.1 fusion.34
  14.1 3.7 all_gather.10
  18.3 148.0 %all-gather.2.cloned.1.call-done = bf16[1024,4096]{1,0:T(8,128)(2,1)} async-done(((bf16[16,4096]{1,0:T(8,128)(2,1)}), bf16[1024,4096]{1,0:T(8,128)(2,1)}) %all-gather.2.cloned.1.call-update) | async-done | bytes 8388624 | tf_op jit(solution)/shard_map/all_gather | solution.py:65
  166.3 6.6 %convolution_bitcast_fusion = f32[128,8,64]{2,1,0:T(8,128)} fusion(bf16[1024,4096]{1,0:T(8,128)(2,1)} %all-gather.2.cloned.1.call-done, bf16[4096,64]{0,1:T(8,128)(2,1)} %param.21), kind=kOutput, calls=%fused_computation.11 | convolution fusion | flops 536870912 | bytes 9175040 | tf_op jit(solution)/shard_map/dot_general | solution.py:64
  172.9 2.1 reshape.251
  175.0 9.4 %all-to-all-start = ((f32[128,1,512]{2,1,0:T(1,128)}), f32[128,1,512]{2,1,0:T(1,128)S(1)}, u32[]{:S(2)}, u32[]{:S(2)}) async-start(f32[128,1,512]{2,1,0:T(1,128)} %reshape.251), calls=%async_computation | async-start | bytes 524288 | tf_op jit(solution)/shard_map/all_to_all | solution.py:74
  184.8 11.2 %all-to-all-done = f32[128,1,512]{2,1,0:T(1,128)S(1)} async-done(((f32[128,1,512]{2,1,0:T(1,128)}), f32[128,1,512]{2,1,0:T(1,128)S(1)}, u32[]{:S(2)}, u32[]{:S(2)}) %all-to-all-start) | async-done | bytes 262176 | tf_op jit(solution)/shard_map/all_to_all | solution.py:74
  197.2 2.2 reduce
  203.6 3.8 all_gather.11
  207.4 2.2 gather_fusion
  209.5 4.0 broadcast_in_dim.16
  213.6 32.4 %scatter_fusion = bf16[128,4,4096]{2,1,0:T(4,128)(2,1)} fusion(bf16[128,4,4096]{2,1,0:T(4,128)(2,1)} %broadcast_in_dim.16, s32[128]{0:T(128)S(1)} %fusion.32, bf16[128,4096]{1,0:T(8,128)(2,1)} %gather_fusion), kind=kCustom, calls=%fused_computation.2 | custom fusion | bytes 3146752 | tf_op jit(solution)/shard_map/scatter | solution.py:100
  245.9 112.3 %all_to_all.26 = bf16[128,4,4096]{2,1,0:T(4,128)(2,1)} all-to-all(bf16[128,4,4096]{2,1,0:T(4,128)(2,1)} %scatter_fusion), channel_id=1, replica_groups=mesh['role'=2,'dev'=64,'head'=2] {'role','dev'}, dimensions={0} | all-to-all | bytes 8388608 | tf_op jit(solution)/shard_map/all_to_all | solution.py:102
  358.3 6.9 %reshape.225 = bf16[512,4096]{1,0:T(8,128)(2,1)} reshape(bf16[128,4,4096]{2,1,0:T(4,128)(2,1)} %all_to_all.26) | data formatting | bytes 8388608 | tf_op jit(solution)/shard_map/reshape | solution.py:106
  365.2 5.6 %fusion.3 = f32[512,384]{1,0:T(8,128)S(1)} fusion(bf16[512,4096]{1,0:T(8,128)(2,1)} %reshape.225, bf16[1,4096,384]{2,1,0:T(8,128)(2,1)} %param.23), kind=kOutput, calls=%fused_computation.7 | convolution fusion | flops 1610612736 | bytes 8126464 | tf_op jit(solution)/shard_map/dot_general | solution.py:36
  370.9 3.1 fusion.8
  373.9 1.8 dot_general.29
  375.8 3.3 convolution_convert_fusion
  379.1 3.2 copy.35
  382.4 104.9 %all_to_all.27 = bf16[128,4,4096]{2,1,0:T(4,128)(2,1)S(1)} all-to-all(bf16[128,4,4096]{2,1,0:T(4,128)(2,1)S(1)} %copy.35), channel_id=1, replica_groups=mesh['role'=2,'dev'=64,'head'=2] {'role','dev'}, dimensions={0} | all-to-all | bytes 8388608 | tf_op jit(solution)/shard_map/all_to_all | solution.py:109
  487.3 4.2 copy.36
  492.6 50.9 %reduce-scatter.2.cloned.1.call-done = bf16[128,2,4096]{2,0,1:T(8,128)(2,1)} async-done(((bf16[128,4,4096]{2,0,1:T(8,128)(2,1)}), bf16[128,2,4096]{2,0,1:T(8,128)(2,1)}) %reduce-scatter.2.cloned.1.call-update) | async-done | bytes 2097168 | tf_op jit(solution)/shard_map/reduce_scatter | solution.py:113
  543.5 5.1 copy.37
  548.6 3.3 gather_fusion.1
  (57 shorter events, 14.8 us)
Async XLA Ops:
  6.5 369.2 %copy-start = (bf16[1,384,4096]{2,1,0:T(8,128)(2,1)S(1)}, bf16[1,384,4096]{2,1,0:T(8,128)(2,1)}, u32[]{:S(2)}) copy-start(bf16[1,384,4096]{2,1,0:T(8,128)(2,1)} %param.25) | copy-start | bytes 9437188
  6.5 7.6 %copy-start.4 = (s32[8,8]{1,0:T(8,128)S(1)}, s32[8,8]{1,0:T(8,128)}, u32[]{:S(2)}) copy-start(s32[8,8]{1,0:T(8,128)} %param.26) | copy-start | bytes 772
  6.5 159.8 %all-gather.2.cloned.1.call-start = ((), (), s32[]{:S(2)}) async-start(), calls=%async_computation.4 | async-start | bytes 8519680 | tf_op jit(solution)/shard_map/all_gather | solution.py:65
  172.9 30.4 %copy-start.3 = (bf16[8,4096]{1,0:T(8,128)(2,1)S(1)}, bf16[8,4096]{1,0:T(8,128)(2,1)}, u32[]{:S(2)}) copy-start(bf16[8,4096]{1,0:T(8,128)(2,1)} %param.14) | copy-start | bytes 196612
  172.9 30.6 %copy-start.5 = (f32[4096]{0:T(1024)S(1)}, f32[4096]{0:T(1024)}, u32[]{:S(2)}) copy-start(f32[4096]{0:T(1024)} %param.22) | copy-start | bytes 49156
  175.0 21.0 %all-to-all-start = ((f32[128,1,512]{2,1,0:T(1,128)}), f32[128,1,512]{2,1,0:T(1,128)S(1)}, u32[]{:S(2)}, u32[]{:S(2)}) async-start(f32[128,1,512]{2,1,0:T(1,128)} %reshape.251), calls=%async_computation | async-start | bytes 524288 | tf_op jit(solution)/shard_map/all_to_all | solution.py:74
  184.5 359.0 %reduce-scatter.2.cloned.1.call-start = ((), (), s32[]{:S(2)}) async-start(), calls=%async_computation.5 | async-start | bytes 6291456 | tf_op jit(solution)/shard_map/reduce_scatter | solution.py:113
  196.0 0.7 copy-start.2
  365.2 5.6 %copy-start.1 = (bf16[512,4096]{1,0:T(8,128)(2,1)S(1)}, bf16[512,4096]{1,0:T(8,128)(2,1)}, u32[]{:S(2)}) copy-start(bf16[512,4096]{1,0:T(8,128)(2,1)} %reshape.225) | copy-start | bytes 12582916
  365.2 5.6 %copy-start.7 = (bf16[1,4096,384]{2,1,0:T(8,128)(2,1)S(1)}, bf16[1,4096,384]{2,1,0:T(8,128)(2,1)}, u32[]{:S(2)}) copy-start(bf16[1,4096,384]{2,1,0:T(8,128)(2,1)} %param.24) | copy-start | bytes 9437188
  491.5 0.7 copy-start.6
Sparse Core Ops, SparseCore 0:
  14.3 152.0 all-gather.1
  491.7 51.7 reduce-scatter.1
where the time goes:
time: 562 us; the launch traced here: 561 us
  blocking collectives  225 us (40%)
  waiting for transfers between devices  210 us (37%)
  local copies, waits for them, and re-layouts  70.7 us (13%)
  matrix products  23.5 us (4%)
  between operations  13.6 us (2%)
  starting transfers between devices  9.48 us (2%)
  other arithmetic  8.69 us (2%)
    all_gather x1, waiting for transfers between devices, on_device(): lax.all_gather(attended, 'dev', axis=0, tiled=True)  148 us
    all_to_all x1, blocking collectives, on_device(): lax.all_to_all(outgoing, ('role', 'dev'), split_axis=0, concat_axis=0, ti...  112 us
    all_to_all x1, blocking collectives, on_device(): lax.all_to_all(partial_value, ('role', 'dev'), split_axis=0, concat_axis=...  105 us
    reduce_scatter x1, waiting for transfers between devices, on_device(): lax.psum_scatter(arrived, 'head', scatter_dimension=1, tiled=True)  50.9 us
    scatter x1, local copies, waits for them, and re-layouts, on_device(): outgoing = jnp.zeros((experts, head_count * capacity, width), jnp.bfloat1...  32.4 us
  transfers between devices with their start and end apart: 3, of which 3 were waited for; matrix products, arithmetic and copies ran while one was open for 0% of the time, Pallas kernels for 0%

commit v1 on v0

v1 whole, which is shorter than its diff:
```python
import math

import jax
import jax.numpy as jnp
from jax import lax
from jax.sharding import Mesh
from jax.sharding import PartitionSpec as P

AXES = ("role", "xh", "y", "zq", "zp", "head")
DEV = ("xh", "y", "zq", "zp")
EXPERT = ("role",) + DEV
ROWS_FROM = ("role", "xh", "y")
SUMS_TO = ("role", "xh", "y", "head")
NEAR = ("zq", "head")
FAR = ("role", "xh", "y", "zp")
CAP = 2


def attend_block(query_rows, key_rows, value_rows, key_new, value_new, valid_len):
    row_count = query_rows.shape[0]
    kv_heads = key_rows.shape[2]
    group_size = query_rows.shape[1] // kv_heads
    head_dim = query_rows.shape[2]
    scaling = 1.0 / math.sqrt(head_dim)
    query_f = query_rows.astype(jnp.float32).reshape(row_count, kv_heads, group_size, head_dim)
    scores = jnp.einsum("bhgd,bthd->bhgt", query_f, key_rows.astype(jnp.float32)) * scaling
    scores_new = jnp.einsum("bhgd,bhd->bhg", query_f, key_new.astype(jnp.float32)) * scaling
    positions = jnp.arange(key_rows.shape[1], dtype=jnp.int32)
    usable = (positions[None, :] < valid_len[:, None])[:, None, None, :]
    masked = jnp.where(usable, scores, -1e30)
    highest = jnp.maximum(jnp.max(masked, axis=-1), scores_new)
    exp_terms = jnp.exp(masked - highest[..., None])
    exp_new = jnp.exp(scores_new - highest)
    totals = jnp.sum(exp_terms, axis=-1) + exp_new
    weights = (exp_terms / totals[..., None]).astype(jnp.bfloat16)
    weight_new = (exp_new / totals).astype(jnp.bfloat16)
    blended = jnp.einsum("bhgt,bthd->bhgd", weights, value_rows, preferred_element_type=jnp.float32)
    blended = (
        blended
        + weight_new.astype(jnp.float32)[..., None] * value_new.astype(jnp.float32)[:, :, None, :]
    )
    return blended.astype(jnp.bfloat16).reshape(row_count, kv_heads * group_size * head_dim)


def swap(blocks, axes):
    return lax.all_to_all(blocks, axes, split_axis=0, concat_axis=0, tiled=True)


def project(attended, out_proj):
    rows, features = attended.shape
    half = features // 2
    role = lax.axis_index("role")
    own_weights = lax.dynamic_slice_in_dim(out_proj.T, role * half, half, axis=1)
    weights = lax.all_gather(own_weights, ("zq", "zp"), axis=0, tiled=True)
    near = lax.axis_size("xh") * lax.axis_size("y")
    halves = attended.reshape(rows, 2, half).transpose(1, 0, 2)
    sent = jnp.broadcast_to(halves[:, None], (2, near, rows, half)).reshape(2 * near, rows, half)
    gathered = swap(sent, ROWS_FROM).reshape(2 * near * rows, half)
    columns = lax.dot_general(
        gathered, weights, (((1,), (1,)), ((), ())), preferred_element_type=jnp.float32
    ).astype(jnp.bfloat16)
    tokens = rows // 2
    width = columns.shape[1]
    arrived = swap(columns.reshape(4 * near, tokens, width), SUMS_TO)
    summed = jnp.sum(arrived.reshape(2, near, 2, tokens, width).astype(jnp.float32), axis=(0, 2))
    return summed.transpose(1, 0, 2).reshape(tokens, near * width)


def slot_tables(ids, levels):
    blocks, tokens, top_k = ids.shape
    far = [lax.axis_size(name) for name in FAR]
    place = jnp.arange(math.prod(far), dtype=jnp.int32)
    pair = place % far[3]
    y_at = place // far[3] % far[2]
    x_at = place // (far[3] * far[2]) % far[1]
    role_at = place // (far[3] * far[2] * far[1])
    quad = lax.axis_size("zq")
    expert = (
        ((role_at * far[1] + x_at) * far[2] + y_at) * quad + lax.axis_index("zq")
    ) * far[3] + pair
    values = levels.astype(jnp.float32)
    shares = values / jnp.sum(values, axis=-1, keepdims=True)
    hits = (ids[None] == expert[:, None, None, None]).astype(jnp.float32)
    named = jnp.sum(hits, axis=-1)
    share = jnp.sum(hits * shares[None], axis=-1)
    earlier = jnp.cumsum(named, axis=2) - named
    slot = jnp.arange(CAP, dtype=jnp.float32)
    chosen = (earlier[:, :, None] == slot[:, None]) & (named[:, :, None] > 0)
    same = jnp.arange(blocks)[:, None] == jnp.arange(blocks)[None]
    picks = (chosen[:, :, :, None] & same[:, None, :, None]).reshape(
        len(place) * blocks * CAP, blocks * tokens
    )
    scaled = jnp.where(
        chosen[:, :, :, None] & same[:, None, :, None], share[:, :, None, None], 0.0
    ).reshape(len(place) * blocks * CAP, blocks * tokens)
    return picks.astype(jnp.bfloat16), scaled


def on_device(
    hidden,
    queries,
    cache_keys,
    cache_values,
    new_keys,
    new_values,
    lengths,
    out_proj,
    norm_gain,
    expert_gate,
    expert_up,
    expert_down,
    expert_ids,
    gate_levels,
):
    tokens, width = hidden.shape
    near = lax.axis_size("zq") * lax.axis_size("head")
    far = math.prod(lax.axis_size(name) for name in FAR)
    choices = lax.all_gather(jnp.stack([expert_ids, gate_levels]), NEAR, axis=0)
    picks, scaled = slot_tables(choices[:, 0], choices[:, 1])
    high = scaled.astype(jnp.bfloat16)
    low = (scaled - high.astype(jnp.float32)).astype(jnp.bfloat16)

    attended = attend_block(queries, cache_keys, cache_values, new_keys, new_values, lengths)
    residual = hidden.astype(jnp.float32) + project(attended, out_proj)
    normed = (
        residual
        * lax.rsqrt(jnp.mean(residual * residual, axis=-1, keepdims=True) + 1e-06)
        * norm_gain
    ).astype(jnp.bfloat16)

    pool = swap(jnp.broadcast_to(normed[None], (near, tokens, width)), NEAR)
    outgoing = jnp.dot(
        picks, pool.reshape(near * tokens, width), preferred_element_type=jnp.float32
    ).astype(jnp.bfloat16)
    slots = near * CAP
    incoming = swap(outgoing.reshape(far, slots, width), FAR).reshape(far * slots, width)
    gate_part = jnp.dot(incoming, expert_gate[0], preferred_element_type=jnp.float32)
    up_part = jnp.dot(incoming, expert_up[0], preferred_element_type=jnp.float32)
    active = (jax.nn.silu(gate_part) * up_part).astype(jnp.bfloat16)
    half_out = jnp.dot(active, expert_down[0], preferred_element_type=jnp.float32).astype(
        jnp.bfloat16
    )
    returned = swap(half_out.reshape(far, slots, width), FAR).reshape(far * slots, width)
    over_slots = (((0,), (0,)), ((), ()))
    mixed = lax.dot_general(high, returned, over_slots, preferred_element_type=jnp.float32)
    mixed = mixed + lax.dot_general(low, returned, over_slots, preferred_element_type=jnp.float32)
    parts = swap(mixed.astype(jnp.bfloat16).reshape(near, tokens, width), NEAR)
    mixture = jnp.sum(parts.astype(jnp.float32), axis=0)
    return (residual + mixture).astype(jnp.bfloat16)


def solution(mesh):
    fine = Mesh(mesh.devices.reshape(2, 2, 4, 4, 2, 2), AXES)
    token = EXPERT + ("head",)
    placed = (
        P(token, None),
        P(EXPERT, "head", None),
        P(EXPERT, None, "head", None),
        P(EXPERT, None, "head", None),
        P(EXPERT, "head", None),
        P(EXPERT, "head", None),
        P(EXPERT),
        P("head", DEV),
        P(),
        P(EXPERT, None, "head"),
        P(EXPERT, None, "head"),
        P(EXPERT, "head", None),
        P(token, None),
        P(token, None),
    )
    return jax.shard_map(
        on_device,
        mesh=fine,
        in_specs=placed,
        out_specs=P(token, None),
        check_vma=False,
    )
```

time: 562 us -> 292 us (0.52)
  the two profiles are of different devices: /device:TPU:1 before, /device:TPU:10 now
where the time goes in v1:
time: 292 us; the launch traced here: 291 us
  blocking collectives  117 us (40%)
  waiting for transfers between devices  73.1 us (25%)
  matrix products  29.7 us (10%)
  starting transfers between devices  28.7 us (10%)
  local copies, waits for them, and re-layouts  15.3 us (5%)
  between operations  13.6 us (5%)
  other arithmetic  13.4 us (5%)
    all_to_all x2, blocking collectives, swap(): return lax.all_to_all(blocks, axes, split_axis=0, concat_axis=0, tiled=True)  75.9 us
    all_to_all x4, waiting for transfers between devices, swap(): return lax.all_to_all(blocks, axes, split_axis=0, concat_axis=0, tiled=True)  73.1 us
    all_gather x1, blocking collectives, on_device(): choices = lax.all_gather(jnp.stack([expert_ids, gate_levels]), NEAR, axis=0)  41.3 us
    all_to_all x4, starting transfers between devices, swap(): return lax.all_to_all(blocks, axes, split_axis=0, concat_axis=0, tiled=True)  28.7 us
    dot_general x1, matrix products, on_device(): jnp.dot(active, expert_down[0], preferred_element_type=jnp.float32)  9.72 us
  transfers between devices with their start and end apart: 5, of which 3 were waited for; matrix products, arithmetic and copies ran while one was open for 9% of the time, Pallas kernels for 0%

profile of v1, /device:TPU:10, one launch (start us, length us, event | category | flops | bytes accessed | tf_op | source)
XLA Modules:
  0.0 291.2 jit_solution(1121215996445329002)
XLA Ops:
  6.5 1.8 dynamic-slice_bitcast_fusion
  10.9 2.1 fusion.45
  13.3 1.7 fusion.16
  16.2 6.6 %all-to-all-start = ((bf16[16,16,2048]{2,1,0:T(8,128)(2,1)}), bf16[16,16,2048]{2,1,0:T(8,128)(2,1)}, u32[]{:S(2)}, u32[]{:S(2)}) async-start(bf16[16,16,2048]{2,1,0:T(8,128)(2,1)} %bitcast.70), calls=%async_computation | async-start | bytes 2097152 | tf_op jit(solution)/shard_map/all_to_all | solution.py:46
  22.9 41.3 %all-gather = s32[16,8,8]{2,1,0:T(8,128)S(1)} all-gather(s32[2,8,8]{2,1,0:T(8,128)S(1)} %pad_add_fusion), channel_id=2, replica_groups=mesh['role'=2,'xh'=2,'y'=4,'zq'=4,'zp'=2,'head'=2] {'zq','head'}, dimensions={0}, use_global_device_ids=true | all-gather | bytes 4608 | tf_op jit(solution)/shard_map/all_gather | solution.py:118
  65.5 3.4 %fusion.14 = bf16[32,8,512]{2,1,0:T(8,128)(2,1)} fusion(bf16[256,2048]{1,0:T(8,128)(2,1)} %bitcast.6, bf16[512,2048]{1,0:T(8,128)(2,1)} %all-gather.3.cloned.1.call-done), kind=kOutput, calls=%fused_computation.16 | convolution fusion | flops 537001984 | bytes 3407872 | tf_op jit(solution)/shard_map/dot_general | solution.py:59
  68.9 8.0 %all-to-all-start.1 = ((bf16[32,8,512]{2,1,0:T(8,128)(2,1)}), bf16[32,8,512]{2,1,0:T(8,128)(2,1)S(1)}, u32[]{:S(2)}, u32[]{:S(2)}) async-start(bf16[32,8,512]{2,1,0:T(8,128)(2,1)} %fusion.14), calls=%async_computation.1 | async-start | bytes 524288 | tf_op jit(solution)/shard_map/all_to_all | solution.py:46
  78.7 5.0 %all-to-all-done.1 = bf16[32,8,512]{2,1,0:T(8,128)(2,1)S(1)} async-done(((bf16[32,8,512]{2,1,0:T(8,128)(2,1)}), bf16[32,8,512]{2,1,0:T(8,128)(2,1)S(1)}, u32[]{:S(2)}, u32[]{:S(2)}) %all-to-all-start.1) | async-done | bytes 262176 | tf_op jit(solution)/shard_map/all_to_all | solution.py:46
  86.6 7.2 %all-to-all-start.2 = ((bf16[8,8,4096]{2,1,0:T(8,128)(2,1)}), bf16[8,8,4096]{2,1,0:T(8,128)(2,1)}, u32[]{:S(2)}, u32[]{:S(2)}) async-start(bf16[8,8,4096]{2,1,0:T(8,128)(2,1)} %broadcast_in_dim.33), calls=%async_computation.2 | async-start | bytes 1048576 | tf_op jit(solution)/shard_map/all_to_all | solution.py:46
  93.8 1.6 fusion.23
  98.6 1.9 and.141
  100.4 8.6 %all-to-all-done.2 = bf16[8,8,4096]{2,1,0:T(8,128)(2,1)} async-done(((bf16[8,8,4096]{2,1,0:T(8,128)(2,1)}), bf16[8,8,4096]{2,1,0:T(8,128)(2,1)}, u32[]{:S(2)}, u32[]{:S(2)}) %all-to-all-start.2) | async-done | bytes 524320 | tf_op jit(solution)/shard_map/all_to_all | solution.py:46
  109.0 2.3 convolution_convert_fusion.1
  111.3 58.0 %all_to_all.30 = bf16[32,16,4096]{2,1,0:T(8,128)(2,1)S(1)} all-to-all(bf16[32,16,4096]{2,1,0:T(8,128)(2,1)S(1)} %bitcast.66), channel_id=1, replica_groups=mesh['role'=2,'xh'=2,'y'=4,'zq'=4,'zp'=2,'head'=2] {'role','xh','y','zp'}, dimensions={0} | all-to-all | bytes 8388608 | tf_op jit(solution)/shard_map/all_to_all | solution.py:46
  169.3 2.0 copy-done.1
  171.3 3.3 %fusion.5 = f32[512,384]{1,0:T(8,128)} fusion(bf16[512,4096]{1,0:T(8,128)(2,1)S(1)} %bitcast.68, bf16[1,4096,384]{2,1,0:T(8,128)(2,1)S(1)} %copy-done.8), kind=kOutput, calls=%fused_computation.8 | convolution fusion | flops 1610612736 | bytes 8126464 | tf_op jit(solution)/shard_map/dot_general | solution.py:137
  174.6 9.7 %convolution_convert_fusion = bf16[512,4096]{1,0:T(8,128)(2,1)} fusion(bf16[1,384,4096]{2,1,0:T(8,128)(2,1)S(1)} %copy-done, bf16[512,4096]{1,0:T(8,128)(2,1)} %bitcast.69, bf16[1,4096,384]{2,1,0:T(8,128)(2,1)} %param.24, f32[512,384]{1,0:T(8,128)} %fusion.5), kind=kOutput, calls=%fused_computation | convolution fusion | flops 3224502272 | bytes 15466496 | tf_op jit(solution)/shard_map/dot_general | solution.py:140
  184.3 6.9 %all-to-all-start.4 = ((bf16[32,16,4096]{2,1,0:T(8,128)(2,1)}), bf16[32,16,4096]{2,1,0:T(8,128)(2,1)}, u32[]{:S(2)}, u32[]{:S(2)}) async-start(bf16[32,16,4096]{2,1,0:T(8,128)(2,1)} %bitcast.67), calls=%async_computation.4 | async-start | bytes 8388608 | tf_op jit(solution)/shard_map/all_to_all | solution.py:46
  193.7 2.6 convert_element_type.119
  197.9 2.0 convert_element_type.126
  199.9 59.5 %all-to-all-done.4 = bf16[32,16,4096]{2,1,0:T(8,128)(2,1)} async-done(((bf16[32,16,4096]{2,1,0:T(8,128)(2,1)}), bf16[32,16,4096]{2,1,0:T(8,128)(2,1)}, u32[]{:S(2)}, u32[]{:S(2)}) %all-to-all-start.4) | async-done | bytes 4194336 | tf_op jit(solution)/shard_map/all_to_all | solution.py:46
  259.4 3.1 %fusion.46 = f32[64,4096]{1,0:T(8,128)S(1)} fusion(bf16[512,64]{1,0:T(8,128)(2,1)} %convert_element_type.119, bf16[512,4096]{1,0:T(8,128)(2,1)} %bitcast.24), kind=kOutput, calls=%fused_computation.89 | convolution fusion | flops 268435456 | bytes 5308416 | tf_op jit(solution)/shard_map/dot_general | solution.py:145
  262.5 3.1 %fusion.1 = bf16[8,8,4096]{2,1,0:T(8,128)(2,1)S(1)} fusion(f32[64,4096]{1,0:T(8,128)S(1)} %fusion.46, bf16[512,64]{1,0:T(8,128)(2,1)S(1)} %convert_element_type.126, bf16[512,4096]{1,0:T(8,128)(2,1)} %bitcast.24), kind=kOutput, calls=%fused_computation.4 | convolution fusion | flops 268959744 | bytes 5832704 | tf_op jit(solution)/shard_map/dot_general | solution.py:146
  265.7 17.9 %all_to_all.31 = bf16[8,8,4096]{2,1,0:T(8,128)(2,1)S(1)} all-to-all(bf16[8,8,4096]{2,1,0:T(8,128)(2,1)S(1)} %fusion.1), channel_id=1, replica_groups=mesh['role'=2,'xh'=2,'y'=4,'zq'=4,'zp'=2,'head'=2] {'zq','head'}, dimensions={0} | all-to-all | bytes 1048576 | tf_op jit(solution)/shard_map/all_to_all | solution.py:46
  (53 shorter events, 17.9 us)
Async XLA Ops:
  6.5 168.0 %copy-start = (bf16[1,384,4096]{2,1,0:T(8,128)(2,1)S(1)}, bf16[1,384,4096]{2,1,0:T(8,128)(2,1)}, u32[]{:S(2)}) copy-start(bf16[1,384,4096]{2,1,0:T(8,128)(2,1)} %param.25) | copy-start | bytes 9437188
  6.5 59.0 %all-gather.3.cloned.1.call-start = ((), (), s32[]{:S(2)}) async-start(), calls=%async_computation.6 | async-start | bytes 2359296 | tf_op jit(solution)/shard_map/all_gather | solution.py:54
  13.3 9.5 %copy-start.6 = (s32[8,8]{1,0:T(8,128)S(1)}, s32[8,8]{1,0:T(8,128)}, u32[]{:S(2)}) copy-start(s32[8,8]{1,0:T(8,128)} %param.27) | copy-start | bytes 772
  13.3 9.5 %copy-start.7 = (s32[8,8]{1,0:T(8,128)S(1)}, s32[8,8]{1,0:T(8,128)}, u32[]{:S(2)}) copy-start(s32[8,8]{1,0:T(8,128)} %param.26) | copy-start | bytes 772
  16.2 69.2 %copy-start.3 = (bf16[8,4096]{1,0:T(8,128)(2,1)S(1)}, bf16[8,4096]{1,0:T(8,128)(2,1)}, u32[]{:S(2)}) copy-start(bf16[8,4096]{1,0:T(8,128)(2,1)} %param.14) | copy-start | bytes 196612
  16.2 69.4 %copy-start.5 = (f32[4096]{0:T(1024)S(1)}, f32[4096]{0:T(1024)}, u32[]{:S(2)}) copy-start(f32[4096]{0:T(1024)} %param.22) | copy-start | bytes 49156
  16.2 49.3 %all-to-all-start = ((bf16[16,16,2048]{2,1,0:T(8,128)(2,1)}), bf16[16,16,2048]{2,1,0:T(8,128)(2,1)}, u32[]{:S(2)}, u32[]{:S(2)}) async-start(bf16[16,16,2048]{2,1,0:T(8,128)(2,1)} %bitcast.70), calls=%async_computation | async-start | bytes 2097152 | tf_op jit(solution)/shard_map/all_to_all | solution.py:46
  68.9 14.9 %all-to-all-start.1 = ((bf16[32,8,512]{2,1,0:T(8,128)(2,1)}), bf16[32,8,512]{2,1,0:T(8,128)(2,1)S(1)}, u32[]{:S(2)}, u32[]{:S(2)}) async-start(bf16[32,8,512]{2,1,0:T(8,128)(2,1)} %fusion.14), calls=%async_computation.1 | async-start | bytes 524288 | tf_op jit(solution)/shard_map/all_to_all | solution.py:46
  83.8 0.7 copy-start.2
  86.6 22.5 %all-to-all-start.2 = ((bf16[8,8,4096]{2,1,0:T(8,128)(2,1)}), bf16[8,8,4096]{2,1,0:T(8,128)(2,1)}, u32[]{:S(2)}, u32[]{:S(2)}) async-start(bf16[8,8,4096]{2,1,0:T(8,128)(2,1)} %broadcast_in_dim.33), calls=%async_computation.2 | async-start | bytes 1048576 | tf_op jit(solution)/shard_map/all_to_all | solution.py:46
  111.3 60.0 %copy-start.8 = (bf16[1,4096,384]{2,1,0:T(8,128)(2,1)S(1)}, bf16[1,4096,384]{2,1,0:T(8,128)(2,1)}, u32[]{:S(2)}) copy-start(bf16[1,4096,384]{2,1,0:T(8,128)(2,1)} %param.23) | copy-start | bytes 9437188
  169.3 2.0 copy-start.1
  184.3 75.1 %all-to-all-start.4 = ((bf16[32,16,4096]{2,1,0:T(8,128)(2,1)}), bf16[32,16,4096]{2,1,0:T(8,128)(2,1)}, u32[]{:S(2)}, u32[]{:S(2)}) async-start(bf16[32,16,4096]{2,1,0:T(8,128)(2,1)} %bitcast.67), calls=%async_computation.4 | async-start | bytes 8388608 | tf_op jit(solution)/shard_map/all_to_all | solution.py:46
  262.5 21.1 %copy-start.4 = (bf16[8,4096]{1,0:T(8,128)(2,1)S(1)}, bf16[8,4096]{1,0:T(8,128)(2,1)}, u32[]{:S(2)}) copy-start(bf16[8,4096]{1,0:T(8,128)(2,1)} %param.14) | copy-start | bytes 196612
Sparse Core Ops, SparseCore 0:
  9.1 43.9 all-gather.2

commit v2 on v1

v2 whole, which is shorter than its diff:
```python
import math

import jax
import jax.numpy as jnp
from jax import lax
from jax.experimental import pallas as pl
from jax.experimental.pallas import tpu as pltpu
from jax.sharding import Mesh
from jax.sharding import PartitionSpec as P

AXES = ("role", "xh", "y", "zq", "zp", "head")
DEV = ("xh", "y", "zq", "zp")
EXPERT = ("role",) + DEV
ROWS_FROM = ("role", "xh", "zq")
SUMS_TO = ("role", "xh", "zq", "head")
NEAR = ("zq", "head")
FAR = ("role", "xh", "y", "zp")
CAP = 2
BLOCK = 8
SLOTS = 16
LANES = 128


def attend_block(query_rows, key_rows, value_rows, key_new, value_new, valid_len):
    row_count = query_rows.shape[0]
    kv_heads = key_rows.shape[2]
    group_size = query_rows.shape[1] // kv_heads
    head_dim = query_rows.shape[2]
    scaling = 1.0 / math.sqrt(head_dim)
    query_f = query_rows.astype(jnp.float32).reshape(row_count, kv_heads, group_size, head_dim)
    scores = jnp.einsum("bhgd,bthd->bhgt", query_f, key_rows.astype(jnp.float32)) * scaling
    scores_new = jnp.einsum("bhgd,bhd->bhg", query_f, key_new.astype(jnp.float32)) * scaling
    positions = jnp.arange(key_rows.shape[1], dtype=jnp.int32)
    usable = (positions[None, :] < valid_len[:, None])[:, None, None, :]
    masked = jnp.where(usable, scores, -1e30)
    highest = jnp.maximum(jnp.max(masked, axis=-1), scores_new)
    exp_terms = jnp.exp(masked - highest[..., None])
    exp_new = jnp.exp(scores_new - highest)
    totals = jnp.sum(exp_terms, axis=-1) + exp_new
    weights = (exp_terms / totals[..., None]).astype(jnp.bfloat16)
    weight_new = (exp_new / totals).astype(jnp.bfloat16)
    blended = jnp.einsum("bhgt,bthd->bhgd", weights, value_rows, preferred_element_type=jnp.float32)
    blended = (
        blended
        + weight_new.astype(jnp.float32)[..., None] * value_new.astype(jnp.float32)[:, :, None, :]
    )
    return blended.astype(jnp.bfloat16).reshape(row_count, kv_heads * group_size * head_dim)


def swap(blocks, axes):
    return lax.all_to_all(blocks, axes, split_axis=0, concat_axis=0, tiled=True)


def shift(block, axis, by):
    count = lax.axis_size(axis)
    return lax.ppermute(block, axis, [(at, (at + by) % count) for at in range(count)])


def call(kernel, out_shape, *operands, spaces=None):
    whole = pl.BlockSpec(memory_space=pltpu.VMEM)
    return pl.pallas_call(
        kernel,
        out_shape=out_shape,
        in_specs=[
            pl.BlockSpec(memory_space=pltpu.SMEM) if operand.dtype == jnp.int32 else whole
            for operand in operands
        ],
        out_specs=jax.tree.map(lambda _: whole, out_shape),
    )(*operands)


def project_kernel(at_ref, rows_ref, *refs):
    pieces, out_ref = refs[:-1], refs[-1]
    count = len(pieces)
    rows = rows_ref[...]
    for by, piece_ref in enumerate(pieces):
        width = piece_ref.shape[0]
        place = lax.rem(at_ref[0] - by + count, count)
        part = lax.dot_general(
            rows, piece_ref[...], (((1,), (1,)), ((), ())), preferred_element_type=jnp.float32
        )
        out_ref[:, pl.ds(pl.multiple_of(place * width, width), width)] = part.astype(jnp.bfloat16)


def norm_kernel(arrived_ref, hidden_ref, gain_ref, choices_ref, residual_ref, sent_ref):
    roles, halves, quads, heads, tokens, width = arrived_ref.shape
    rows = width // LANES
    total = jnp.zeros((tokens, LANES), jnp.float32)
    for x in range(halves):
        for q in range(quads):
            for y in range(rows):
                span = slice(y * LANES, (y + 1) * LANES)
                first = ((x * rows + y) * quads + q) * LANES
                to = slice(first, first + LANES)
                value = hidden_ref[:, to].astype(jnp.float32)
                for r in range(roles):
                    for h in range(heads):
                        value = value + arrived_ref[r, x, q, h, :, span].astype(jnp.float32)
                residual_ref[:, to] = value
                total = total + value * value
    count = residual_ref.shape[1]
    scale = lax.rsqrt(jnp.sum(total, axis=1, keepdims=True) / count + 1e-06)
    normed = (residual_ref[...] * scale * gain_ref[...]).astype(jnp.bfloat16)
    for copy in range(sent_ref.shape[0]):
        sent_ref[copy, :, :count] = normed
        sent_ref[copy, :, count:] = choices_ref[...]


def pick_kernel(top_k, quad_ref, choices_ref, pool_ref, out_ref, scaled_ref, picks):
    count, tokens = picks.shape

    @pl.when(pl.program_id(0) == 0)
    def _():
        table = choices_ref[...].astype(jnp.float32).T
        slot = lax.broadcasted_iota(jnp.int32, (count, tokens), 0)
        token = lax.broadcasted_iota(jnp.int32, (count, tokens), 1)
        place = slot // SLOTS
        expert = place // 2 * 8 + quad_ref[0] * 2 + place % 2
        expert = expert.astype(jnp.float32)
        levels = table[top_k : 2 * top_k]
        shares = levels / jnp.sum(levels, axis=0, keepdims=True)
        named = jnp.zeros((count, tokens), jnp.float32)
        share = jnp.zeros((count, tokens), jnp.float32)
        for at in range(top_k):
            hit = table[at : at + 1] == expert
            named = named + jnp.where(hit, 1.0, 0.0)
            share = share + jnp.where(hit, shares[at : at + 1], 0.0)
        row = lax.broadcasted_iota(jnp.int32, (tokens, tokens), 0)
        col = lax.broadcasted_iota(jnp.int32, (tokens, tokens), 1)
        before = jnp.where((row // BLOCK == col // BLOCK) & (row < col), 1.0, 0.0)
        earlier = jnp.dot(
            named.astype(jnp.bfloat16),
            before.astype(jnp.bfloat16),
            preferred_element_type=jnp.float32,
        )
        rank = (slot % CAP).astype(jnp.float32)
        chosen = (named > 0) & (earlier == rank) & (token // BLOCK == slot % SLOTS // CAP)
        picks[...] = jnp.where(chosen, 1.0, 0.0).astype(jnp.bfloat16)
        scaled_ref[...] = jnp.where(chosen, share, 0.0).astype(jnp.bfloat16)

    out_ref[...] = jnp.dot(
        picks[...], pool_ref[...], preferred_element_type=jnp.float32
    ).astype(jnp.bfloat16)


def pick_rows(pool, width, top_k):
    tokens = pool.shape[0]
    count = math.prod(lax.axis_size(name) for name in FAR) * SLOTS
    block = 1024
    quad = lax.axis_index("zq").astype(jnp.int32).reshape(1)
    return pl.pallas_call(
        lambda *refs: pick_kernel(top_k, *refs),
        out_shape=(
            jax.ShapeDtypeStruct((count, width), jnp.bfloat16),
            jax.ShapeDtypeStruct((count, tokens), jnp.bfloat16),
        ),
        grid=(width // block,),
        in_specs=[
            pl.BlockSpec(memory_space=pltpu.SMEM),
            pl.BlockSpec((tokens, LANES), lambda s: (0, width // LANES)),
            pl.BlockSpec((tokens, block), lambda s: (0, s)),
        ],
        out_specs=(
            pl.BlockSpec((count, block), lambda s: (0, s)),
            pl.BlockSpec((count, tokens), lambda s: (0, 0)),
        ),
        scratch_shapes=[pltpu.VMEM((count, tokens), jnp.bfloat16)],
        compiler_params=pltpu.CompilerParams(
            dimension_semantics=("arbitrary",), vmem_limit_bytes=16 << 20
        ),
    )(quad, pool, pool)


def ffn_kernel(unit_steps, rows_ref, gate_ref, up_ref, down_ref, out_ref, active):
    step = pl.program_id(0)

    @pl.when(step < unit_steps)
    def _():
        units = gate_ref.shape[1]
        both = jnp.dot(
            rows_ref[...],
            jnp.concatenate([gate_ref[...], up_ref[...]], axis=1),
            preferred_element_type=jnp.float32,
        )
        gated = jax.nn.silu(both[:, :units]) * both[:, units:]
        to = pl.ds(pl.multiple_of(step * units, units), units)
        active[:, to] = gated.astype(jnp.bfloat16)

    @pl.when(step >= unit_steps)
    def _():
        out_ref[...] = jnp.dot(
            active[...], down_ref[...], preferred_element_type=jnp.float32
        ).astype(jnp.bfloat16)


def expert_rows(rows, gate, up, down):
    count, width = rows.shape
    units = gate.shape[2]
    block, columns = LANES, 1024
    steps = units // block

    def early(step):
        return jnp.minimum(step, steps - 1)

    def late(step):
        return jnp.maximum(step - steps, 0)

    return pl.pallas_call(
        lambda *refs: ffn_kernel(steps, *refs),
        out_shape=jax.ShapeDtypeStruct((count, width), jnp.bfloat16),
        grid=(steps + width // columns,),
        in_specs=[
            pl.BlockSpec((count, width), lambda s: (0, 0), pipeline_mode=pl.Buffered(1)),
            pl.BlockSpec((None, width, block), lambda s: (0, 0, early(s))),
            pl.BlockSpec((None, width, block), lambda s: (0, 0, early(s))),
            pl.BlockSpec((None, units, columns), lambda s: (0, 0, late(s))),
        ],
        out_specs=pl.BlockSpec((count, columns), lambda s: (0, late(s))),
        scratch_shapes=[pltpu.VMEM((count, units), jnp.bfloat16)],
        compiler_params=pltpu.CompilerParams(
            dimension_semantics=("arbitrary",), vmem_limit_bytes=24 << 20
        ),
        cost_estimate=pl.CostEstimate(
            flops=6 * count * width * units,
            bytes_accessed=2 * (2 * count * width + 3 * width * units),
            transcendentals=count * units,
        ),
    )(rows, gate, up, down)


def weight_pair(out_proj):
    cols = out_proj.shape[1]
    half = out_proj.shape[0] // 2
    own = lax.dynamic_slice_in_dim(out_proj.T, lax.axis_index("role") * half, half, axis=1)
    other = shift(own, "zp", 1)
    first = lax.axis_index("zp") == 0
    pair = jnp.where(
        first, jnp.concatenate([own, other], axis=0), jnp.concatenate([other, own], axis=0)
    )
    return pair


def project(attended, pair):
    rows, features = attended.shape
    half = features // 2
    near = lax.axis_size("xh") * lax.axis_size("zq")
    halves = attended.reshape(rows, 2, half).transpose(1, 0, 2)
    sent = jnp.broadcast_to(halves[:, None], (2, near, rows, half)).reshape(2 * near, rows, half)
    sent, pair = lax.optimization_barrier((sent, pair))
    pieces = [pair] + [shift(pair, "y", by) for by in range(1, lax.axis_size("y"))]
    gathered = swap(sent, ROWS_FROM).reshape(2 * near * rows, half)
    width = len(pieces) * pieces[0].shape[0]
    columns = call(
        project_kernel,
        jax.ShapeDtypeStruct((2 * near * rows, width), jnp.bfloat16),
        lax.axis_index("y").astype(jnp.int32).reshape(1),
        gathered,
        *pieces,
    )
    return swap(columns.reshape(4 * near, rows // 2, width), SUMS_TO)


def on_device(
    hidden,
    queries,
    cache_keys,
    cache_values,
    new_keys,
    new_values,
    lengths,
    out_proj,
    norm_gain,
    expert_gate,
    expert_up,
    expert_down,
    expert_ids,
    gate_levels,
):
    tokens, width = hidden.shape
    top_k = expert_ids.shape[1]
    near = lax.axis_size("zq") * lax.axis_size("head")
    far = math.prod(lax.axis_size(name) for name in FAR)

    pair = weight_pair(out_proj)
    attended = attend_block(queries, cache_keys, cache_values, new_keys, new_values, lengths)
    arrived = project(attended, pair)
    choices = jnp.concatenate([expert_ids, gate_levels], axis=1).astype(jnp.bfloat16)
    choices = jnp.pad(choices, ((0, 0), (0, LANES - 2 * top_k)))
    residual, sent = call(
        norm_kernel,
        (
            jax.ShapeDtypeStruct((tokens, width), jnp.float32),
            jax.ShapeDtypeStruct((near, tokens, width + LANES), jnp.bfloat16),
        ),
        arrived.reshape([lax.axis_size(name) for name in SUMS_TO] + list(arrived.shape[1:])),
        hidden,
        norm_gain.reshape(1, width),
        choices,
    )

    pool = swap(sent, NEAR).reshape(near * tokens, width + LANES)
    outgoing, scaled = pick_rows(pool, width, top_k)
    incoming = swap(outgoing.reshape(far, SLOTS, width), FAR).reshape(far * SLOTS, width)
    half_out = expert_rows(incoming, expert_gate, expert_up, expert_down)
    returned = swap(half_out.reshape(far, SLOTS, width), FAR).reshape(far * SLOTS, width)
    mixed = lax.dot_general(
        scaled, returned, (((0,), (0,)), ((), ())), preferred_element_type=jnp.float32
    ).astype(jnp.bfloat16)
    parts = swap(mixed.reshape(near, tokens, width), NEAR)
    mixture = jnp.sum(parts.astype(jnp.float32), axis=0)
    return (residual + mixture).astype(jnp.bfloat16)


def solution(mesh):
    fine = Mesh(mesh.devices.reshape(2, 2, 4, 4, 2, 2), AXES)
    token = EXPERT + ("head",)
    placed = (
        P(token, None),
        P(EXPERT, "head", None),
        P(EXPERT, None, "head", None),
        P(EXPERT, None, "head", None),
        P(EXPERT, "head", None),
        P(EXPERT, "head", None),
        P(EXPERT),
        P("head", DEV),
        P(),
        P(EXPERT, None, "head"),
        P(EXPERT, None, "head"),
        P(EXPERT, "head", None),
        P(token, None),
        P(token, None),
    )
    return jax.shard_map(
        on_device,
        mesh=fine,
        in_specs=placed,
        out_specs=P(token, None),
        check_vma=False,
    )
```

time: 292 us -> 251 us (0.86)
  the two profiles are of different devices: /device:TPU:10 before, /device:TPU:1 now
where the time goes in v2:
time: 251 us; the launch traced here: 248 us
  blocking collectives  134 us (53%)
  waiting for transfers between devices  52.9 us (21%)
  starting transfers between devices  31.4 us (13%)
  Pallas kernels  17 us (7%)
  matrix products  5.28 us (2%)
  local copies, waits for them, and re-layouts  4 us (2%)
  other arithmetic  3.26 us (1%)
    all_to_all x3, blocking collectives, swap(): return lax.all_to_all(blocks, axes, split_axis=0, concat_axis=0, tiled=True)  134 us
    all_to_all x3, waiting for transfers between devices, swap(): return lax.all_to_all(blocks, axes, split_axis=0, concat_axis=0, tiled=True)  27.3 us
    ppermute x4, waiting for transfers between devices, shift(): lax.ppermute(block, axis, [(at, (at + by) % count) for at in range(count)])  25.6 us
    all_to_all x3, starting transfers between devices, swap(): return lax.all_to_all(blocks, axes, split_axis=0, concat_axis=0, tiled=True)  25.1 us
    pallas_call x1, Pallas kernels, expert_rows(): pl.pallas_call(lambda *refs: ffn_kernel(steps, *refs), out_shape=jax.Shap...  8.44 us
    ppermute x4, starting transfers between devices, shift(): lax.ppermute(block, axis, [(at, (at + by) % count) for at in range(count)])  6.33 us
    pallas_call x2, Pallas kernels, call(): pl.pallas_call(kernel, out_shape=out_shape, in_specs=[pl.BlockSpec(memory...  5.75 us
  transfers between devices with their start and end apart: 7, of which 4 were waited for; matrix products, arithmetic and copies ran while one was open for 3% of the time, Pallas kernels for 0%

profile of v2, /device:TPU:1, one launch (start us, length us, event | category | flops | bytes accessed | tf_op | source)
XLA Modules:
  0.0 247.8 jit_solution(15129547851450159072)
XLA Ops:
  0.0 1.1 dynamic-slice_bitcast_fusion
  1.1 2.6 %collective-permute-start = (bf16[64,2048]{1,0:T(8,128)(2,1)S(1)}, bf16[64,2048]{1,0:T(8,128)(2,1)S(1)}, u32[]{:S(2)}, u32[]{:S(2)}) collective-permute-start(bf16[64,2048]{1,0:T(8,128)(2,1)S(1)} %dynamic-slice_bitcast_fusion), channel_id=1, source_target_pairs={{0,2},{2,0},{1,3},{3,1},{4,6},{6,4},{5,7},{7,5},{8,10},{10,8},{9,1... | collective-permute-start | bytes 786440 | tf_op jit(solution)/shard_map/ppermute | solution.py:56
  3.6 0.7 iota_compare_fusion
  5.0 1.1 fusion.8
  6.1 1.7 fusion.15
  8.2 1.7 fusion.2
  10.1 1.1 broadcast_in_dim.16
  11.2 11.7 %all-to-all-start = ((bf16[16,16,2048]{2,1,0:T(8,128)(2,1)}), bf16[16,16,2048]{2,1,0:T(8,128)(2,1)S(1)}, u32[]{:S(2)}, u32[]{:S(2)}) async-start(bf16[16,16,2048]{2,1,0:T(8,128)(2,1)} %bitcast.6), calls=%async_computation | async-start | bytes 2097152 | tf_op jit(solution)/shard_map/all_to_all | solution.py:51
  22.9 2.7 %collective-permute-start.3 = (bf16[128,2048]{1,0:T(8,128)(2,1)S(1)}, bf16[128,2048]{1,0:T(8,128)(2,1)S(1)}, u32[]{:S(2)}, u32[]{:S(2)}) collective-permute-start(bf16[128,2048]{1,0:T(8,128)(2,1)S(1)} %maximum_select_fusion.refs_0_), channel_id=1, source_target_pairs={{0,48},{16,0},{32,16},{48,32},{1,49},{17,1},{33,17},{49,33},{2,50}... | collective-permute-start | bytes 1572872 | tf_op jit(solution)/shard_map/ppermute | solution.py:56
  26.7 21.2 %collective-permute-done.3.refs_3_ = bf16[128,2048]{1,0:T(8,128)(2,1)S(1)} collective-permute-done((bf16[128,2048]{1,0:T(8,128)(2,1)S(1)}, bf16[128,2048]{1,0:T(8,128)(2,1)S(1)}, u32[]{:S(2)}, u32[]{:S(2)}) %collective-permute-start.3) | collective-permute-done | bytes 524320 | tf_op jit(solution)/shard_map/ppermute | solution.py:56
  47.9 4.4 %collective-permute-done.1.refs_1_ = bf16[128,2048]{1,0:T(8,128)(2,1)} collective-permute-done((bf16[128,2048]{1,0:T(8,128)(2,1)S(1)}, bf16[128,2048]{1,0:T(8,128)(2,1)}, u32[]{:S(2)}, u32[]{:S(2)}) %collective-permute-start.1) | collective-permute-done | bytes 524320 | tf_op jit(solution)/shard_map/ppermute | solution.py:56
  52.4 1.0 copy-done.4
  53.3 3.8 %shard_map.136 = bf16[256,512]{1,0:T(8,128)(2,1)} custom-call(s32[1]{0:T(128)} %bitcast.at_ref, bf16[256,2048]{1,0:T(8,128)(2,1)} %bitcast.33, bf16[128,2048]{1,0:T(8,128)(2,1)} %copy-done.5, bf16[128,2048]{1,0:T(8,128)(2,1)} %collective-permute-done.1.refs_1_, bf16[128,2048]{1,0:T(8,128)(2,1)} %collective-permute-done.2.refs_2_, bf16[128,2048]{1,0:T(8,128)(2,1)} %copy-done.7), custom_call_target="tpu_custom_call" | custom-call | tf_op jit(solution)/shard_map/pallas_call | solution.py:61
  57.1 9.9 %all-to-all-start.1 = ((bf16[32,8,512]{2,1,0:T(8,128)(2,1)}), bf16[32,8,512]{2,1,0:T(8,128)(2,1)S(1)}, u32[]{:S(2)}, u32[]{:S(2)}) async-start(bf16[32,8,512]{2,1,0:T(8,128)(2,1)} %bitcast.34), calls=%async_computation.1 | async-start | bytes 524288 | tf_op jit(solution)/shard_map/all_to_all | solution.py:51
  67.7 13.0 %all-to-all-done.1 = bf16[32,8,512]{2,1,0:T(8,128)(2,1)S(1)} async-done(((bf16[32,8,512]{2,1,0:T(8,128)(2,1)}), bf16[32,8,512]{2,1,0:T(8,128)(2,1)S(1)}, u32[]{:S(2)}, u32[]{:S(2)}) %all-to-all-start.1) | async-done | bytes 262176 | tf_op jit(solution)/shard_map/all_to_all | solution.py:51
  81.4 2.0 shard_map.137
  83.3 3.5 %all-to-all-start.2 = ((bf16[8,8,4224]{2,1,0:T(8,128)(2,1)}), bf16[8,8,4224]{2,1,0:T(8,128)(2,1)S(1)}, u32[]{:S(2)}, u32[]{:S(2)}) async-start(bf16[8,8,4224]{2,1,0:T(8,128)(2,1)} %get-tuple-element.14), calls=%async_computation.2 | async-start | bytes 1081344 | tf_op jit(solution)/shard_map/all_to_all | solution.py:51
  86.9 14.3 %all-to-all-done.2 = bf16[8,8,4224]{2,1,0:T(8,128)(2,1)S(1)} async-done(((bf16[8,8,4224]{2,1,0:T(8,128)(2,1)}), bf16[8,8,4224]{2,1,0:T(8,128)(2,1)S(1)}, u32[]{:S(2)}, u32[]{:S(2)}) %all-to-all-start.2) | async-done | bytes 540704 | tf_op jit(solution)/shard_map/all_to_all | solution.py:51
  101.2 2.8 %shard_map.138 = (bf16[512,4096]{1,0:T(8,128)(2,1)S(1)}, bf16[512,64]{1,0:T(8,128)(2,1)S(1)}) custom-call(s32[1]{0:T(128)} %bitcast.12.refs_0_, bf16[64,4224]{1,0:T(8,128)(2,1)S(1)} %bitcast.27, bf16[64,4224]{1,0:T(8,128)(2,1)S(1)} %bitcast.28), custom_call_target="tpu_custom_call" | custom-call | tf_op jit(solution)/shard_map/pallas_call | solution.py:151
  104.0 59.6 %all_to_all.30 = bf16[32,16,4096]{2,1,0:T(8,128)(2,1)S(1)} all-to-all(bf16[32,16,4096]{2,1,0:T(8,128)(2,1)S(1)} %bitcast.29), channel_id=1, replica_groups=mesh['role'=2,'xh'=2,'y'=4,'zq'=4,'zp'=2,'head'=2] {'role','xh','y','zp'}, dimensions={0} | all-to-all | bytes 8388608 | tf_op jit(solution)/shard_map/all_to_all | solution.py:51
  163.6 8.4 %shard_map.139 = bf16[512,4096]{1,0:T(8,128)(2,1)S(1)} custom-call(bf16[512,4096]{1,0:T(8,128)(2,1)S(1)} %bitcast.30, bf16[1,4096,384]{2,1,0:T(8,128)(2,1)S(1)} %copy-done.1, bf16[1,4096,384]{2,1,0:T(8,128)(2,1)S(1)} %copy-done.2, bf16[1,384,4096]{2,1,0:T(8,128)(2,1)S(1)} %copy-done.3), custom_call_target="tpu_custom_call" | custom-call | flops 4831838208 | bytes 17825792 | tf_op jit(solution)/shard_map/pallas_call | solution.py:208
  172.0 59.0 %all_to_all.31 = bf16[32,16,4096]{2,1,0:T(8,128)(2,1)S(1)} all-to-all(bf16[32,16,4096]{2,1,0:T(8,128)(2,1)S(1)} %bitcast.31), channel_id=1, replica_groups=mesh['role'=2,'xh'=2,'y'=4,'zq'=4,'zp'=2,'head'=2] {'role','xh','y','zp'}, dimensions={0} | all-to-all | bytes 8388608 | tf_op jit(solution)/shard_map/all_to_all | solution.py:51
  231.1 0.9 fusion
  231.9 15.1 %all_to_all.32 = bf16[8,8,4096]{2,1,0:T(8,128)(2,1)S(1)} all-to-all(bf16[8,8,4096]{2,1,0:T(8,128)(2,1)S(1)} %fusion), channel_id=1, replica_groups=mesh['role'=2,'xh'=2,'y'=4,'zq'=4,'zp'=2,'head'=2] {'zq','head'}, dimensions={0} | all-to-all | bytes 1048576 | tf_op jit(solution)/shard_map/all_to_all | solution.py:51
  (38 shorter events, 4.4 us)
Async XLA Ops:
  0.0 6.1 %copy-start = (bf16[16,128,2,128]{3,2,1,0:T(2,128)(2,1)S(1)}, bf16[16,128,2,128]{3,2,1,0:T(2,128)(2,1)}, u32[]{:S(2)}) copy-start(bf16[16,128,2,128]{3,2,1,0:T(2,128)(2,1)} %param.16) | copy-start | bytes 3145732
  1.1 8.9 %collective-permute-start = (bf16[64,2048]{1,0:T(8,128)(2,1)S(1)}, bf16[64,2048]{1,0:T(8,128)(2,1)S(1)}, u32[]{:S(2)}, u32[]{:S(2)}) collective-permute-start(bf16[64,2048]{1,0:T(8,128)(2,1)S(1)} %dynamic-slice_bitcast_fusion), channel_id=1, source_target_pairs={{0,2},{2,0},{1,3},{3,1},{4,6},{6,4},{5,7},{7,5},{8,10},{10,8},{9,1... | collective-permute-start | bytes 786440 | tf_op jit(solution)/shard_map/ppermute | solution.py:56
  9.9 57.1 %copy-start.9 = (s32[8,8]{1,0:T(8,128)S(1)}, s32[8,8]{1,0:T(8,128)}, u32[]{:S(2)}) copy-start(s32[8,8]{1,0:T(8,128)} %param.26) | copy-start | bytes 772
  9.9 57.1 %copy-start.10 = (s32[8,8]{1,0:T(8,128)S(1)}, s32[8,8]{1,0:T(8,128)}, u32[]{:S(2)}) copy-start(s32[8,8]{1,0:T(8,128)} %param.27) | copy-start | bytes 772
  10.1 42.3 %copy-start.5 = (bf16[128,2048]{1,0:T(8,128)(2,1)}, bf16[128,2048]{1,0:T(8,128)(2,1)S(1)}, u32[]{:S(2)}) copy-start(bf16[128,2048]{1,0:T(8,128)(2,1)S(1)} %maximum_select_fusion.refs_0_) | copy-start | bytes 1572868
  11.2 41.1 %all-to-all-start = ((bf16[16,16,2048]{2,1,0:T(8,128)(2,1)}), bf16[16,16,2048]{2,1,0:T(8,128)(2,1)S(1)}, u32[]{:S(2)}, u32[]{:S(2)}) async-start(bf16[16,16,2048]{2,1,0:T(8,128)(2,1)} %bitcast.6), calls=%async_computation | async-start | bytes 2097152 | tf_op jit(solution)/shard_map/all_to_all | solution.py:51
  22.9 25.0 %collective-permute-start.3 = (bf16[128,2048]{1,0:T(8,128)(2,1)S(1)}, bf16[128,2048]{1,0:T(8,128)(2,1)S(1)}, u32[]{:S(2)}, u32[]{:S(2)}) collective-permute-start(bf16[128,2048]{1,0:T(8,128)(2,1)S(1)} %maximum_select_fusion.refs_0_), channel_id=1, source_target_pairs={{0,48},{16,0},{32,16},{48,32},{1,49},{17,1},{33,17},{49,33},{2,50}... | collective-permute-start | bytes 1572872 | tf_op jit(solution)/shard_map/ppermute | solution.py:56
  25.6 22.3 %collective-permute-start.2 = (bf16[128,2048]{1,0:T(8,128)(2,1)S(1)}, bf16[128,2048]{1,0:T(8,128)(2,1)}, u32[]{:S(2)}, u32[]{:S(2)}) collective-permute-start(bf16[128,2048]{1,0:T(8,128)(2,1)S(1)} %maximum_select_fusion.refs_0_), channel_id=1, source_target_pairs={{0,32},{16,48},{32,0},{48,16},{1,33},{17,49},{33,1},{49,17},{2,34}... | collective-permute-start | bytes 1572872 | tf_op jit(solution)/shard_map/ppermute | solution.py:56
  26.0 26.3 %collective-permute-start.1 = (bf16[128,2048]{1,0:T(8,128)(2,1)S(1)}, bf16[128,2048]{1,0:T(8,128)(2,1)}, u32[]{:S(2)}, u32[]{:S(2)}) collective-permute-start(bf16[128,2048]{1,0:T(8,128)(2,1)S(1)} %maximum_select_fusion.refs_0_), channel_id=1, source_target_pairs={{0,16},{16,32},{32,48},{48,0},{1,17},{17,33},{33,49},{49,1},{2,18}... | collective-permute-start | bytes 1572872 | tf_op jit(solution)/shard_map/ppermute | solution.py:56
  47.9 4.4 %copy-start.7 = (bf16[128,2048]{1,0:T(8,128)(2,1)}, bf16[128,2048]{1,0:T(8,128)(2,1)S(1)}, u32[]{:S(2)}) copy-start(bf16[128,2048]{1,0:T(8,128)(2,1)S(1)} %collective-permute-done.3.refs_3_) | copy-start | bytes 1572868
  52.3 1.0 copy-start.4
  57.1 23.6 %all-to-all-start.1 = ((bf16[32,8,512]{2,1,0:T(8,128)(2,1)}), bf16[32,8,512]{2,1,0:T(8,128)(2,1)S(1)}, u32[]{:S(2)}, u32[]{:S(2)}) async-start(bf16[32,8,512]{2,1,0:T(8,128)(2,1)} %bitcast.34), calls=%async_computation.1 | async-start | bytes 524288 | tf_op jit(solution)/shard_map/all_to_all | solution.py:51
  80.7 0.7 copy-start.6
  83.3 17.8 %all-to-all-start.2 = ((bf16[8,8,4224]{2,1,0:T(8,128)(2,1)}), bf16[8,8,4224]{2,1,0:T(8,128)(2,1)S(1)}, u32[]{:S(2)}, u32[]{:S(2)}) async-start(bf16[8,8,4224]{2,1,0:T(8,128)(2,1)} %get-tuple-element.14), calls=%async_computation.2 | async-start | bytes 1081344 | tf_op jit(solution)/shard_map/all_to_all | solution.py:51
  101.2 62.4 %copy-start.3 = (bf16[1,384,4096]{2,1,0:T(8,128)(2,1)S(1)}, bf16[1,384,4096]{2,1,0:T(8,128)(2,1)}, u32[]{:S(2)}) copy-start(bf16[1,384,4096]{2,1,0:T(8,128)(2,1)} %refs_3_.1) | copy-start | bytes 9437188
  104.0 59.6 %copy-start.1 = (bf16[1,4096,384]{2,1,0:T(8,128)(2,1)S(1)}, bf16[1,4096,384]{2,1,0:T(8,128)(2,1)}, u32[]{:S(2)}) copy-start(bf16[1,4096,384]{2,1,0:T(8,128)(2,1)} %refs_1_.1) | copy-start | bytes 9437188
  104.0 59.6 %copy-start.2 = (bf16[1,4096,384]{2,1,0:T(8,128)(2,1)S(1)}, bf16[1,4096,384]{2,1,0:T(8,128)(2,1)}, u32[]{:S(2)}) copy-start(bf16[1,4096,384]{2,1,0:T(8,128)(2,1)} %refs_2_.1) | copy-start | bytes 9437188
  231.1 16.0 %copy-start.8 = (f32[8,4096]{1,0:T(8,128)S(1)}, f32[8,4096]{1,0:T(8,128)}, u32[]{:S(2)}) copy-start(f32[8,4096]{1,0:T(8,128)} %get-tuple-element.13) | copy-start | bytes 393220

commit v3 on v2

--- a/solution.py
+++ b/solution.py
@@ -11,13 +11,14 @@
 AXES = ("role", "xh", "y", "zq", "zp", "head")
 DEV = ("xh", "y", "zq", "zp")
 EXPERT = ("role",) + DEV
-ROWS_FROM = ("role", "xh", "zq")
-SUMS_TO = ("role", "xh", "zq", "head")
-NEAR = ("zq", "head")
-FAR = ("role", "xh", "y", "zp")
+RING = ("zq", "zp")
+ROWS_FROM = ("role", "xh", "y")
+SUMS_TO = ("role", "xh", "y", "head")
+NEAR = "zq"
+FAR = ("role", "xh", "y", "zp", "head")
 CAP = 2
 BLOCK = 8
-SLOTS = 16
+SLOTS = 8
 LANES = 128
 
 
@@ -44,7 +45,7 @@
         blended
         + weight_new.astype(jnp.float32)[..., None] * value_new.astype(jnp.float32)[:, :, None, :]
     )
-    return blended.astype(jnp.bfloat16).reshape(row_count, kv_heads * group_size * head_dim)
+    return blended.astype(jnp.bfloat16)
 
 
 def swap(blocks, axes):
@@ -56,67 +57,62 @@
     return lax.ppermute(block, axis, [(at, (at + by) % count) for at in range(count)])
 
 
-def call(kernel, out_shape, *operands, spaces=None):
-    whole = pl.BlockSpec(memory_space=pltpu.VMEM)
-    return pl.pallas_call(
-        kernel,
-        out_shape=out_shape,
-        in_specs=[
-            pl.BlockSpec(memory_space=pltpu.SMEM) if operand.dtype == jnp.int32 else whole
-            for operand in operands
-        ],
-        out_specs=jax.tree.map(lambda _: whole, out_shape),
-    )(*operands)
-
-
-def project_kernel(at_ref, rows_ref, *refs):
-    pieces, out_ref = refs[:-1], refs[-1]
-    count = len(pieces)
-    rows = rows_ref[...]
-    for by, piece_ref in enumerate(pieces):
-        width = piece_ref.shape[0]
-        place = lax.rem(at_ref[0] - by + count, count)
-        part = lax.dot_general(
-            rows, piece_ref[...], (((1,), (1,)), ((), ())), preferred_element_type=jnp.float32
-        )
-        out_ref[:, pl.ds(pl.multiple_of(place * width, width), width)] = part.astype(jnp.bfloat16)
+def spread_kernel(attended_ref, out_ref):
+    roles, near, rows, _ = out_ref.shape
+    for role in range(roles):
+        for head in range(attended_ref.shape[2]):
+            part = attended_ref[:, role, head, :]
+            for copy in range(near):
+                out_ref[role, copy, :, head * LANES : (head + 1) * LANES] = part
+
+
+def project_kernel(spots, at_ref, rows_ref, *refs):
+    pieces, out_ref, weights = refs[:-2], refs[-2], refs[-1]
+    width = pieces[0].shape[0]
+    count = weights.shape[0] // width
+    for (by, first), piece_ref in zip(spots, pieces):
+        place = lax.rem(at_ref[0] - by + count, count) * width + first
+        to = pl.ds(pl.multiple_of(place, width // 2), piece_ref.shape[0])
+        weights[to, :] = piece_ref[...]
+    out_ref[...] = lax.dot_general(
+        rows_ref[...], weights[...], (((1,), (1,)), ((), ())), preferred_element_type=jnp.float32
+    ).astype(jnp.bfloat16)
 
 
 def norm_kernel(arrived_ref, hidden_ref, gain_ref, choices_ref, residual_ref, sent_ref):
-    roles, halves, quads, heads, tokens, width = arrived_ref.shape
+    roles, halves, rings, heads, tokens, width = arrived_ref.shape
     rows = width // LANES
     total = jnp.zeros((tokens, LANES), jnp.float32)
     for x in range(halves):
-        for q in range(quads):
-            for y in range(rows):
-                span = slice(y * LANES, (y + 1) * LANES)
-                first = ((x * rows + y) * quads + q) * LANES
+        for y in range(rings):
+            for z in range(rows):
+                span = slice(z * LANES, (z + 1) * LANES)
+                first = (x * rings + y) * width + z * LANES
                 to = slice(first, first + LANES)
                 value = hidden_ref[:, to].astype(jnp.float32)
                 for r in range(roles):
                     for h in range(heads):
-                        value = value + arrived_ref[r, x, q, h, :, span].astype(jnp.float32)
+                        value = value + arrived_ref[r, x, y, h, :, span].astype(jnp.float32)
                 residual_ref[:, to] = value
                 total = total + value * value
     count = residual_ref.shape[1]
     scale = lax.rsqrt(jnp.sum(total, axis=1, keepdims=True) / count + 1e-06)
-    normed = (residual_ref[...] * scale * gain_ref[...]).astype(jnp.bfloat16)
-    for copy in range(sent_ref.shape[0]):
-        sent_ref[copy, :, :count] = normed
-        sent_ref[copy, :, count:] = choices_ref[...]
-
-
-def pick_kernel(top_k, quad_ref, choices_ref, pool_ref, out_ref, scaled_ref, picks):
+    sent_ref[:, :count] = (residual_ref[...] * scale * gain_ref[...]).astype(jnp.bfloat16)
+    sent_ref[:, count:] = choices_ref[...]
+
+
+def pick_kernel(top_k, blocks, quad_ref, *refs):
+    choices_refs, pool_refs = refs[:blocks], refs[blocks : 2 * blocks]
+    out_ref, scaled_ref, picks = refs[2 * blocks :]
     count, tokens = picks.shape
 
     @pl.when(pl.program_id(0) == 0)
     def _():
-        table = choices_ref[...].astype(jnp.float32).T
+        table = jnp.concatenate([ref[...].astype(jnp.float32) for ref in choices_refs], axis=0).T
         slot = lax.broadcasted_iota(jnp.int32, (count, tokens), 0)
         token = lax.broadcasted_iota(jnp.int32, (count, tokens), 1)
-        place = slot // SLOTS
-        expert = place // 2 * 8 + quad_ref[0] * 2 + place % 2
-        expert = expert.astype(jnp.float32)
+        place = slot // (2 * SLOTS)
+        expert = (place // 2 * 8 + quad_ref[0] * 2 + place % 2).astype(jnp.float32)
         levels = table[top_k : 2 * top_k]
         shares = levels / jnp.sum(levels, axis=0, keepdims=True)
         named = jnp.zeros((count, tokens), jnp.float32)
@@ -135,31 +131,31 @@
         )
         rank = (slot % CAP).astype(jnp.float32)
         chosen = (named > 0) & (earlier == rank) & (token // BLOCK == slot % SLOTS // CAP)
+        scaled_ref[...] = jnp.where(chosen, share, 0.0).astype(jnp.bfloat16)
         picks[...] = jnp.where(chosen, 1.0, 0.0).astype(jnp.bfloat16)
-        scaled_ref[...] = jnp.where(chosen, share, 0.0).astype(jnp.bfloat16)
-
-    out_ref[...] = jnp.dot(
-        picks[...], pool_ref[...], preferred_element_type=jnp.float32
-    ).astype(jnp.bfloat16)
+
+    pool = jnp.concatenate([ref[...] for ref in pool_refs], axis=0)
+    out_ref[...] = jnp.dot(picks[...], pool, preferred_element_type=jnp.float32).astype(
+        jnp.bfloat16
+    )
 
 
 def pick_rows(pool, width, top_k):
-    tokens = pool.shape[0]
-    count = math.prod(lax.axis_size(name) for name in FAR) * SLOTS
+    blocks, rows = len(pool), pool[0].shape[0]
+    tokens = blocks * rows
+    count = lax.axis_size(FAR) * SLOTS
     block = 1024
     quad = lax.axis_index("zq").astype(jnp.int32).reshape(1)
     return pl.pallas_call(
-        lambda *refs: pick_kernel(top_k, *refs),
+        lambda *refs: pick_kernel(top_k, blocks, *refs),
         out_shape=(
             jax.ShapeDtypeStruct((count, width), jnp.bfloat16),
             jax.ShapeDtypeStruct((count, tokens), jnp.bfloat16),
         ),
         grid=(width // block,),
-        in_specs=[
-            pl.BlockSpec(memory_space=pltpu.SMEM),
-            pl.BlockSpec((tokens, LANES), lambda s: (0, width // LANES)),
-            pl.BlockSpec((tokens, block), lambda s: (0, s)),
-        ],
+        in_specs=[pl.BlockSpec(memory_space=pltpu.SMEM)]
+        + [pl.BlockSpec((rows, LANES), lambda s: (0, width // LANES))] * blocks
+        + [pl.BlockSpec((rows, block), lambda s: (0, s))] * blocks,
         out_specs=(
             pl.BlockSpec((count, block), lambda s: (0, s)),
             pl.BlockSpec((count, tokens), lambda s: (0, 0)),
@@ -168,7 +164,7 @@
         compiler_params=pltpu.CompilerParams(
             dimension_semantics=("arbitrary",), vmem_limit_bytes=16 << 20
         ),
-    )(quad, pool, pool)
+    )(quad, *pool, *pool)
 
 
 def ffn_kernel(unit_steps, rows_ref, gate_ref, up_ref, down_ref, out_ref, active):
@@ -218,7 +214,7 @@
         out_specs=pl.BlockSpec((count, columns), lambda s: (0, late(s))),
         scratch_shapes=[pltpu.VMEM((count, units), jnp.bfloat16)],
         compiler_params=pltpu.CompilerParams(
-            dimension_semantics=("arbitrary",), vmem_limit_bytes=24 << 20
+            dimension_semantics=("arbitrary",), vmem_limit_bytes=44 << 20
         ),
         cost_estimate=pl.CostEstimate(
             flops=6 * count * width * units,
@@ -228,36 +224,42 @@
     )(rows, gate, up, down)
 
 
-def weight_pair(out_proj):
-    cols = out_proj.shape[1]
+def half_weights(out_proj):
     half = out_proj.shape[0] // 2
-    own = lax.dynamic_slice_in_dim(out_proj.T, lax.axis_index("role") * half, half, axis=1)
-    other = shift(own, "zp", 1)
-    first = lax.axis_index("zp") == 0
-    pair = jnp.where(
-        first, jnp.concatenate([own, other], axis=0), jnp.concatenate([other, own], axis=0)
-    )
-    return pair
-
-
-def project(attended, pair):
-    rows, features = attended.shape
-    half = features // 2
-    near = lax.axis_size("xh") * lax.axis_size("zq")
-    halves = attended.reshape(rows, 2, half).transpose(1, 0, 2)
-    sent = jnp.broadcast_to(halves[:, None], (2, near, rows, half)).reshape(2 * near, rows, half)
-    sent, pair = lax.optimization_barrier((sent, pair))
-    pieces = [pair] + [shift(pair, "y", by) for by in range(1, lax.axis_size("y"))]
-    gathered = swap(sent, ROWS_FROM).reshape(2 * near * rows, half)
-    width = len(pieces) * pieces[0].shape[0]
-    columns = call(
-        project_kernel,
-        jax.ShapeDtypeStruct((2 * near * rows, width), jnp.bfloat16),
-        lax.axis_index("y").astype(jnp.int32).reshape(1),
-        gathered,
-        *pieces,
-    )
-    return swap(columns.reshape(4 * near, rows // 2, width), SUMS_TO)
+    return lax.dynamic_slice_in_dim(out_proj.T, lax.axis_index("role") * half, half, axis=1)
+
+
+def project(attended, own):
+    rows, roles, group, head_dim = attended.shape
+    half = group * head_dim
+    near = lax.axis_size("xh") * lax.axis_size("y")
+    ring, cols = lax.axis_size(RING), own.shape[0]
+    up, down = shift(own, RING, 1), shift(own, RING, -1)
+    attended, up, down = lax.optimization_barrier((attended, up, down))
+    whole = pl.BlockSpec(memory_space=pltpu.VMEM)
+    sent = pl.pallas_call(
+        spread_kernel,
+        out_shape=jax.ShapeDtypeStruct((roles, near, rows, half), jnp.bfloat16),
+        in_specs=[whole],
+        out_specs=whole,
+    )(attended)
+    gathered = swap(sent.reshape(roles * near, rows, half), ROWS_FROM)
+    gathered = gathered.reshape(roles * near * rows, half)
+    pieces, spots = [own, up, down], [(0, 0), (1, 0), (-1, 0)]
+    for by in range(2, ring // 2):
+        up, down = shift(up, RING, 1), shift(down, RING, -1)
+        pieces, spots = pieces + [up, down], spots + [(by, 0), (-by, 0)]
+    part = cols // 2
+    pieces = pieces + [shift(up[:part], RING, 1), shift(down[part:], RING, -1)]
+    spots = spots + [(ring // 2, 0), (ring // 2, part)]
+    columns = pl.pallas_call(
+        lambda *refs: project_kernel(spots, *refs),
+        out_shape=jax.ShapeDtypeStruct((roles * near * rows, ring * cols), jnp.bfloat16),
+        in_specs=[pl.BlockSpec(memory_space=pltpu.SMEM)] + [whole] * (len(pieces) + 1),
+        out_specs=whole,
+        scratch_shapes=[pltpu.VMEM((ring * cols, half), jnp.bfloat16)],
+    )(lax.axis_index(RING).astype(jnp.int32).reshape(1), gathered, *pieces)
+    return swap(columns.reshape(2 * roles * near, rows // 2, ring * cols), SUMS_TO)
 
 
 def on_device(
@@ -278,27 +280,30 @@
 ):
     tokens, width = hidden.shape
     top_k = expert_ids.shape[1]
-    near = lax.axis_size("zq") * lax.axis_size("head")
-    far = math.prod(lax.axis_size(name) for name in FAR)
-
-    pair = weight_pair(out_proj)
+    near, far = lax.axis_size(NEAR), lax.axis_size(FAR)
+
+    own = half_weights(out_proj)
     attended = attend_block(queries, cache_keys, cache_values, new_keys, new_values, lengths)
-    arrived = project(attended, pair)
+    arrived = project(attended, own)
     choices = jnp.concatenate([expert_ids, gate_levels], axis=1).astype(jnp.bfloat16)
     choices = jnp.pad(choices, ((0, 0), (0, LANES - 2 * top_k)))
-    residual, sent = call(
+    whole = pl.BlockSpec(memory_space=pltpu.VMEM)
+    residual, sent = pl.pallas_call(
         norm_kernel,
-        (
+        out_shape=(
             jax.ShapeDtypeStruct((tokens, width), jnp.float32),
-            jax.ShapeDtypeStruct((near, tokens, width + LANES), jnp.bfloat16),
-        ),
+            jax.ShapeDtypeStruct((tokens, width + LANES), jnp.bfloat16),
+        ),
+        in_specs=[whole] * 4,
+        out_specs=(whole, whole),
+    )(
         arrived.reshape([lax.axis_size(name) for name in SUMS_TO] + list(arrived.shape[1:])),
         hidden,
         norm_gain.reshape(1, width),
         choices,
     )
 
-    pool = swap(sent, NEAR).reshape(near * tokens, width + LANES)
+    pool = [sent] + [shift(sent, NEAR, by) for by in range(1, near)]
     outgoing, scaled = pick_rows(pool, width, top_k)
     incoming = swap(outgoing.reshape(far, SLOTS, width), FAR).reshape(far * SLOTS, width)
     half_out = expert_rows(incoming, expert_gate, expert_up, expert_down)
@@ -306,8 +311,10 @@
     mixed = lax.dot_general(
         scaled, returned, (((0,), (0,)), ((), ())), preferred_element_type=jnp.float32
     ).astype(jnp.bfloat16)
-    parts = swap(mixed.reshape(near, tokens, width), NEAR)
-    mixture = jnp.sum(parts.astype(jnp.float32), axis=0)
+    parts = [mixed[:tokens]] + [
+        shift(mixed[by * tokens : (by + 1) * tokens], NEAR, -by) for by in range(1, near)
+    ]
+    mixture = sum(part.astype(jnp.float32) for part in parts)
     return (residual + mixture).astype(jnp.bfloat16)
 
 

time: 251 us -> 234 us (0.932)
  waiting for transfers between devices: 52.9 us -> 35.2 us
  blocking collectives: 134 us -> 119 us
  starting transfers between devices: 31.4 us -> 41.6 us
  Pallas kernels: 17 us -> 21.3 us
  local copies, waits for them, and re-layouts: 4 us -> 7.04 us
    all_to_all x3 -> x2, waiting for transfers between devices: 27.3 us -> 8.23 us  [swap(): return lax.all_to_all(blocks, axes, split_axis=0, concat_axis=0, tiled=True)]
    ppermute x4 -> x14, starting transfers between devices: 6.33 us -> 23 us  [shift(): lax.ppermute(block, axis, [(at, (at + by) % count) for at in range(count)])]
    all_to_all x3 -> x2, blocking collectives: 134 us -> 119 us  [swap(): return lax.all_to_all(blocks, axes, split_axis=0, concat_axis=0, tiled=True)]
    all_to_all x3 -> x2, starting transfers between devices: 25.1 us -> 18.6 us  [swap(): return lax.all_to_all(blocks, axes, split_axis=0, concat_axis=0, tiled=True)]
    unnamed x22 -> x38, local copies, waits for them, and re-layouts: 1.71 us -> 5.23 us
    pallas_call x1, Pallas kernels: 8.44 us -> 11.3 us  [expert_rows(): pl.pallas_call(lambda *refs: ffn_kernel(steps, *refs), out_shape=jax.Shap...]
    pallas_call x3 -> x4, Pallas kernels: 8.53 us -> 9.94 us  [the longest x1 3.4 us: project(): pl.pallas_call(lambda *refs: project_kernel(spots, *refs), out_shape=jax....]
    ppermute x4 -> x14, waiting for transfers between devices: 25.6 us -> 26.9 us  [shift(): lax.ppermute(block, axis, [(at, (at + by) % count) for at in range(count)])]
  transfers between devices with their start and end apart: 7 -> 16, of which waited for: 4 -> 10; matrix products, arithmetic and copies ran while one was open for 3% -> 4% of each run, Pallas kernels for 0% -> 0%
where the time goes in v3:
time: 234 us; the launch traced here: 233 us
  blocking collectives  119 us (51%)
  starting transfers between devices  41.6 us (18%)
  waiting for transfers between devices  35.2 us (15%)
  Pallas kernels  21.3 us (9%)
  local copies, waits for them, and re-layouts  7.04 us (3%)
  matrix products  5.92 us (3%)
  other arithmetic  3.11 us (1%)
    all_to_all x2, blocking collectives, swap(): return lax.all_to_all(blocks, axes, split_axis=0, concat_axis=0, tiled=True)  119 us
    ppermute x14, waiting for transfers between devices, shift(): lax.ppermute(block, axis, [(at, (at + by) % count) for at in range(count)])  26.9 us
    ppermute x14, starting transfers between devices, shift(): lax.ppermute(block, axis, [(at, (at + by) % count) for at in range(count)])  23 us
    all_to_all x2, starting transfers between devices, swap(): return lax.all_to_all(blocks, axes, split_axis=0, concat_axis=0, tiled=True)  18.6 us
    pallas_call x1, Pallas kernels, expert_rows(): pl.pallas_call(lambda *refs: ffn_kernel(steps, *refs), out_shape=jax.Shap...  11.3 us
    all_to_all x2, waiting for transfers between devices, swap(): return lax.all_to_all(blocks, axes, split_axis=0, concat_axis=0, tiled=True)  8.23 us
    unnamed x38, local copies, waits for them, and re-layouts  5.23 us
  transfers between devices with their start and end apart: 16, of which 10 were waited for; matrix products, arithmetic and copies ran while one was open for 4% of the time, Pallas kernels for 0%

profile of v3, /device:TPU:1, one launch (start us, length us, event | category | flops | bytes accessed | tf_op | source)
XLA Modules:
  0.0 232.9 jit_solution(6695821571255411855)
XLA Ops:
  1.1 6.5 %collective-permute-start.1 = (bf16[64,2048]{1,0:T(8,128)(2,1)S(1)}, bf16[64,2048]{1,0:T(8,128)(2,1)S(1)}, u32[]{:S(2)}, u32[]{:S(2)}) collective-permute-start(bf16[64,2048]{1,0:T(8,128)(2,1)S(1)} %dynamic-slice_bitcast_fusion.refs_2_), channel_id=1, source_target_pairs={{0,14},{2,0},{4,2},{6,4},{8,6},{10,8},{12,10},{14,12},{1,15},{3,1}... | collective-permute-start | bytes 786440 | tf_op jit(solution)/shard_map/ppermute | solution.py:57
  10.1 1.7 fusion.16
  12.1 2.3 %fusion.2.attended_ref = bf16[16,2,16,128]{3,2,1,0:T(8,128)(2,1)} fusion(bf16[16,128,2,128]{3,2,1,0:T(2,128)(2,1)} %param.17, f32[16,2,16,128]{3,2,1,0:T(8,128)S(1)} %get-tuple-element.25, f32[16,2,128]{2,1,0:T(2,128)S(1)} %convert_element_type.42, f32[16,2,16]{2,1,0:T(2,128)S(1)} %get-tuple-element.23, f32[16,2,16]{2,1,0:T(2,128)S(1)} %get-tuple-element.22, ...), kind=kOutput, calls=%fused_computation.5 | convolution fusion | flops 17170432 | bytes 1464320 | tf_op jit(solution)/shard_map/bhgt,bthd->bhgd/dot_general | solution.py:43
  15.6 2.2 shard_map.136
  17.8 8.8 %all-to-all-start = ((bf16[16,16,2048]{2,1,0:T(8,128)(2,1)}), bf16[16,16,2048]{2,1,0:T(8,128)(2,1)S(1)}, u32[]{:S(2)}, u32[]{:S(2)}) async-start(bf16[16,16,2048]{2,1,0:T(8,128)(2,1)} %bitcast.26), calls=%async_computation | async-start | bytes 2097152 | tf_op jit(solution)/shard_map/all_to_all | solution.py:52
  26.7 2.7 %collective-permute-start.3 = (bf16[64,2048]{1,0:T(8,128)(2,1)S(1)}, bf16[64,2048]{1,0:T(8,128)(2,1)S(1)}, u32[]{:S(2)}, u32[]{:S(2)}) collective-permute-start(bf16[64,2048]{1,0:T(8,128)(2,1)S(1)} %collective-permute-done.1.refs_4_), channel_id=1, source_target_pairs={{0,14},{2,0},{4,2},{6,4},{8,6},{10,8},{12,10},{14,12},{1,15},{3,1}... | collective-permute-start | bytes 786440 | tf_op jit(solution)/shard_map/ppermute | solution.py:57
  29.3 6.3 %collective-permute-done.2.refs_5_ = bf16[64,2048]{1,0:T(8,128)(2,1)S(1)} collective-permute-done((bf16[64,2048]{1,0:T(8,128)(2,1)S(1)}, bf16[64,2048]{1,0:T(8,128)(2,1)S(1)}, u32[]{:S(2)}, u32[]{:S(2)}) %collective-permute-start.2) | collective-permute-done | bytes 262176 | tf_op jit(solution)/shard_map/ppermute | solution.py:57
  36.3 2.1 collective-permute-start.5
  38.4 5.3 %collective-permute-done.4.refs_7_ = bf16[64,2048]{1,0:T(8,128)(2,1)S(1)} collective-permute-done((bf16[64,2048]{1,0:T(8,128)(2,1)S(1)}, bf16[64,2048]{1,0:T(8,128)(2,1)S(1)}, u32[]{:S(2)}, u32[]{:S(2)}) %collective-permute-start.4) | collective-permute-done | bytes 262176 | tf_op jit(solution)/shard_map/ppermute | solution.py:57
  44.4 2.7 %collective-permute-start.7 = (bf16[32,2048]{1,0:T(8,128)(2,1)S(1)}, bf16[32,2048]{1,0:T(8,128)(2,1)S(1)}, u32[]{:S(2)}, u32[]{:S(2)}) collective-permute-start(bf16[32,2048]{1,0:T(8,128)(2,1)S(1)} %slice.25), channel_id=1, source_target_pairs={{0,14},{2,0},{4,2},{6,4},{8,6},{10,8},{12,10},{14,12},{1,15},{3,1}... | collective-permute-start | bytes 393224 | tf_op jit(solution)/shard_map/ppermute | solution.py:57
  47.2 2.5 %collective-permute-done.6.refs_9_ = bf16[32,2048]{1,0:T(8,128)(2,1)S(1)} collective-permute-done((bf16[32,2048]{1,0:T(8,128)(2,1)}, bf16[32,2048]{1,0:T(8,128)(2,1)S(1)}, u32[]{:S(2)}, u32[]{:S(2)}) %collective-permute-start.6) | collective-permute-done | bytes 131104 | tf_op jit(solution)/shard_map/ppermute | solution.py:57
  50.7 3.4 %shard_map.137 = bf16[256,512]{1,0:T(8,128)(2,1)} custom-call(s32[1]{0:T(128)} %bitcast.refs_0_, bf16[256,2048]{1,0:T(8,128)(2,1)} %bitcast.25, bf16[64,2048]{1,0:T(8,128)(2,1)} %copy-done.6, bf16[64,2048]{1,0:T(8,128)(2,1)} %copy-done.11, bf16[64,2048]{1,0:T(8,128)(2,1)} %copy-done.10, bf16[64,2048]{1,0:T(8,128)(2,1)} %copy-done.12, ...), custom_call_target="tpu_custom_call" | custom-call | tf_op jit(solution)/shard_map/pallas_call | solution.py:255
  54.1 9.8 %all-to-all-start.1 = ((bf16[32,8,512]{2,1,0:T(8,128)(2,1)}), bf16[32,8,512]{2,1,0:T(8,128)(2,1)S(1)}, u32[]{:S(2)}, u32[]{:S(2)}) async-start(bf16[32,8,512]{2,1,0:T(8,128)(2,1)} %bitcast.27), calls=%async_computation.1 | async-start | bytes 524288 | tf_op jit(solution)/shard_map/all_to_all | solution.py:52
  64.7 8.2 %all-to-all-done.1 = bf16[32,8,512]{2,1,0:T(8,128)(2,1)S(1)} async-done(((bf16[32,8,512]{2,1,0:T(8,128)(2,1)}), bf16[32,8,512]{2,1,0:T(8,128)(2,1)S(1)}, u32[]{:S(2)}, u32[]{:S(2)}) %all-to-all-start.1) | async-done | bytes 262176 | tf_op jit(solution)/shard_map/all_to_all | solution.py:52
  73.6 1.8 shard_map.138
  76.4 1.4 collective-permute-start.9
  80.1 4.8 %collective-permute-done.9.refs_3_.refs_7_ = bf16[8,4224]{1,0:T(8,128)(2,1)S(1)} collective-permute-done((bf16[8,4224]{1,0:T(8,128)(2,1)}, bf16[8,4224]{1,0:T(8,128)(2,1)S(1)}, u32[]{:S(2)}, u32[]{:S(2)}) %collective-permute-start.9) | collective-permute-done | bytes 67616 | tf_op jit(solution)/shard_map/ppermute | solution.py:57
  86.5 2.6 %shard_map.139 = (bf16[512,4096]{1,0:T(8,128)(2,1)S(1)}, bf16[512,32]{1,0:T(8,128)(2,1)S(1)}) custom-call(s32[1]{0:T(128)} %bitcast.11.refs_0_, bf16[8,4224]{1,0:T(8,128)(2,1)S(1)} %copy-done.1, bf16[8,4224]{1,0:T(8,128)(2,1)S(1)} %collective-permute-done.8.refs_2_.refs_6_, bf16[8,4224]{1,0:T(8,128)(2,1)S(1)} %collective-permute-done.9.refs_3_.refs_7_, ...), custom_call_target="tpu_custom_call" | custom-call | tf_op jit(solution)/shard_map/pallas_call | solution.py:149
  89.1 60.3 %all_to_all.20 = bf16[64,8,4096]{2,1,0:T(8,128)(2,1)} all-to-all(bf16[64,8,4096]{2,1,0:T(8,128)(2,1)S(1)} %bitcast.22), channel_id=1, replica_groups=mesh['role'=2,'xh'=2,'y'=4,'zq'=4,'zp'=2,'head'=2] {'role','xh','y','zp'..., dimensions={0} | all-to-all | bytes 8388608 | tf_op jit(solution)/shard_map/all_to_all | solution.py:52
  149.3 1.9 copy-done.4
  151.2 11.3 %shard_map.140 = bf16[512,4096]{1,0:T(8,128)(2,1)} custom-call(bf16[512,4096]{1,0:T(8,128)(2,1)} %bitcast.23, bf16[1,4096,384]{2,1,0:T(8,128)(2,1)S(1)} %copy-done.2, bf16[1,4096,384]{2,1,0:T(8,128)(2,1)S(1)} %copy-done.3, bf16[1,384,4096]{2,1,0:T(8,128)(2,1)S(1)} %copy-done.4), custom_call_target="tpu_custom_call" | custom-call | flops 4831838208 | bytes 17825792 | tf_op jit(solution)/shard_map/pallas_call | solution.py:204
  162.6 58.3 %all_to_all.21 = bf16[64,8,4096]{2,1,0:T(8,128)(2,1)S(1)} all-to-all(bf16[64,8,4096]{2,1,0:T(8,128)(2,1)} %bitcast.24), channel_id=1, replica_groups=mesh['role'=2,'xh'=2,'y'=4,'zq'=4,'zp'=2,'head'=2] {'role','xh','y','zp'..., dimensions={0} | all-to-all | bytes 8388608 | tf_op jit(solution)/shard_map/all_to_all | solution.py:52
  224.2 2.8 %collective-permute-start.12 = (bf16[8,4096]{1,0:T(8,128)(2,1)S(1)}, bf16[8,4096]{1,0:T(8,128)(2,1)S(1)}, u32[]{:S(2)}, u32[]{:S(2)}) collective-permute-start(bf16[8,4096]{1,0:T(8,128)(2,1)S(1)} %get-tuple-element.21), channel_id=1, source_target_pairs={{0,8},{4,12},{8,0},{12,4},{1,9},{5,13},{9,1},{13,5},{2,10},{6,14},... | collective-permute-start | bytes 196616 | tf_op jit(solution)/shard_map/ppermute | solution.py:57
  228.1 4.1 %collective-permute-done.12 = bf16[8,4096]{1,0:T(8,128)(2,1)S(1)} collective-permute-done((bf16[8,4096]{1,0:T(8,128)(2,1)S(1)}, bf16[8,4096]{1,0:T(8,128)(2,1)S(1)}, u32[]{:S(2)}, u32[]{:S(2)}) %collective-permute-start.12) | collective-permute-done | bytes 65568 | tf_op jit(solution)/shard_map/ppermute | solution.py:57
  (70 shorter events, 19.1 us)
Async XLA Ops:
  1.1 43.3 %copy-start.6 = (bf16[64,2048]{1,0:T(8,128)(2,1)}, bf16[64,2048]{1,0:T(8,128)(2,1)S(1)}, u32[]{:S(2)}) copy-start(bf16[64,2048]{1,0:T(8,128)(2,1)S(1)} %dynamic-slice_bitcast_fusion.refs_2_) | copy-start | bytes 786436
  1.1 13.4 %collective-permute-start.1 = (bf16[64,2048]{1,0:T(8,128)(2,1)S(1)}, bf16[64,2048]{1,0:T(8,128)(2,1)S(1)}, u32[]{:S(2)}, u32[]{:S(2)}) collective-permute-start(bf16[64,2048]{1,0:T(8,128)(2,1)S(1)} %dynamic-slice_bitcast_fusion.refs_2_), channel_id=1, source_target_pairs={{0,14},{2,0},{4,2},{6,4},{8,6},{10,8},{12,10},{14,12},{1,15},{3,1}... | collective-permute-start | bytes 786440 | tf_op jit(solution)/shard_map/ppermute | solution.py:57
  7.6 8.1 %collective-permute-start = (bf16[64,2048]{1,0:T(8,128)(2,1)S(1)}, bf16[64,2048]{1,0:T(8,128)(2,1)S(1)}, u32[]{:S(2)}, u32[]{:S(2)}) collective-permute-start(bf16[64,2048]{1,0:T(8,128)(2,1)S(1)} %dynamic-slice_bitcast_fusion.refs_2_), channel_id=1, source_target_pairs={{0,2},{2,4},{4,6},{6,8},{8,10},{10,12},{12,14},{14,0},{1,3},{3,5},... | collective-permute-start | bytes 786440 | tf_op jit(solution)/shard_map/ppermute | solution.py:57
  14.4 49.5 %copy-start.17 = (s32[8,8]{1,0:T(8,128)S(1)}, s32[8,8]{1,0:T(8,128)}, u32[]{:S(2)}) copy-start(s32[8,8]{1,0:T(8,128)} %param.26) | copy-start | bytes 772
  14.4 49.5 %copy-start.18 = (s32[8,8]{1,0:T(8,128)S(1)}, s32[8,8]{1,0:T(8,128)}, u32[]{:S(2)}) copy-start(s32[8,8]{1,0:T(8,128)} %param.27) | copy-start | bytes 772
  14.4 35.2 %copy-start.10 = (bf16[64,2048]{1,0:T(8,128)(2,1)}, bf16[64,2048]{1,0:T(8,128)(2,1)S(1)}, u32[]{:S(2)}) copy-start(bf16[64,2048]{1,0:T(8,128)(2,1)S(1)} %collective-permute-done.1.refs_4_) | copy-start | bytes 786436
  15.6 34.0 %copy-start.11 = (bf16[64,2048]{1,0:T(8,128)(2,1)}, bf16[64,2048]{1,0:T(8,128)(2,1)S(1)}, u32[]{:S(2)}) copy-start(bf16[64,2048]{1,0:T(8,128)(2,1)S(1)} %collective-permute-done.refs_3_) | copy-start | bytes 786436
  17.8 31.8 %all-to-all-start = ((bf16[16,16,2048]{2,1,0:T(8,128)(2,1)}), bf16[16,16,2048]{2,1,0:T(8,128)(2,1)S(1)}, u32[]{:S(2)}, u32[]{:S(2)}) async-start(bf16[16,16,2048]{2,1,0:T(8,128)(2,1)} %bitcast.26), calls=%async_computation | async-start | bytes 2097152 | tf_op jit(solution)/shard_map/all_to_all | solution.py:52
  26.7 9.0 %collective-permute-start.2 = (bf16[64,2048]{1,0:T(8,128)(2,1)S(1)}, bf16[64,2048]{1,0:T(8,128)(2,1)S(1)}, u32[]{:S(2)}, u32[]{:S(2)}) collective-permute-start(bf16[64,2048]{1,0:T(8,128)(2,1)S(1)} %collective-permute-done.refs_3_), channel_id=1, source_target_pairs={{0,2},{2,4},{4,6},{6,8},{8,10},{10,12},{12,14},{14,0},{1,3},{3,5},... | collective-permute-start | bytes 786440 | tf_op jit(solution)/shard_map/ppermute | solution.py:57
  26.7 9.0 %collective-permute-start.3 = (bf16[64,2048]{1,0:T(8,128)(2,1)S(1)}, bf16[64,2048]{1,0:T(8,128)(2,1)S(1)}, u32[]{:S(2)}, u32[]{:S(2)}) collective-permute-start(bf16[64,2048]{1,0:T(8,128)(2,1)S(1)} %collective-permute-done.1.refs_4_), channel_id=1, source_target_pairs={{0,14},{2,0},{4,2},{6,4},{8,6},{10,8},{12,10},{14,12},{1,15},{3,1}... | collective-permute-start | bytes 786440 | tf_op jit(solution)/shard_map/ppermute | solution.py:57
  35.6 8.0 %collective-permute-start.4 = (bf16[64,2048]{1,0:T(8,128)(2,1)S(1)}, bf16[64,2048]{1,0:T(8,128)(2,1)S(1)}, u32[]{:S(2)}, u32[]{:S(2)}) collective-permute-start(bf16[64,2048]{1,0:T(8,128)(2,1)S(1)} %collective-permute-done.2.refs_5_), channel_id=1, source_target_pairs={{0,2},{2,4},{4,6},{6,8},{8,10},{10,12},{12,14},{14,0},{1,3},{3,5},... | collective-permute-start | bytes 786440 | tf_op jit(solution)/shard_map/ppermute | solution.py:57
  36.3 8.1 %collective-permute-start.5 = (bf16[64,2048]{1,0:T(8,128)(2,1)S(1)}, bf16[64,2048]{1,0:T(8,128)(2,1)S(1)}, u32[]{:S(2)}, u32[]{:S(2)}) collective-permute-start(bf16[64,2048]{1,0:T(8,128)(2,1)S(1)} %collective-permute-done.3.refs_6_), channel_id=1, source_target_pairs={{0,14},{2,0},{4,2},{6,4},{8,6},{10,8},{12,10},{14,12},{1,15},{3,1}... | collective-permute-start | bytes 786440 | tf_op jit(solution)/shard_map/ppermute | solution.py:57
  44.4 5.2 %collective-permute-start.6 = (bf16[32,2048]{1,0:T(8,128)(2,1)}, bf16[32,2048]{1,0:T(8,128)(2,1)S(1)}, u32[]{:S(2)}, u32[]{:S(2)}) collective-permute-start(bf16[32,2048]{1,0:T(8,128)(2,1)} %slice.24), channel_id=1, source_target_pairs={{0,2},{2,4},{4,6},{6,8},{8,10},{10,12},{12,14},{14,0},{1,3},{3,5},... | collective-permute-start | bytes 393224 | tf_op jit(solution)/shard_map/ppermute | solution.py:57
  44.4 5.2 %collective-permute-start.7 = (bf16[32,2048]{1,0:T(8,128)(2,1)S(1)}, bf16[32,2048]{1,0:T(8,128)(2,1)S(1)}, u32[]{:S(2)}, u32[]{:S(2)}) collective-permute-start(bf16[32,2048]{1,0:T(8,128)(2,1)S(1)} %slice.25), channel_id=1, source_target_pairs={{0,14},{2,0},{4,2},{6,4},{8,6},{10,8},{12,10},{14,12},{1,15},{3,1}... | collective-permute-start | bytes 393224 | tf_op jit(solution)/shard_map/ppermute | solution.py:57
  54.1 18.8 %all-to-all-start.1 = ((bf16[32,8,512]{2,1,0:T(8,128)(2,1)}), bf16[32,8,512]{2,1,0:T(8,128)(2,1)S(1)}, u32[]{:S(2)}, u32[]{:S(2)}) async-start(bf16[32,8,512]{2,1,0:T(8,128)(2,1)} %bitcast.27), calls=%async_computation.1 | async-start | bytes 524288 | tf_op jit(solution)/shard_map/all_to_all | solution.py:52
  75.3 4.8 %collective-permute-start.10 = (bf16[8,4224]{1,0:T(8,128)(2,1)}, bf16[8,4224]{1,0:T(8,128)(2,1)S(1)}, u32[]{:S(2)}, u32[]{:S(2)}) collective-permute-start(bf16[8,4224]{1,0:T(8,128)(2,1)} %get-tuple-element.16.refs_1_.refs_5_), channel_id=1, source_target_pairs={{0,12},{4,0},{8,4},{12,8},{1,13},{5,1},{9,5},{13,9},{2,14},{6,2},{... | collective-permute-start | bytes 202760 | tf_op jit(solution)/shard_map/ppermute | solution.py:57
  76.4 8.5 %collective-permute-start.9 = (bf16[8,4224]{1,0:T(8,128)(2,1)}, bf16[8,4224]{1,0:T(8,128)(2,1)S(1)}, u32[]{:S(2)}, u32[]{:S(2)}) collective-permute-start(bf16[8,4224]{1,0:T(8,128)(2,1)} %get-tuple-element.16.refs_1_.refs_5_), channel_id=1, source_target_pairs={{0,8},{4,12},{8,0},{12,4},{1,9},{5,13},{9,1},{13,5},{2,10},{6,14},... | collective-permute-start | bytes 202760 | tf_op jit(solution)/shard_map/ppermute | solution.py:57
  77.8 7.8 %collective-permute-start.8 = (bf16[8,4224]{1,0:T(8,128)(2,1)}, bf16[8,4224]{1,0:T(8,128)(2,1)S(1)}, u32[]{:S(2)}, u32[]{:S(2)}) collective-permute-start(bf16[8,4224]{1,0:T(8,128)(2,1)} %get-tuple-element.16.refs_1_.refs_5_), channel_id=1, source_target_pairs={{0,4},{4,8},{8,12},{12,0},{1,5},{5,9},{9,13},{13,1},{2,6},{6,10},{... | collective-permute-start | bytes 202760 | tf_op jit(solution)/shard_map/ppermute | solution.py:57
  89.0 60.3 %copy-start.2 = (bf16[1,4096,384]{2,1,0:T(8,128)(2,1)S(1)}, bf16[1,4096,384]{2,1,0:T(8,128)(2,1)}, u32[]{:S(2)}) copy-start(bf16[1,4096,384]{2,1,0:T(8,128)(2,1)} %refs_1_.1) | copy-start | bytes 9437188
  89.0 60.3 %copy-start.3 = (bf16[1,4096,384]{2,1,0:T(8,128)(2,1)S(1)}, bf16[1,4096,384]{2,1,0:T(8,128)(2,1)}, u32[]{:S(2)}) copy-start(bf16[1,4096,384]{2,1,0:T(8,128)(2,1)} %refs_2_.1) | copy-start | bytes 9437188
  220.9 11.4 %copy-start.14 = (f32[8,4096]{1,0:T(8,128)S(1)}, f32[8,4096]{1,0:T(8,128)}, u32[]{:S(2)}) copy-start(f32[8,4096]{1,0:T(8,128)} %get-tuple-element.15) | copy-start | bytes 393220
  221.7 5.2 %collective-permute-start.11 = (bf16[8,4096]{1,0:T(8,128)(2,1)S(1)}, bf16[8,4096]{1,0:T(8,128)(2,1)S(1)}, u32[]{:S(2)}, u32[]{:S(2)}) collective-permute-start(bf16[8,4096]{1,0:T(8,128)(2,1)S(1)} %get-tuple-element.19), channel_id=1, source_target_pairs={{0,12},{4,0},{8,4},{12,8},{1,13},{5,1},{9,5},{13,9},{2,14},{6,2},{... | collective-permute-start | bytes 196616 | tf_op jit(solution)/shard_map/ppermute | solution.py:57
  222.8 5.3 %collective-permute-start.13 = (bf16[8,4096]{1,0:T(8,128)(2,1)S(1)}, bf16[8,4096]{1,0:T(8,128)(2,1)S(1)}, u32[]{:S(2)}, u32[]{:S(2)}) collective-permute-start(bf16[8,4096]{1,0:T(8,128)(2,1)S(1)} %get-tuple-element.20), channel_id=1, source_target_pairs={{0,4},{4,8},{8,12},{12,0},{1,5},{5,9},{9,13},{13,1},{2,6},{6,10},{... | collective-permute-start | bytes 196616 | tf_op jit(solution)/shard_map/ppermute | solution.py:57
  224.2 8.0 %collective-permute-start.12 = (bf16[8,4096]{1,0:T(8,128)(2,1)S(1)}, bf16[8,4096]{1,0:T(8,128)(2,1)S(1)}, u32[]{:S(2)}, u32[]{:S(2)}) collective-permute-start(bf16[8,4096]{1,0:T(8,128)(2,1)S(1)} %get-tuple-element.21), channel_id=1, source_target_pairs={{0,8},{4,12},{8,0},{12,4},{1,9},{5,13},{9,1},{13,5},{2,10},{6,14},... | collective-permute-start | bytes 196616 | tf_op jit(solution)/shard_map/ppermute | solution.py:57
  (11 other events, 36.0 us)

commit v4 on v3

--- a/solution.py
+++ b/solution.py
@@ -15,7 +15,7 @@
 ROWS_FROM = ("role", "xh", "y")
 SUMS_TO = ("role", "xh", "y", "head")
 NEAR = "zq"
-FAR = ("role", "xh", "y", "zp", "head")
+FAR = ("xh", "head", "y", "zp", "role")
 CAP = 2
 BLOCK = 8
 SLOTS = 8
@@ -57,6 +57,10 @@
     return lax.ppermute(block, axis, [(at, (at + by) % count) for at in range(count)])
 
 
+def held(memory, *arrays):
+    return [pltpu.with_memory_space_constraint(array, memory) for array in arrays]
+
+
 def spread_kernel(attended_ref, out_ref):
     roles, near, rows, _ = out_ref.shape
     for role in range(roles):
@@ -111,8 +115,10 @@
         table = jnp.concatenate([ref[...].astype(jnp.float32) for ref in choices_refs], axis=0).T
         slot = lax.broadcasted_iota(jnp.int32, (count, tokens), 0)
         token = lax.broadcasted_iota(jnp.int32, (count, tokens), 1)
-        place = slot // (2 * SLOTS)
-        expert = (place // 2 * 8 + quad_ref[0] * 2 + place % 2).astype(jnp.float32)
+        far = slot // SLOTS
+        chip = far // 32 * 4 + far // 4 % 4
+        expert = far % 2 * 64 + chip * 8 + quad_ref[0] * 2 + far // 2 % 2
+        expert = expert.astype(jnp.float32)
         levels = table[top_k : 2 * top_k]
         shares = levels / jnp.sum(levels, axis=0, keepdims=True)
         named = jnp.zeros((count, tokens), jnp.float32)
@@ -164,64 +170,69 @@
         compiler_params=pltpu.CompilerParams(
             dimension_semantics=("arbitrary",), vmem_limit_bytes=16 << 20
         ),
-    )(quad, *pool, *pool)
-
-
-def ffn_kernel(unit_steps, rows_ref, gate_ref, up_ref, down_ref, out_ref, active):
+    )(quad, *held(pltpu.HBM, pool[0]), *pool[1:], *held(pltpu.HBM, pool[0]), *pool[1:])
+
+
+def ffn_kernel(unit_steps, rows_ref, gate_ref, up_ref, down_hbm, out_ref, active, down_ref, arrival):
     step = pl.program_id(0)
+    fetch = pltpu.make_async_copy(down_hbm, down_ref, arrival)
+
+    @pl.when(step == 0)
+    def _():
+        fetch.start()
+
+    @pl.when(step == unit_steps)
+    def _():
+        fetch.wait()
 
     @pl.when(step < unit_steps)
     def _():
-        units = gate_ref.shape[1]
+        to = pl.ds(pl.multiple_of(step * LANES, LANES), LANES)
         both = jnp.dot(
             rows_ref[...],
-            jnp.concatenate([gate_ref[...], up_ref[...]], axis=1),
+            jnp.concatenate([gate_ref[0, :, to], up_ref[0, :, to]], axis=1),
             preferred_element_type=jnp.float32,
         )
-        gated = jax.nn.silu(both[:, :units]) * both[:, units:]
-        to = pl.ds(pl.multiple_of(step * units, units), units)
+        gated = jax.nn.silu(both[:, :LANES]) * both[:, LANES:]
         active[:, to] = gated.astype(jnp.bfloat16)
 
     @pl.when(step >= unit_steps)
     def _():
+        columns = out_ref.shape[1]
+        first = jnp.maximum(step - unit_steps, 0) * columns
         out_ref[...] = jnp.dot(
-            active[...], down_ref[...], preferred_element_type=jnp.float32
+            active[...],
+            down_ref[0, :, pl.ds(pl.multiple_of(first, columns), columns)],
+            preferred_element_type=jnp.float32,
         ).astype(jnp.bfloat16)
 
 
 def expert_rows(rows, gate, up, down):
     count, width = rows.shape
     units = gate.shape[2]
-    block, columns = LANES, 1024
-    steps = units // block
-
-    def early(step):
-        return jnp.minimum(step, steps - 1)
-
-    def late(step):
-        return jnp.maximum(step - steps, 0)
-
+    columns = 1024
+    steps = units // LANES
+    whole = pl.BlockSpec(memory_space=pltpu.VMEM)
     return pl.pallas_call(
         lambda *refs: ffn_kernel(steps, *refs),
         out_shape=jax.ShapeDtypeStruct((count, width), jnp.bfloat16),
         grid=(steps + width // columns,),
-        in_specs=[
-            pl.BlockSpec((count, width), lambda s: (0, 0), pipeline_mode=pl.Buffered(1)),
-            pl.BlockSpec((None, width, block), lambda s: (0, 0, early(s))),
-            pl.BlockSpec((None, width, block), lambda s: (0, 0, early(s))),
-            pl.BlockSpec((None, units, columns), lambda s: (0, 0, late(s))),
+        in_specs=[whole] * 3 + [pl.BlockSpec(memory_space=pl.ANY)],
+        out_specs=pl.BlockSpec((count, columns), lambda s: (0, jnp.maximum(s - steps, 0))),
+        scratch_shapes=[
+            pltpu.VMEM((count, units), jnp.bfloat16),
+            pltpu.VMEM(down.shape, jnp.bfloat16),
+            pltpu.SemaphoreType.DMA,
         ],
-        out_specs=pl.BlockSpec((count, columns), lambda s: (0, late(s))),
-        scratch_shapes=[pltpu.VMEM((count, units), jnp.bfloat16)],
         compiler_params=pltpu.CompilerParams(
-            dimension_semantics=("arbitrary",), vmem_limit_bytes=44 << 20
+            dimension_semantics=("arbitrary",), vmem_limit_bytes=16 << 20
         ),
         cost_estimate=pl.CostEstimate(
             flops=6 * count * width * units,
             bytes_accessed=2 * (2 * count * width + 3 * width * units),
             transcendentals=count * units,
         ),
-    )(rows, gate, up, down)
+    )(*held(pltpu.VMEM, rows, gate, up), *held(pltpu.HBM, down))
 
 
 def half_weights(out_proj):
@@ -235,7 +246,6 @@
     near = lax.axis_size("xh") * lax.axis_size("y")
     ring, cols = lax.axis_size(RING), own.shape[0]
     up, down = shift(own, RING, 1), shift(own, RING, -1)
-    attended, up, down = lax.optimization_barrier((attended, up, down))
     whole = pl.BlockSpec(memory_space=pltpu.VMEM)
     sent = pl.pallas_call(
         spread_kernel,
@@ -243,9 +253,10 @@
         in_specs=[whole],
         out_specs=whole,
     )(attended)
+    sent, up, down = lax.optimization_barrier((sent, up, down))
+    pieces, spots = [own, up, down], [(0, 0), (1, 0), (-1, 0)]
     gathered = swap(sent.reshape(roles * near, rows, half), ROWS_FROM)
     gathered = gathered.reshape(roles * near * rows, half)
-    pieces, spots = [own, up, down], [(0, 0), (1, 0), (-1, 0)]
     for by in range(2, ring // 2):
         up, down = shift(up, RING, 1), shift(down, RING, -1)
         pieces, spots = pieces + [up, down], spots + [(by, 0), (-by, 0)]
@@ -255,10 +266,11 @@
     columns = pl.pallas_call(
         lambda *refs: project_kernel(spots, *refs),
         out_shape=jax.ShapeDtypeStruct((roles * near * rows, ring * cols), jnp.bfloat16),
+        grid=(1,),
         in_specs=[pl.BlockSpec(memory_space=pltpu.SMEM)] + [whole] * (len(pieces) + 1),
-        out_specs=whole,
+        out_specs=pl.BlockSpec((roles * near * rows, ring * cols), lambda s: (0, 0)),
         scratch_shapes=[pltpu.VMEM((ring * cols, half), jnp.bfloat16)],
-    )(lax.axis_index(RING).astype(jnp.int32).reshape(1), gathered, *pieces)
+    )(lax.axis_index(RING).astype(jnp.int32).reshape(1), *held(pltpu.VMEM, gathered, *pieces))
     return swap(columns.reshape(2 * roles * near, rows // 2, ring * cols), SUMS_TO)
 
 
@@ -297,7 +309,10 @@
         in_specs=[whole] * 4,
         out_specs=(whole, whole),
     )(
-        arrived.reshape([lax.axis_size(name) for name in SUMS_TO] + list(arrived.shape[1:])),
+        *held(
+            pltpu.VMEM,
+            arrived.reshape([lax.axis_size(name) for name in SUMS_TO] + list(arrived.shape[1:])),
+        ),
         hidden,
         norm_gain.reshape(1, width),
         choices,

time: 234 us -> 221 us (0.944)
  local copies, waits for them, and re-layouts: 7.04 us -> 1.07 us
  Pallas kernels: 21.3 us -> 16.2 us
    unnamed x38 -> x12, local copies, waits for them, and re-layouts: 5.23 us -> 0.03 us
    pallas_call x1, Pallas kernels: 11.3 us -> 7.11 us  [expert_rows(): pl.pallas_call(lambda *refs: ffn_kernel(steps, *refs), out_shape=jax.Shap...]
  transfers between devices with their start and end apart: 16 -> 16, of which waited for: 10 -> 9; matrix products, arithmetic and copies ran while one was open for 4% -> 3% of each run, Pallas kernels for 0% -> 1%
where the time goes in v4:
time: 221 us; the launch traced here: 220 us
  blocking collectives  118 us (53%)
  starting transfers between devices  42.4 us (19%)
  waiting for transfers between devices  33.5 us (15%)
  Pallas kernels  16.2 us (7%)
  matrix products  6.05 us (3%)
  other arithmetic  3.11 us (1%)
    all_to_all x2, blocking collectives, swap(): return lax.all_to_all(blocks, axes, split_axis=0, concat_axis=0, tiled=True)  118 us
    ppermute x14, waiting for transfers between devices, shift(): lax.ppermute(block, axis, [(at, (at + by) % count) for at in range(count)])  25.3 us
    ppermute x14, starting transfers between devices, shift(): lax.ppermute(block, axis, [(at, (at + by) % count) for at in range(count)])  25 us
    all_to_all x2, starting transfers between devices, swap(): return lax.all_to_all(blocks, axes, split_axis=0, concat_axis=0, tiled=True)  17.4 us
    all_to_all x2, waiting for transfers between devices, swap(): return lax.all_to_all(blocks, axes, split_axis=0, concat_axis=0, tiled=True)  8.23 us
    pallas_call x1, Pallas kernels, expert_rows(): pl.pallas_call(lambda *refs: ffn_kernel(steps, *refs), out_shape=jax.Shap...  7.11 us
  transfers between devices with their start and end apart: 16, of which 9 were waited for; matrix products, arithmetic and copies ran while one was open for 3% of the time, Pallas kernels for 1%

profile of v4, /device:TPU:1, one launch (start us, length us, event | category | flops | bytes accessed | tf_op | source)
XLA Modules:
  0.0 220.1 jit_solution(12399117594018010468)
XLA Ops:
  1.0 6.5 %collective-permute-start.1 = (bf16[64,2048]{1,0:T(8,128)(2,1)S(1)}, bf16[64,2048]{1,0:T(8,128)(2,1)S(1)}, u32[]{:S(2)}, u32[]{:S(2)}) collective-permute-start(bf16[64,2048]{1,0:T(8,128)(2,1)S(1)} %dynamic-slice_bitcast_fusion.refs_2_), channel_id=1, source_target_pairs={{0,14},{2,0},{4,2},{6,4},{8,6},{10,8},{12,10},{14,12},{1,15},{3,1}... | collective-permute-start | bytes 786440 | tf_op jit(solution)/shard_map/ppermute | solution.py:57
  9.8 2.0 fusion.16
  12.2 2.3 %fusion.2.attended_ref = bf16[16,2,16,128]{3,2,1,0:T(8,128)(2,1)} fusion(bf16[16,128,2,128]{3,2,1,0:T(2,128)(2,1)} %param.17, f32[16,2,16,128]{3,2,1,0:T(8,128)S(1)} %get-tuple-element.25, f32[16,2,128]{2,1,0:T(2,128)S(1)} %convert_element_type.42, f32[16,2,16]{2,1,0:T(2,128)S(1)} %get-tuple-element.23, f32[16,2,16]{2,1,0:T(2,128)S(1)} %get-tuple-element.22, ...), kind=kOutput, calls=%fused_computation.5 | convolution fusion | flops 17170432 | bytes 1464320 | tf_op jit(solution)/shard_map/bhgt,bthd->bhgd/dot_general | solution.py:43
  14.5 2.2 shard_map.136
  16.7 7.9 %all-to-all-start = ((bf16[16,16,2048]{2,1,0:T(8,128)(2,1)}), bf16[16,16,2048]{2,1,0:T(8,128)(2,1)S(1)}, u32[]{:S(2)}, u32[]{:S(2)}) async-start(bf16[16,16,2048]{2,1,0:T(8,128)(2,1)} %bitcast.29), calls=%async_computation | async-start | bytes 2097152 | tf_op jit(solution)/shard_map/all_to_all | solution.py:52
  24.6 3.0 %collective-permute-start.3 = (bf16[64,2048]{1,0:T(8,128)(2,1)S(1)}, bf16[64,2048]{1,0:T(8,128)(2,1)S(1)}, u32[]{:S(2)}, u32[]{:S(2)}) collective-permute-start(bf16[64,2048]{1,0:T(8,128)(2,1)S(1)} %collective-permute-done.1.refs_4_), channel_id=1, source_target_pairs={{0,14},{2,0},{4,2},{6,4},{8,6},{10,8},{12,10},{14,12},{1,15},{3,1}... | collective-permute-start | bytes 786440 | tf_op jit(solution)/shard_map/ppermute | solution.py:57
  27.6 6.5 %collective-permute-done.2.refs_5_ = bf16[64,2048]{1,0:T(8,128)(2,1)S(1)} collective-permute-done((bf16[64,2048]{1,0:T(8,128)(2,1)S(1)}, bf16[64,2048]{1,0:T(8,128)(2,1)S(1)}, u32[]{:S(2)}, u32[]{:S(2)}) %collective-permute-start.2) | collective-permute-done | bytes 262176 | tf_op jit(solution)/shard_map/ppermute | solution.py:57
  34.1 2.7 %collective-permute-start.5 = (bf16[64,2048]{1,0:T(8,128)(2,1)S(1)}, bf16[64,2048]{1,0:T(8,128)(2,1)S(1)}, u32[]{:S(2)}, u32[]{:S(2)}) collective-permute-start(bf16[64,2048]{1,0:T(8,128)(2,1)S(1)} %collective-permute-done.3.refs_6_), channel_id=1, source_target_pairs={{0,14},{2,0},{4,2},{6,4},{8,6},{10,8},{12,10},{14,12},{1,15},{3,1}... | collective-permute-start | bytes 786440 | tf_op jit(solution)/shard_map/ppermute | solution.py:57
  36.8 5.7 %collective-permute-done.4.refs_7_ = bf16[64,2048]{1,0:T(8,128)(2,1)S(1)} collective-permute-done((bf16[64,2048]{1,0:T(8,128)(2,1)S(1)}, bf16[64,2048]{1,0:T(8,128)(2,1)S(1)}, u32[]{:S(2)}, u32[]{:S(2)}) %collective-permute-start.4) | collective-permute-done | bytes 262176 | tf_op jit(solution)/shard_map/ppermute | solution.py:57
  42.7 2.7 %collective-permute-start.7 = (bf16[32,2048]{1,0:T(8,128)(2,1)S(1)}, bf16[32,2048]{1,0:T(8,128)(2,1)S(1)}, u32[]{:S(2)}, u32[]{:S(2)}) collective-permute-start(bf16[32,2048]{1,0:T(8,128)(2,1)S(1)} %slice.25), channel_id=1, source_target_pairs={{0,14},{2,0},{4,2},{6,4},{8,6},{10,8},{12,10},{14,12},{1,15},{3,1}... | collective-permute-start | bytes 393224 | tf_op jit(solution)/shard_map/ppermute | solution.py:57
  45.4 2.3 %collective-permute-done.6.refs_9_ = bf16[32,2048]{1,0:T(8,128)(2,1)S(1)} collective-permute-done((bf16[32,2048]{1,0:T(8,128)(2,1)S(1)}, bf16[32,2048]{1,0:T(8,128)(2,1)S(1)}, u32[]{:S(2)}, u32[]{:S(2)}) %collective-permute-start.6) | collective-permute-done | bytes 131104 | tf_op jit(solution)/shard_map/ppermute | solution.py:57
  47.7 1.6 shard_map.137
  49.2 9.5 %all-to-all-start.1 = ((bf16[32,8,512]{2,1,0:T(8,128)(2,1)}), bf16[32,8,512]{2,1,0:T(8,128)(2,1)S(1)}, u32[]{:S(2)}, u32[]{:S(2)}) async-start(bf16[32,8,512]{2,1,0:T(8,128)(2,1)} %bitcast.30), calls=%async_computation.1 | async-start | bytes 524288 | tf_op jit(solution)/shard_map/all_to_all | solution.py:52
  59.4 8.2 %all-to-all-done.1 = bf16[32,8,512]{2,1,0:T(8,128)(2,1)S(1)} async-done(((bf16[32,8,512]{2,1,0:T(8,128)(2,1)}), bf16[32,8,512]{2,1,0:T(8,128)(2,1)S(1)}, u32[]{:S(2)}, u32[]{:S(2)}) %all-to-all-start.1) | async-done | bytes 262176 | tf_op jit(solution)/shard_map/all_to_all | solution.py:52
  67.7 1.6 shard_map.138
  70.6 2.5 %collective-permute-start.9 = (bf16[8,4224]{1,0:T(8,128)(2,1)}, bf16[8,4224]{1,0:T(8,128)(2,1)S(1)}, u32[]{:S(2)}, u32[]{:S(2)}) collective-permute-start(bf16[8,4224]{1,0:T(8,128)(2,1)} %get-tuple-element.16.refs_1_.refs_5_), channel_id=1, source_target_pairs={{0,8},{4,12},{8,0},{12,4},{1,9},{5,13},{9,1},{13,5},{2,10},{6,14},... | collective-permute-start | bytes 202760 | tf_op jit(solution)/shard_map/ppermute | solution.py:57
  74.1 3.7 %collective-permute-done.9.refs_3_.refs_7_ = bf16[8,4224]{1,0:T(8,128)(2,1)S(1)} collective-permute-done((bf16[8,4224]{1,0:T(8,128)(2,1)}, bf16[8,4224]{1,0:T(8,128)(2,1)S(1)}, u32[]{:S(2)}, u32[]{:S(2)}) %collective-permute-start.9) | collective-permute-done | bytes 67616 | tf_op jit(solution)/shard_map/ppermute | solution.py:57
  77.9 2.1 collective-permute-done.8.refs_2_.refs_6_
  80.0 3.7 %shard_map.139 = (bf16[512,4096]{1,0:T(8,128)(2,1)S(1)}, bf16[512,32]{1,0:T(8,128)(2,1)S(1)}) custom-call(s32[1]{0:T(128)} %bitcast.11.refs_0_, bf16[8,4224]{1,0:T(8,128)(2,1)} %get-tuple-element.16.refs_1_.refs_5_, bf16[8,4224]{1,0:T(8,128)(2,1)S(1)} %collective-permute-done.8.refs_2_.refs_6_, bf16[8,4224]{1,0:T(8,128)(2,1)S(1)} %collective-permute-done.9.refs_3_.refs_7_, ...), custom_call_target="tpu_custom_call" | custom-call | tf_op jit(solution)/shard_map/pallas_call | solution.py:155
  83.7 59.5 %all_to_all.20 = bf16[64,8,4096]{2,1,0:T(8,128)(2,1)S(1)} all-to-all(bf16[64,8,4096]{2,1,0:T(8,128)(2,1)S(1)} %bitcast.24), channel_id=1, replica_groups=mesh['role'=2,'xh'=2,'y'=4,'zq'=4,'zp'=2,'head'=2] {'xh','head','y','zp'..., dimensions={0} | all-to-all | bytes 8388608 | tf_op jit(solution)/shard_map/all_to_all | solution.py:52
  143.2 7.1 %shard_map.140 = bf16[512,4096]{1,0:T(8,128)(2,1)S(1)} custom-call(bf16[512,4096]{1,0:T(8,128)(2,1)S(1)} %bitcast.25, bf16[1,4096,384]{2,1,0:T(8,128)(2,1)S(1)} %copy-done.1, bf16[1,4096,384]{2,1,0:T(8,128)(2,1)S(1)} %copy-done.2, bf16[1,384,4096]{2,1,0:T(8,128)(2,1)} %refs_3_.1), custom_call_target="tpu_custom_call" | custom-call | flops 4831838208 | bytes 17825792 | tf_op jit(solution)/shard_map/pallas_call | solution.py:216
  150.3 58.0 %all_to_all.21 = bf16[64,8,4096]{2,1,0:T(8,128)(2,1)S(1)} all-to-all(bf16[64,8,4096]{2,1,0:T(8,128)(2,1)S(1)} %bitcast.26), channel_id=1, replica_groups=mesh['role'=2,'xh'=2,'y'=4,'zq'=4,'zp'=2,'head'=2] {'xh','head','y','zp'..., dimensions={0} | all-to-all | bytes 8388608 | tf_op jit(solution)/shard_map/all_to_all | solution.py:52
  211.7 2.8 %collective-permute-start.12 = (bf16[8,4096]{1,0:T(8,128)(2,1)S(1)}, bf16[8,4096]{1,0:T(8,128)(2,1)S(1)}, u32[]{:S(2)}, u32[]{:S(2)}) collective-permute-start(bf16[8,4096]{1,0:T(8,128)(2,1)S(1)} %get-tuple-element.21), channel_id=1, source_target_pairs={{0,8},{4,12},{8,0},{12,4},{1,9},{5,13},{9,1},{13,5},{2,10},{6,14},... | collective-permute-start | bytes 196616 | tf_op jit(solution)/shard_map/ppermute | solution.py:57
  215.9 3.5 %collective-permute-done.12 = bf16[8,4096]{1,0:T(8,128)(2,1)S(1)} collective-permute-done((bf16[8,4096]{1,0:T(8,128)(2,1)S(1)}, bf16[8,4096]{1,0:T(8,128)(2,1)S(1)}, u32[]{:S(2)}, u32[]{:S(2)}) %collective-permute-start.12) | collective-permute-done | bytes 65568 | tf_op jit(solution)/shard_map/ppermute | solution.py:57
  (44 shorter events, 12.2 us)
Async XLA Ops:
  0.0 8.9 %copy-start = (bf16[16,32,128]{2,1,0:T(8,128)(2,1)S(1)}, bf16[16,32,128]{2,1,0:T(8,128)(2,1)}, u32[]{:S(2)}) copy-start(bf16[16,32,128]{2,1,0:T(8,128)(2,1)} %param.15) | copy-start | bytes 393220
  1.0 15.7 %collective-permute-start.1 = (bf16[64,2048]{1,0:T(8,128)(2,1)S(1)}, bf16[64,2048]{1,0:T(8,128)(2,1)S(1)}, u32[]{:S(2)}, u32[]{:S(2)}) collective-permute-start(bf16[64,2048]{1,0:T(8,128)(2,1)S(1)} %dynamic-slice_bitcast_fusion.refs_2_), channel_id=1, source_target_pairs={{0,14},{2,0},{4,2},{6,4},{8,6},{10,8},{12,10},{14,12},{1,15},{3,1}... | collective-permute-start | bytes 786440 | tf_op jit(solution)/shard_map/ppermute | solution.py:57
  7.5 9.2 %collective-permute-start = (bf16[64,2048]{1,0:T(8,128)(2,1)S(1)}, bf16[64,2048]{1,0:T(8,128)(2,1)S(1)}, u32[]{:S(2)}, u32[]{:S(2)}) collective-permute-start(bf16[64,2048]{1,0:T(8,128)(2,1)S(1)} %dynamic-slice_bitcast_fusion.refs_2_), channel_id=1, source_target_pairs={{0,2},{2,4},{4,6},{6,8},{8,10},{10,12},{12,14},{14,0},{1,3},{3,5},... | collective-permute-start | bytes 786440 | tf_op jit(solution)/shard_map/ppermute | solution.py:57
  14.5 44.2 %copy-start.4 = (s32[8,8]{1,0:T(8,128)S(1)}, s32[8,8]{1,0:T(8,128)}, u32[]{:S(2)}) copy-start(s32[8,8]{1,0:T(8,128)} %param.26) | copy-start | bytes 772
  14.5 44.3 %copy-start.5 = (s32[8,8]{1,0:T(8,128)S(1)}, s32[8,8]{1,0:T(8,128)}, u32[]{:S(2)}) copy-start(s32[8,8]{1,0:T(8,128)} %param.27) | copy-start | bytes 772
  16.7 31.0 %all-to-all-start = ((bf16[16,16,2048]{2,1,0:T(8,128)(2,1)}), bf16[16,16,2048]{2,1,0:T(8,128)(2,1)S(1)}, u32[]{:S(2)}, u32[]{:S(2)}) async-start(bf16[16,16,2048]{2,1,0:T(8,128)(2,1)} %bitcast.29), calls=%async_computation | async-start | bytes 2097152 | tf_op jit(solution)/shard_map/all_to_all | solution.py:52
  24.6 9.6 %collective-permute-start.2 = (bf16[64,2048]{1,0:T(8,128)(2,1)S(1)}, bf16[64,2048]{1,0:T(8,128)(2,1)S(1)}, u32[]{:S(2)}, u32[]{:S(2)}) collective-permute-start(bf16[64,2048]{1,0:T(8,128)(2,1)S(1)} %collective-permute-done.refs_3_), channel_id=1, source_target_pairs={{0,2},{2,4},{4,6},{6,8},{8,10},{10,12},{12,14},{14,0},{1,3},{3,5},... | collective-permute-start | bytes 786440 | tf_op jit(solution)/shard_map/ppermute | solution.py:57
  24.6 9.6 %collective-permute-start.3 = (bf16[64,2048]{1,0:T(8,128)(2,1)S(1)}, bf16[64,2048]{1,0:T(8,128)(2,1)S(1)}, u32[]{:S(2)}, u32[]{:S(2)}) collective-permute-start(bf16[64,2048]{1,0:T(8,128)(2,1)S(1)} %collective-permute-done.1.refs_4_), channel_id=1, source_target_pairs={{0,14},{2,0},{4,2},{6,4},{8,6},{10,8},{12,10},{14,12},{1,15},{3,1}... | collective-permute-start | bytes 786440 | tf_op jit(solution)/shard_map/ppermute | solution.py:57
  34.1 8.4 %collective-permute-start.4 = (bf16[64,2048]{1,0:T(8,128)(2,1)S(1)}, bf16[64,2048]{1,0:T(8,128)(2,1)S(1)}, u32[]{:S(2)}, u32[]{:S(2)}) collective-permute-start(bf16[64,2048]{1,0:T(8,128)(2,1)S(1)} %collective-permute-done.2.refs_5_), channel_id=1, source_target_pairs={{0,2},{2,4},{4,6},{6,8},{8,10},{10,12},{12,14},{14,0},{1,3},{3,5},... | collective-permute-start | bytes 786440 | tf_op jit(solution)/shard_map/ppermute | solution.py:57
  34.1 8.5 %collective-permute-start.5 = (bf16[64,2048]{1,0:T(8,128)(2,1)S(1)}, bf16[64,2048]{1,0:T(8,128)(2,1)S(1)}, u32[]{:S(2)}, u32[]{:S(2)}) collective-permute-start(bf16[64,2048]{1,0:T(8,128)(2,1)S(1)} %collective-permute-done.3.refs_6_), channel_id=1, source_target_pairs={{0,14},{2,0},{4,2},{6,4},{8,6},{10,8},{12,10},{14,12},{1,15},{3,1}... | collective-permute-start | bytes 786440 | tf_op jit(solution)/shard_map/ppermute | solution.py:57
  42.5 5.1 %collective-permute-start.6 = (bf16[32,2048]{1,0:T(8,128)(2,1)S(1)}, bf16[32,2048]{1,0:T(8,128)(2,1)S(1)}, u32[]{:S(2)}, u32[]{:S(2)}) collective-permute-start(bf16[32,2048]{1,0:T(8,128)(2,1)S(1)} %slice.24), channel_id=1, source_target_pairs={{0,2},{2,4},{4,6},{6,8},{8,10},{10,12},{12,14},{14,0},{1,3},{3,5},... | collective-permute-start | bytes 393224 | tf_op jit(solution)/shard_map/ppermute | solution.py:57
  42.7 5.0 %collective-permute-start.7 = (bf16[32,2048]{1,0:T(8,128)(2,1)S(1)}, bf16[32,2048]{1,0:T(8,128)(2,1)S(1)}, u32[]{:S(2)}, u32[]{:S(2)}) collective-permute-start(bf16[32,2048]{1,0:T(8,128)(2,1)S(1)} %slice.25), channel_id=1, source_target_pairs={{0,14},{2,0},{4,2},{6,4},{8,6},{10,8},{12,10},{14,12},{1,15},{3,1}... | collective-permute-start | bytes 393224 | tf_op jit(solution)/shard_map/ppermute | solution.py:57
  49.2 18.4 %all-to-all-start.1 = ((bf16[32,8,512]{2,1,0:T(8,128)(2,1)}), bf16[32,8,512]{2,1,0:T(8,128)(2,1)S(1)}, u32[]{:S(2)}, u32[]{:S(2)}) async-start(bf16[32,8,512]{2,1,0:T(8,128)(2,1)} %bitcast.30), calls=%async_computation.1 | async-start | bytes 524288 | tf_op jit(solution)/shard_map/all_to_all | solution.py:52
  69.3 4.8 %collective-permute-start.10 = (bf16[8,4224]{1,0:T(8,128)(2,1)}, bf16[8,4224]{1,0:T(8,128)(2,1)S(1)}, u32[]{:S(2)}, u32[]{:S(2)}) collective-permute-start(bf16[8,4224]{1,0:T(8,128)(2,1)} %get-tuple-element.16.refs_1_.refs_5_), channel_id=1, source_target_pairs={{0,12},{4,0},{8,4},{12,8},{1,13},{5,1},{9,5},{13,9},{2,14},{6,2},{... | collective-permute-start | bytes 202760 | tf_op jit(solution)/shard_map/ppermute | solution.py:57
  70.6 7.3 %collective-permute-start.9 = (bf16[8,4224]{1,0:T(8,128)(2,1)}, bf16[8,4224]{1,0:T(8,128)(2,1)S(1)}, u32[]{:S(2)}, u32[]{:S(2)}) collective-permute-start(bf16[8,4224]{1,0:T(8,128)(2,1)} %get-tuple-element.16.refs_1_.refs_5_), channel_id=1, source_target_pairs={{0,8},{4,12},{8,0},{12,4},{1,9},{5,13},{9,1},{13,5},{2,10},{6,14},... | collective-permute-start | bytes 202760 | tf_op jit(solution)/shard_map/ppermute | solution.py:57
  73.1 6.9 %collective-permute-start.8 = (bf16[8,4224]{1,0:T(8,128)(2,1)}, bf16[8,4224]{1,0:T(8,128)(2,1)S(1)}, u32[]{:S(2)}, u32[]{:S(2)}) collective-permute-start(bf16[8,4224]{1,0:T(8,128)(2,1)} %get-tuple-element.16.refs_1_.refs_5_), channel_id=1, source_target_pairs={{0,4},{4,8},{8,12},{12,0},{1,5},{5,9},{9,13},{13,1},{2,6},{6,10},{... | collective-permute-start | bytes 202760 | tf_op jit(solution)/shard_map/ppermute | solution.py:57
  83.7 59.6 %copy-start.1 = (bf16[1,4096,384]{2,1,0:T(8,128)(2,1)S(1)}, bf16[1,4096,384]{2,1,0:T(8,128)(2,1)}, u32[]{:S(2)}) copy-start(bf16[1,4096,384]{2,1,0:T(8,128)(2,1)} %refs_1_.1) | copy-start | bytes 9437188
  83.7 59.6 %copy-start.2 = (bf16[1,4096,384]{2,1,0:T(8,128)(2,1)S(1)}, bf16[1,4096,384]{2,1,0:T(8,128)(2,1)}, u32[]{:S(2)}) copy-start(bf16[1,4096,384]{2,1,0:T(8,128)(2,1)} %refs_2_.1) | copy-start | bytes 9437188
  208.4 11.0 %copy-start.3 = (f32[8,4096]{1,0:T(8,128)S(1)}, f32[8,4096]{1,0:T(8,128)}, u32[]{:S(2)}) copy-start(f32[8,4096]{1,0:T(8,128)} %get-tuple-element.15) | copy-start | bytes 393220
  209.3 5.6 %collective-permute-start.11 = (bf16[8,4096]{1,0:T(8,128)(2,1)S(1)}, bf16[8,4096]{1,0:T(8,128)(2,1)S(1)}, u32[]{:S(2)}, u32[]{:S(2)}) collective-permute-start(bf16[8,4096]{1,0:T(8,128)(2,1)S(1)} %get-tuple-element.19), channel_id=1, source_target_pairs={{0,12},{4,0},{8,4},{12,8},{1,13},{5,1},{9,5},{13,9},{2,14},{6,2},{... | collective-permute-start | bytes 196616 | tf_op jit(solution)/shard_map/ppermute | solution.py:57
  210.6 5.3 %collective-permute-start.13 = (bf16[8,4096]{1,0:T(8,128)(2,1)S(1)}, bf16[8,4096]{1,0:T(8,128)(2,1)S(1)}, u32[]{:S(2)}, u32[]{:S(2)}) collective-permute-start(bf16[8,4096]{1,0:T(8,128)(2,1)S(1)} %get-tuple-element.20), channel_id=1, source_target_pairs={{0,4},{4,8},{8,12},{12,0},{1,5},{5,9},{9,13},{13,1},{2,6},{6,10},{... | collective-permute-start | bytes 196616 | tf_op jit(solution)/shard_map/ppermute | solution.py:57
  211.7 7.7 %collective-permute-start.12 = (bf16[8,4096]{1,0:T(8,128)(2,1)S(1)}, bf16[8,4096]{1,0:T(8,128)(2,1)S(1)}, u32[]{:S(2)}, u32[]{:S(2)}) collective-permute-start(bf16[8,4096]{1,0:T(8,128)(2,1)S(1)} %get-tuple-element.21), channel_id=1, source_target_pairs={{0,8},{4,12},{8,0},{12,4},{1,9},{5,13},{9,1},{13,5},{2,10},{6,14},... | collective-permute-start | bytes 196616 | tf_op jit(solution)/shard_map/ppermute | solution.py:57

commit v5 on v4

--- a/solution.py
+++ b/solution.py
@@ -20,32 +20,86 @@
 BLOCK = 8
 SLOTS = 8
 LANES = 128
-
-
-def attend_block(query_rows, key_rows, value_rows, key_new, value_new, valid_len):
-    row_count = query_rows.shape[0]
-    kv_heads = key_rows.shape[2]
-    group_size = query_rows.shape[1] // kv_heads
-    head_dim = query_rows.shape[2]
-    scaling = 1.0 / math.sqrt(head_dim)
-    query_f = query_rows.astype(jnp.float32).reshape(row_count, kv_heads, group_size, head_dim)
-    scores = jnp.einsum("bhgd,bthd->bhgt", query_f, key_rows.astype(jnp.float32)) * scaling
-    scores_new = jnp.einsum("bhgd,bhd->bhg", query_f, key_new.astype(jnp.float32)) * scaling
-    positions = jnp.arange(key_rows.shape[1], dtype=jnp.int32)
-    usable = (positions[None, :] < valid_len[:, None])[:, None, None, :]
-    masked = jnp.where(usable, scores, -1e30)
-    highest = jnp.maximum(jnp.max(masked, axis=-1), scores_new)
-    exp_terms = jnp.exp(masked - highest[..., None])
-    exp_new = jnp.exp(scores_new - highest)
-    totals = jnp.sum(exp_terms, axis=-1) + exp_new
-    weights = (exp_terms / totals[..., None]).astype(jnp.bfloat16)
-    weight_new = (exp_new / totals).astype(jnp.bfloat16)
-    blended = jnp.einsum("bhgt,bthd->bhgd", weights, value_rows, preferred_element_type=jnp.float32)
-    blended = (
-        blended
-        + weight_new.astype(jnp.float32)[..., None] * value_new.astype(jnp.float32)[:, :, None, :]
+RING_COST = 5 * 10**9
+
+
+def attend_kernel(
+    queries_ref, keys_ref, values_ref, new_keys_ref, new_values_ref, lengths_ref, out_ref,
+    scores, blended
+):
+    requests, columns, size = keys_ref.shape
+    heads = queries_ref.shape[1]
+    kv_heads = new_keys_ref.shape[1]
+    group = heads // kv_heads
+    scaling = 1.0 / math.sqrt(size)
+    for request in range(requests):
+        scores[request] = lax.dot_general(
+            queries_ref[request],
+            keys_ref[request],
+            (((1,), (1,)), ((), ())),
+            preferred_element_type=jnp.float32,
+        )
+    row = lax.broadcasted_iota(jnp.int32, (heads, columns), 0)
+    column = lax.broadcasted_iota(jnp.int32, (heads, columns), 1)
+    own = row // group == column % kv_heads
+    position = column // kv_heads
+    first = lax.broadcasted_iota(jnp.int32, (heads, size), 0) < group
+
+    def of_head(pair_ref, request):
+        pair = pair_ref[request].astype(jnp.float32)
+        return jnp.where(first, pair[0:1], pair[1:2])
+
+    for request in range(requests):
+        query = queries_ref[request].astype(jnp.float32)
+        latest = jnp.sum(query * of_head(new_keys_ref, request), axis=1, keepdims=True) * scaling
+        usable = own & (position < lengths_ref[request])
+        masked = jnp.where(usable, scores[request] * scaling, -1e30)
+        highest = jnp.maximum(jnp.max(masked, axis=1, keepdims=True), latest)
+        terms = jnp.exp(masked - highest)
+        newest = jnp.exp(latest - highest)
+        total = jnp.sum(terms, axis=1, keepdims=True) + newest
+        weights = (terms / total).astype(jnp.bfloat16)
+        weight = (newest / total).astype(jnp.bfloat16).astype(jnp.float32)
+        blend = jnp.dot(weights, values_ref[request], preferred_element_type=jnp.float32)
+        blend = blend + weight * of_head(new_values_ref, request)
+        blended[request * heads : (request + 1) * heads, :] = blend
+    roles, near, rows, _ = out_ref.shape
+    for role in range(roles):
+        for head in range(group):
+            part = blended[pl.ds(role * group + head, rows, stride=heads), :]
+            part = part.astype(jnp.bfloat16)
+            for copy in range(near):
+                out_ref[role, copy, :, head * LANES : (head + 1) * LANES] = part
+
+
+def attend(queries, keys, values, new_keys, new_values, lengths, near):
+    rows, heads, size = queries.shape
+    positions, kv_heads = keys.shape[1:3]
+    columns = positions * kv_heads
+    whole = pl.BlockSpec(memory_space=pltpu.VMEM)
+    return pl.pallas_call(
+        attend_kernel,
+        out_shape=jax.ShapeDtypeStruct(
+            (kv_heads, near, rows, heads // kv_heads * size), jnp.bfloat16
+        ),
+        in_specs=[whole] * 5 + [pl.BlockSpec(memory_space=pltpu.SMEM)],
+        out_specs=whole,
+        scratch_shapes=[
+            pltpu.VMEM((rows, heads, columns), jnp.float32),
+            pltpu.VMEM((rows * heads, size), jnp.float32),
+        ],
+        compiler_params=pltpu.CompilerParams(vmem_limit_bytes=16 << 20),
+    )(
+        *held(
+            pltpu.HBM,
+            queries,
+            keys.reshape(rows, columns, size),
+            values.reshape(rows, columns, size),
+            new_keys,
+            new_values,
+        ),
+        lengths,
     )
-    return blended.astype(jnp.bfloat16)
 
 
 def swap(blocks, axes):
@@ -61,13 +115,10 @@
     return [pltpu.with_memory_space_constraint(array, memory) for array in arrays]
 
 
-def spread_kernel(attended_ref, out_ref):
-    roles, near, rows, _ = out_ref.shape
-    for role in range(roles):
-        for head in range(attended_ref.shape[2]):
-            part = attended_ref[:, role, head, :]
-            for copy in range(near):
-                out_ref[role, copy, :, head * LANES : (head + 1) * LANES] = part
+def join_kernel(top_ref, bottom_ref, out_ref):
+    part = top_ref.shape[0]
+    out_ref[:part, :] = top_ref[...]
+    out_ref[part:, :] = bottom_ref[...]
 
 
 def project_kernel(spots, at_ref, rows_ref, *refs):
@@ -240,19 +291,11 @@
     return lax.dynamic_slice_in_dim(out_proj.T, lax.axis_index("role") * half, half, axis=1)
 
 
-def project(attended, own):
-    rows, roles, group, head_dim = attended.shape
-    half = group * head_dim
-    near = lax.axis_size("xh") * lax.axis_size("y")
+def project(sent, own):
+    roles, near, rows, half = sent.shape
     ring, cols = lax.axis_size(RING), own.shape[0]
     up, down = shift(own, RING, 1), shift(own, RING, -1)
     whole = pl.BlockSpec(memory_space=pltpu.VMEM)
-    sent = pl.pallas_call(
-        spread_kernel,
-        out_shape=jax.ShapeDtypeStruct((roles, near, rows, half), jnp.bfloat16),
-        in_specs=[whole],
-        out_specs=whole,
-    )(attended)
     sent, up, down = lax.optimization_barrier((sent, up, down))
     pieces, spots = [own, up, down], [(0, 0), (1, 0), (-1, 0)]
     gathered = swap(sent.reshape(roles * near, rows, half), ROWS_FROM)
@@ -261,8 +304,16 @@
         up, down = shift(up, RING, 1), shift(down, RING, -1)
         pieces, spots = pieces + [up, down], spots + [(by, 0), (-by, 0)]
     part = cols // 2
-    pieces = pieces + [shift(up[:part], RING, 1), shift(down[part:], RING, -1)]
-    spots = spots + [(ring // 2, 0), (ring // 2, part)]
+    last = shift(up[:part], RING, 1), shift(down[part:], RING, -1)
+    across = pl.pallas_call(
+        join_kernel,
+        out_shape=jax.ShapeDtypeStruct(own.shape, jnp.bfloat16),
+        grid=(1,),
+        in_specs=[whole, whole],
+        out_specs=pl.BlockSpec(own.shape, lambda s: (0, 0)),
+        cost_estimate=pl.CostEstimate(flops=RING_COST, bytes_accessed=0, transcendentals=0),
+    )(*held(pltpu.VMEM, *last))
+    pieces, spots = pieces + [across], spots + [(ring // 2, 0)]
     columns = pl.pallas_call(
         lambda *refs: project_kernel(spots, *refs),
         out_shape=jax.ShapeDtypeStruct((roles * near * rows, ring * cols), jnp.bfloat16),
@@ -295,8 +346,9 @@
     near, far = lax.axis_size(NEAR), lax.axis_size(FAR)
 
     own = half_weights(out_proj)
-    attended = attend_block(queries, cache_keys, cache_values, new_keys, new_values, lengths)
-    arrived = project(attended, own)
+    copies = lax.axis_size("xh") * lax.axis_size("y")
+    sent = attend(queries, cache_keys, cache_values, new_keys, new_values, lengths, copies)
+    arrived = project(sent, own)
     choices = jnp.concatenate([expert_ids, gate_levels], axis=1).astype(jnp.bfloat16)
     choices = jnp.pad(choices, ((0, 0), (0, LANES - 2 * top_k)))
     whole = pl.BlockSpec(memory_space=pltpu.VMEM)

time: 221 us -> 215 us (0.973)
  matrix products: 6.05 us -> 0.86 us
  starting transfers between devices: 42.4 us -> 39.7 us
    dot_general x3 -> x0, matrix products: 5.19 us -> none  [the longest x1 2.34 us: attend_block(): jnp.einsum('bhgt,bthd->bhgd', weights, value_rows, preferred_element_type...]
    all_to_all x2, waiting for transfers between devices: 8.23 us -> 10.6 us  [swap(): return lax.all_to_all(blocks, axes, split_axis=0, concat_axis=0, tiled=True)]
    ppermute x14, waiting for transfers between devices: 25.3 us -> 23 us  [shift(): lax.ppermute(block, axis, [(at, (at + by) % count) for at in range(count)])]
  transfers between devices with their start and end apart: 16 -> 16, of which waited for: 9 -> 11; matrix products, arithmetic and copies ran while one was open for 3% -> 0% of each run, Pallas kernels for 1% -> 2%
where the time goes in v5:
time: 215 us
  blocking collectives  118 us (55%)
  starting transfers between devices  39.7 us (18%)
  waiting for transfers between devices  33.6 us (16%)
  Pallas kernels  18.3 us (9%)
  local copies, waits for them, and re-layouts  2.63 us (1%)
    all_to_all x2, blocking collectives, swap(): return lax.all_to_all(blocks, axes, split_axis=0, concat_axis=0, tiled=True)  118 us
    ppermute x14, starting transfers between devices, shift(): lax.ppermute(block, axis, [(at, (at + by) % count) for at in range(count)])  24 us
    ppermute x14, waiting for transfers between devices, shift(): lax.ppermute(block, axis, [(at, (at + by) % count) for at in range(count)])  23 us
    all_to_all x2, starting transfers between devices, swap(): return lax.all_to_all(blocks, axes, split_axis=0, concat_axis=0, tiled=True)  15.7 us
    all_to_all x2, waiting for transfers between devices, swap(): return lax.all_to_all(blocks, axes, split_axis=0, concat_axis=0, tiled=True)  10.6 us
    pallas_call x1, Pallas kernels, expert_rows(): pl.pallas_call(lambda *refs: ffn_kernel(steps, *refs), out_shape=jax.Shap...  7.11 us
  transfers between devices with their start and end apart: 16, of which 11 were waited for; matrix products, arithmetic and copies ran while one was open for 0% of the time, Pallas kernels for 2%

profile of v5, /device:TPU:1, one launch (start us, length us, event | category | flops | bytes accessed | tf_op | source)
XLA Modules:
  0.0 214.9 jit_solution(3516962283732751557)
XLA Ops:
  1.0 6.5 %collective-permute-start.1 = (bf16[64,2048]{1,0:T(8,128)(2,1)S(1)}, bf16[64,2048]{1,0:T(8,128)(2,1)S(1)}, u32[]{:S(2)}, u32[]{:S(2)}) collective-permute-start(bf16[64,2048]{1,0:T(8,128)(2,1)S(1)} %dynamic-slice_bitcast_fusion.refs_2_), channel_id=1, source_target_pairs={{0,14},{2,0},{4,2},{6,4},{8,6},{10,8},{12,10},{14,12},{1,15},{3,1}... | collective-permute-start | bytes 786440 | tf_op jit(solution)/shard_map/ppermute | solution.py:111
  8.1 3.6 %shard_map.136 = bf16[2,8,16,2048]{3,2,1,0:T(8,128)(2,1)} custom-call(bf16[16,32,128]{2,1,0:T(8,128)(2,1)} %queries_ref.1, bf16[16,256,128]{2,1,0:T(8,128)(2,1)} %bitcast.24, bf16[16,256,128]{2,1,0:T(8,128)(2,1)} %bitcast.25, bf16[16,2,128]{2,1,0:T(2,128)(2,1)} %new_keys_ref.1, bf16[16,2,128]{2,1,0:T(2,128)(2,1)} %new_values_ref.1, s32[16]{0:T(128)S(1)} %copy-done.1), custom_call_target="tpu_custom_call" | custom-call | tf_op jit(solution)/shard_map/pallas_call | solution.py:80
  12.4 3.1 %collective-permute-done.refs_3_ = bf16[64,2048]{1,0:T(8,128)(2,1)S(1)} collective-permute-done((bf16[64,2048]{1,0:T(8,128)(2,1)S(1)}, bf16[64,2048]{1,0:T(8,128)(2,1)S(1)}, u32[]{:S(2)}, u32[]{:S(2)}) %collective-permute-start) | collective-permute-done | bytes 262176 | tf_op jit(solution)/shard_map/ppermute | solution.py:111
  15.5 2.7 %collective-permute-start.3 = (bf16[64,2048]{1,0:T(8,128)(2,1)S(1)}, bf16[64,2048]{1,0:T(8,128)(2,1)S(1)}, u32[]{:S(2)}, u32[]{:S(2)}) collective-permute-start(bf16[64,2048]{1,0:T(8,128)(2,1)S(1)} %collective-permute-done.1.refs_4_), channel_id=1, source_target_pairs={{0,14},{2,0},{4,2},{6,4},{8,6},{10,8},{12,10},{14,12},{1,15},{3,1}... | collective-permute-start | bytes 786440 | tf_op jit(solution)/shard_map/ppermute | solution.py:111
  18.2 9.4 %all-to-all-start = ((bf16[16,16,2048]{2,1,0:T(8,128)(2,1)}), bf16[16,16,2048]{2,1,0:T(8,128)(2,1)S(1)}, u32[]{:S(2)}, u32[]{:S(2)}) async-start(bf16[16,16,2048]{2,1,0:T(8,128)(2,1)} %bitcast.4), calls=%async_computation | async-start | bytes 2097152 | tf_op jit(solution)/shard_map/all_to_all | solution.py:106
  27.7 2.7 %collective-permute-start.5 = (bf16[64,2048]{1,0:T(8,128)(2,1)S(1)}, bf16[64,2048]{1,0:T(8,128)(2,1)S(1)}, u32[]{:S(2)}, u32[]{:S(2)}) collective-permute-start(bf16[64,2048]{1,0:T(8,128)(2,1)S(1)} %collective-permute-done.3.refs_6_), channel_id=1, source_target_pairs={{0,14},{2,0},{4,2},{6,4},{8,6},{10,8},{12,10},{14,12},{1,15},{3,1}... | collective-permute-start | bytes 786440 | tf_op jit(solution)/shard_map/ppermute | solution.py:111
  30.4 6.4 %collective-permute-done.4.refs_7_ = bf16[64,2048]{1,0:T(8,128)(2,1)S(1)} collective-permute-done((bf16[64,2048]{1,0:T(8,128)(2,1)S(1)}, bf16[64,2048]{1,0:T(8,128)(2,1)S(1)}, u32[]{:S(2)}, u32[]{:S(2)}) %collective-permute-start.4) | collective-permute-done | bytes 262176 | tf_op jit(solution)/shard_map/ppermute | solution.py:111
  36.9 2.7 %collective-permute-start.7 = (bf16[32,2048]{1,0:T(8,128)(2,1)S(1)}, bf16[32,2048]{1,0:T(8,128)(2,1)S(1)}, u32[]{:S(2)}, u32[]{:S(2)}) collective-permute-start(bf16[32,2048]{1,0:T(8,128)(2,1)S(1)} %slice.25), channel_id=1, source_target_pairs={{0,14},{2,0},{4,2},{6,4},{8,6},{10,8},{12,10},{14,12},{1,15},{3,1}... | collective-permute-start | bytes 393224 | tf_op jit(solution)/shard_map/ppermute | solution.py:111
  39.6 2.6 %collective-permute-done.6.top_ref = bf16[32,2048]{1,0:T(8,128)(2,1)S(1)} collective-permute-done((bf16[32,2048]{1,0:T(8,128)(2,1)S(1)}, bf16[32,2048]{1,0:T(8,128)(2,1)S(1)}, u32[]{:S(2)}, u32[]{:S(2)}) %collective-permute-start.6) | collective-permute-done | bytes 131104 | tf_op jit(solution)/shard_map/ppermute | solution.py:111
  42.9 2.4 %all-to-all-done = bf16[16,16,2048]{2,1,0:T(8,128)(2,1)S(1)} async-done(((bf16[16,16,2048]{2,1,0:T(8,128)(2,1)}), bf16[16,16,2048]{2,1,0:T(8,128)(2,1)S(1)}, u32[]{:S(2)}, u32[]{:S(2)}) %all-to-all-start) | async-done | bytes 1048608 | tf_op jit(solution)/shard_map/all_to_all | solution.py:106
  46.2 1.6 shard_map.138
  47.8 6.3 %all-to-all-start.1 = ((bf16[32,8,512]{2,1,0:T(8,128)(2,1)}), bf16[32,8,512]{2,1,0:T(8,128)(2,1)S(1)}, u32[]{:S(2)}, u32[]{:S(2)}) async-start(bf16[32,8,512]{2,1,0:T(8,128)(2,1)} %bitcast.23), calls=%async_computation.1 | async-start | bytes 524288 | tf_op jit(solution)/shard_map/all_to_all | solution.py:106
  54.8 8.2 %all-to-all-done.1 = bf16[32,8,512]{2,1,0:T(8,128)(2,1)S(1)} async-done(((bf16[32,8,512]{2,1,0:T(8,128)(2,1)}), bf16[32,8,512]{2,1,0:T(8,128)(2,1)S(1)}, u32[]{:S(2)}, u32[]{:S(2)}) %all-to-all-start.1) | async-done | bytes 262176 | tf_op jit(solution)/shard_map/all_to_all | solution.py:106
  63.1 1.6 shard_map.139
  66.0 1.4 collective-permute-start.9
  68.5 1.5 collective-permute-done.10.refs_4_.refs_8_
  70.0 4.5 %collective-permute-done.9.refs_3_.refs_7_ = bf16[8,4224]{1,0:T(8,128)(2,1)S(1)} collective-permute-done((bf16[8,4224]{1,0:T(8,128)(2,1)}, bf16[8,4224]{1,0:T(8,128)(2,1)S(1)}, u32[]{:S(2)}, u32[]{:S(2)}) %collective-permute-start.9) | collective-permute-done | bytes 67616 | tf_op jit(solution)/shard_map/ppermute | solution.py:111
  74.5 3.7 %shard_map.140 = (bf16[512,4096]{1,0:T(8,128)(2,1)S(1)}, bf16[512,32]{1,0:T(8,128)(2,1)S(1)}) custom-call(s32[1]{0:T(128)} %bitcast.9.refs_0_, bf16[8,4224]{1,0:T(8,128)(2,1)} %get-tuple-element.16.refs_1_.refs_5_, bf16[8,4224]{1,0:T(8,128)(2,1)S(1)} %collective-permute-done.8.refs_2_.refs_6_, bf16[8,4224]{1,0:T(8,128)(2,1)S(1)} %collective-permute-done.9.refs_3_.refs_7_, ...), custom_call_target="tpu_custom_call" | custom-call | tf_op jit(solution)/shard_map/pallas_call | solution.py:206
  78.2 60.3 %all_to_all.20 = bf16[64,8,4096]{2,1,0:T(8,128)(2,1)S(1)} all-to-all(bf16[64,8,4096]{2,1,0:T(8,128)(2,1)S(1)} %bitcast.18), channel_id=1, replica_groups=mesh['role'=2,'xh'=2,'y'=4,'zq'=4,'zp'=2,'head'=2] {'xh','head','y','zp'..., dimensions={0} | all-to-all | bytes 8388608 | tf_op jit(solution)/shard_map/all_to_all | solution.py:106
  138.5 7.1 %shard_map.141 = bf16[512,4096]{1,0:T(8,128)(2,1)S(1)} custom-call(bf16[512,4096]{1,0:T(8,128)(2,1)S(1)} %bitcast.19, bf16[1,4096,384]{2,1,0:T(8,128)(2,1)S(1)} %copy-done.2, bf16[1,4096,384]{2,1,0:T(8,128)(2,1)S(1)} %copy-done.3, bf16[1,384,4096]{2,1,0:T(8,128)(2,1)} %refs_3_.1), custom_call_target="tpu_custom_call" | custom-call | flops 4831838208 | bytes 17825792 | tf_op jit(solution)/shard_map/pallas_call | solution.py:267
  145.6 58.0 %all_to_all.21 = bf16[64,8,4096]{2,1,0:T(8,128)(2,1)S(1)} all-to-all(bf16[64,8,4096]{2,1,0:T(8,128)(2,1)S(1)} %bitcast.20), channel_id=1, replica_groups=mesh['role'=2,'xh'=2,'y'=4,'zq'=4,'zp'=2,'head'=2] {'xh','head','y','zp'..., dimensions={0} | all-to-all | bytes 8388608 | tf_op jit(solution)/shard_map/all_to_all | solution.py:106
  204.5 1.4 collective-permute-start.11
  207.0 3.1 %collective-permute-start.12 = (bf16[8,4096]{1,0:T(8,128)(2,1)S(1)}, bf16[8,4096]{1,0:T(8,128)(2,1)S(1)}, u32[]{:S(2)}, u32[]{:S(2)}) collective-permute-start(bf16[8,4096]{1,0:T(8,128)(2,1)S(1)} %get-tuple-element.21), channel_id=1, source_target_pairs={{0,8},{4,12},{8,0},{12,4},{1,9},{5,13},{9,1},{13,5},{2,10},{6,14},... | collective-permute-start | bytes 196616 | tf_op jit(solution)/shard_map/ppermute | solution.py:111
  211.2 3.0 %collective-permute-done.12 = bf16[8,4096]{1,0:T(8,128)(2,1)S(1)} collective-permute-done((bf16[8,4096]{1,0:T(8,128)(2,1)S(1)}, bf16[8,4096]{1,0:T(8,128)(2,1)S(1)}, u32[]{:S(2)}, u32[]{:S(2)}) %collective-permute-start.12) | collective-permute-done | bytes 65568 | tf_op jit(solution)/shard_map/ppermute | solution.py:111
  (39 shorter events, 11.0 us)
Async XLA Ops:
  1.0 11.5 %collective-permute-start.1 = (bf16[64,2048]{1,0:T(8,128)(2,1)S(1)}, bf16[64,2048]{1,0:T(8,128)(2,1)S(1)}, u32[]{:S(2)}, u32[]{:S(2)}) collective-permute-start(bf16[64,2048]{1,0:T(8,128)(2,1)S(1)} %dynamic-slice_bitcast_fusion.refs_2_), channel_id=1, source_target_pairs={{0,14},{2,0},{4,2},{6,4},{8,6},{10,8},{12,10},{14,12},{1,15},{3,1}... | collective-permute-start | bytes 786440 | tf_op jit(solution)/shard_map/ppermute | solution.py:111
  7.5 8.1 %collective-permute-start = (bf16[64,2048]{1,0:T(8,128)(2,1)S(1)}, bf16[64,2048]{1,0:T(8,128)(2,1)S(1)}, u32[]{:S(2)}, u32[]{:S(2)}) collective-permute-start(bf16[64,2048]{1,0:T(8,128)(2,1)S(1)} %dynamic-slice_bitcast_fusion.refs_2_), channel_id=1, source_target_pairs={{0,2},{2,4},{4,6},{6,8},{8,10},{10,12},{12,14},{14,0},{1,3},{3,5},... | collective-permute-start | bytes 786440 | tf_op jit(solution)/shard_map/ppermute | solution.py:111
  7.5 0.7 copy-start.1
  15.5 12.1 %collective-permute-start.2 = (bf16[64,2048]{1,0:T(8,128)(2,1)S(1)}, bf16[64,2048]{1,0:T(8,128)(2,1)S(1)}, u32[]{:S(2)}, u32[]{:S(2)}) collective-permute-start(bf16[64,2048]{1,0:T(8,128)(2,1)S(1)} %collective-permute-done.refs_3_), channel_id=1, source_target_pairs={{0,2},{2,4},{4,6},{6,8},{8,10},{10,12},{12,14},{14,0},{1,3},{3,5},... | collective-permute-start | bytes 786440 | tf_op jit(solution)/shard_map/ppermute | solution.py:111
  15.5 12.1 %collective-permute-start.3 = (bf16[64,2048]{1,0:T(8,128)(2,1)S(1)}, bf16[64,2048]{1,0:T(8,128)(2,1)S(1)}, u32[]{:S(2)}, u32[]{:S(2)}) collective-permute-start(bf16[64,2048]{1,0:T(8,128)(2,1)S(1)} %collective-permute-done.1.refs_4_), channel_id=1, source_target_pairs={{0,14},{2,0},{4,2},{6,4},{8,6},{10,8},{12,10},{14,12},{1,15},{3,1}... | collective-permute-start | bytes 786440 | tf_op jit(solution)/shard_map/ppermute | solution.py:111
  18.2 27.0 %all-to-all-start = ((bf16[16,16,2048]{2,1,0:T(8,128)(2,1)}), bf16[16,16,2048]{2,1,0:T(8,128)(2,1)S(1)}, u32[]{:S(2)}, u32[]{:S(2)}) async-start(bf16[16,16,2048]{2,1,0:T(8,128)(2,1)} %bitcast.4), calls=%async_computation | async-start | bytes 2097152 | tf_op jit(solution)/shard_map/all_to_all | solution.py:106
  27.6 9.2 %collective-permute-start.4 = (bf16[64,2048]{1,0:T(8,128)(2,1)S(1)}, bf16[64,2048]{1,0:T(8,128)(2,1)S(1)}, u32[]{:S(2)}, u32[]{:S(2)}) collective-permute-start(bf16[64,2048]{1,0:T(8,128)(2,1)S(1)} %collective-permute-done.2.refs_5_), channel_id=1, source_target_pairs={{0,2},{2,4},{4,6},{6,8},{8,10},{10,12},{12,14},{14,0},{1,3},{3,5},... | collective-permute-start | bytes 786440 | tf_op jit(solution)/shard_map/ppermute | solution.py:111
  27.7 9.2 %collective-permute-start.5 = (bf16[64,2048]{1,0:T(8,128)(2,1)S(1)}, bf16[64,2048]{1,0:T(8,128)(2,1)S(1)}, u32[]{:S(2)}, u32[]{:S(2)}) collective-permute-start(bf16[64,2048]{1,0:T(8,128)(2,1)S(1)} %collective-permute-done.3.refs_6_), channel_id=1, source_target_pairs={{0,14},{2,0},{4,2},{6,4},{8,6},{10,8},{12,10},{14,12},{1,15},{3,1}... | collective-permute-start | bytes 786440 | tf_op jit(solution)/shard_map/ppermute | solution.py:111
  36.7 5.4 %collective-permute-start.6 = (bf16[32,2048]{1,0:T(8,128)(2,1)S(1)}, bf16[32,2048]{1,0:T(8,128)(2,1)S(1)}, u32[]{:S(2)}, u32[]{:S(2)}) collective-permute-start(bf16[32,2048]{1,0:T(8,128)(2,1)S(1)} %slice.24), channel_id=1, source_target_pairs={{0,2},{2,4},{4,6},{6,8},{8,10},{10,12},{12,14},{14,0},{1,3},{3,5},... | collective-permute-start | bytes 393224 | tf_op jit(solution)/shard_map/ppermute | solution.py:111
  36.9 5.3 %collective-permute-start.7 = (bf16[32,2048]{1,0:T(8,128)(2,1)S(1)}, bf16[32,2048]{1,0:T(8,128)(2,1)S(1)}, u32[]{:S(2)}, u32[]{:S(2)}) collective-permute-start(bf16[32,2048]{1,0:T(8,128)(2,1)S(1)} %slice.25), channel_id=1, source_target_pairs={{0,14},{2,0},{4,2},{6,4},{8,6},{10,8},{12,10},{14,12},{1,15},{3,1}... | collective-permute-start | bytes 393224 | tf_op jit(solution)/shard_map/ppermute | solution.py:111
  39.6 14.5 %copy-start.5 = (s32[8,8]{1,0:T(8,128)S(1)}, s32[8,8]{1,0:T(8,128)}, u32[]{:S(2)}) copy-start(s32[8,8]{1,0:T(8,128)} %param.26) | copy-start | bytes 772
  39.6 14.6 %copy-start.6 = (s32[8,8]{1,0:T(8,128)S(1)}, s32[8,8]{1,0:T(8,128)}, u32[]{:S(2)}) copy-start(s32[8,8]{1,0:T(8,128)} %param.27) | copy-start | bytes 772
  45.2 1.0 copy-start
  47.8 15.3 %all-to-all-start.1 = ((bf16[32,8,512]{2,1,0:T(8,128)(2,1)}), bf16[32,8,512]{2,1,0:T(8,128)(2,1)S(1)}, u32[]{:S(2)}, u32[]{:S(2)}) async-start(bf16[32,8,512]{2,1,0:T(8,128)(2,1)} %bitcast.23), calls=%async_computation.1 | async-start | bytes 524288 | tf_op jit(solution)/shard_map/all_to_all | solution.py:106
  64.7 5.3 %collective-permute-start.10 = (bf16[8,4224]{1,0:T(8,128)(2,1)}, bf16[8,4224]{1,0:T(8,128)(2,1)S(1)}, u32[]{:S(2)}, u32[]{:S(2)}) collective-permute-start(bf16[8,4224]{1,0:T(8,128)(2,1)} %get-tuple-element.16.refs_1_.refs_5_), channel_id=1, source_target_pairs={{0,12},{4,0},{8,4},{12,8},{1,13},{5,1},{9,5},{13,9},{2,14},{6,2},{... | collective-permute-start | bytes 202760 | tf_op jit(solution)/shard_map/ppermute | solution.py:111
  66.0 8.6 %collective-permute-start.9 = (bf16[8,4224]{1,0:T(8,128)(2,1)}, bf16[8,4224]{1,0:T(8,128)(2,1)S(1)}, u32[]{:S(2)}, u32[]{:S(2)}) collective-permute-start(bf16[8,4224]{1,0:T(8,128)(2,1)} %get-tuple-element.16.refs_1_.refs_5_), channel_id=1, source_target_pairs={{0,8},{4,12},{8,0},{12,4},{1,9},{5,13},{9,1},{13,5},{2,10},{6,14},... | collective-permute-start | bytes 202760 | tf_op jit(solution)/shard_map/ppermute | solution.py:111
  67.4 7.1 %collective-permute-start.8 = (bf16[8,4224]{1,0:T(8,128)(2,1)}, bf16[8,4224]{1,0:T(8,128)(2,1)S(1)}, u32[]{:S(2)}, u32[]{:S(2)}) collective-permute-start(bf16[8,4224]{1,0:T(8,128)(2,1)} %get-tuple-element.16.refs_1_.refs_5_), channel_id=1, source_target_pairs={{0,4},{4,8},{8,12},{12,0},{1,5},{5,9},{9,13},{13,1},{2,6},{6,10},{... | collective-permute-start | bytes 202760 | tf_op jit(solution)/shard_map/ppermute | solution.py:111
  78.2 60.3 %copy-start.2 = (bf16[1,4096,384]{2,1,0:T(8,128)(2,1)S(1)}, bf16[1,4096,384]{2,1,0:T(8,128)(2,1)}, u32[]{:S(2)}) copy-start(bf16[1,4096,384]{2,1,0:T(8,128)(2,1)} %refs_1_.1) | copy-start | bytes 9437188
  78.2 60.3 %copy-start.3 = (bf16[1,4096,384]{2,1,0:T(8,128)(2,1)S(1)}, bf16[1,4096,384]{2,1,0:T(8,128)(2,1)}, u32[]{:S(2)}) copy-start(bf16[1,4096,384]{2,1,0:T(8,128)(2,1)} %refs_2_.1) | copy-start | bytes 9437188
  203.6 10.6 %copy-start.4 = (f32[8,4096]{1,0:T(8,128)S(1)}, f32[8,4096]{1,0:T(8,128)}, u32[]{:S(2)}) copy-start(f32[8,4096]{1,0:T(8,128)} %get-tuple-element.15) | copy-start | bytes 393220
  204.5 5.6 %collective-permute-start.11 = (bf16[8,4096]{1,0:T(8,128)(2,1)S(1)}, bf16[8,4096]{1,0:T(8,128)(2,1)S(1)}, u32[]{:S(2)}, u32[]{:S(2)}) collective-permute-start(bf16[8,4096]{1,0:T(8,128)(2,1)S(1)} %get-tuple-element.19), channel_id=1, source_target_pairs={{0,12},{4,0},{8,4},{12,8},{1,13},{5,1},{9,5},{13,9},{2,14},{6,2},{... | collective-permute-start | bytes 196616 | tf_op jit(solution)/shard_map/ppermute | solution.py:111
  205.9 5.3 %collective-permute-start.13 = (bf16[8,4096]{1,0:T(8,128)(2,1)S(1)}, bf16[8,4096]{1,0:T(8,128)(2,1)S(1)}, u32[]{:S(2)}, u32[]{:S(2)}) collective-permute-start(bf16[8,4096]{1,0:T(8,128)(2,1)S(1)} %get-tuple-element.20), channel_id=1, source_target_pairs={{0,4},{4,8},{8,12},{12,0},{1,5},{5,9},{9,13},{13,1},{2,6},{6,10},{... | collective-permute-start | bytes 196616 | tf_op jit(solution)/shard_map/ppermute | solution.py:111
  207.0 7.2 %collective-permute-start.12 = (bf16[8,4096]{1,0:T(8,128)(2,1)S(1)}, bf16[8,4096]{1,0:T(8,128)(2,1)S(1)}, u32[]{:S(2)}, u32[]{:S(2)}) collective-permute-start(bf16[8,4096]{1,0:T(8,128)(2,1)S(1)} %get-tuple-element.21), channel_id=1, source_target_pairs={{0,8},{4,12},{8,0},{12,4},{1,9},{5,13},{9,1},{13,5},{2,10},{6,14},... | collective-permute-start | bytes 196616 | tf_op jit(solution)/shard_map/ppermute | solution.py:111

commit v6 on v5

--- a/solution.py
+++ b/solution.py
@@ -115,13 +115,11 @@
     return [pltpu.with_memory_space_constraint(array, memory) for array in arrays]
 
 
-def join_kernel(top_ref, bottom_ref, out_ref):
-    part = top_ref.shape[0]
-    out_ref[:part, :] = top_ref[...]
-    out_ref[part:, :] = bottom_ref[...]
-
-
-def project_kernel(spots, at_ref, rows_ref, *refs):
+def token_kernel(top_ref, bottom_ref, out_ref):
+    out_ref[...] = top_ref[:BLOCK, :LANES] + bottom_ref[:BLOCK, :LANES]
+
+
+def project_kernel(spots, at_ref, _, rows_ref, *refs):
     pieces, out_ref, weights = refs[:-2], refs[-2], refs[-1]
     width = pieces[0].shape[0]
     count = weights.shape[0] // width
@@ -291,12 +289,12 @@
     return lax.dynamic_slice_in_dim(out_proj.T, lax.axis_index("role") * half, half, axis=1)
 
 
-def project(sent, own):
+def project(sent, own, choices):
     roles, near, rows, half = sent.shape
     ring, cols = lax.axis_size(RING), own.shape[0]
     up, down = shift(own, RING, 1), shift(own, RING, -1)
     whole = pl.BlockSpec(memory_space=pltpu.VMEM)
-    sent, up, down = lax.optimization_barrier((sent, up, down))
+    sent, up, down, choices = lax.optimization_barrier((sent, up, down, choices))
     pieces, spots = [own, up, down], [(0, 0), (1, 0), (-1, 0)]
     gathered = swap(sent.reshape(roles * near, rows, half), ROWS_FROM)
     gathered = gathered.reshape(roles * near * rows, half)
@@ -305,24 +303,25 @@
         pieces, spots = pieces + [up, down], spots + [(by, 0), (-by, 0)]
     part = cols // 2
     last = shift(up[:part], RING, 1), shift(down[part:], RING, -1)
-    across = pl.pallas_call(
-        join_kernel,
-        out_shape=jax.ShapeDtypeStruct(own.shape, jnp.bfloat16),
-        grid=(1,),
+    pieces = pieces + list(last)
+    spots = spots + [(ring // 2, 0), (ring // 2, part)]
+    token = pl.pallas_call(
+        token_kernel,
+        out_shape=jax.ShapeDtypeStruct((BLOCK, LANES), jnp.bfloat16),
         in_specs=[whole, whole],
-        out_specs=pl.BlockSpec(own.shape, lambda s: (0, 0)),
+        out_specs=whole,
         cost_estimate=pl.CostEstimate(flops=RING_COST, bytes_accessed=0, transcendentals=0),
     )(*held(pltpu.VMEM, *last))
-    pieces, spots = pieces + [across], spots + [(ring // 2, 0)]
     columns = pl.pallas_call(
         lambda *refs: project_kernel(spots, *refs),
         out_shape=jax.ShapeDtypeStruct((roles * near * rows, ring * cols), jnp.bfloat16),
         grid=(1,),
-        in_specs=[pl.BlockSpec(memory_space=pltpu.SMEM)] + [whole] * (len(pieces) + 1),
+        in_specs=[pl.BlockSpec(memory_space=pltpu.SMEM), pl.BlockSpec(memory_space=pl.ANY)]
+        + [whole] * (len(pieces) + 1),
         out_specs=pl.BlockSpec((roles * near * rows, ring * cols), lambda s: (0, 0)),
         scratch_shapes=[pltpu.VMEM((ring * cols, half), jnp.bfloat16)],
-    )(lax.axis_index(RING).astype(jnp.int32).reshape(1), *held(pltpu.VMEM, gathered, *pieces))
-    return swap(columns.reshape(2 * roles * near, rows // 2, ring * cols), SUMS_TO)
+    )(lax.axis_index(RING).astype(jnp.int32).reshape(1), token, *held(pltpu.VMEM, gathered, *pieces))
+    return choices, swap(columns.reshape(2 * roles * near, rows // 2, ring * cols), SUMS_TO)
 
 
 def on_device(
@@ -348,9 +347,9 @@
     own = half_weights(out_proj)
     copies = lax.axis_size("xh") * lax.axis_size("y")
     sent = attend(queries, cache_keys, cache_values, new_keys, new_values, lengths, copies)
-    arrived = project(sent, own)
     choices = jnp.concatenate([expert_ids, gate_levels], axis=1).astype(jnp.bfloat16)
     choices = jnp.pad(choices, ((0, 0), (0, LANES - 2 * top_k)))
+    choices, arrived = project(sent, own, choices)
     whole = pl.BlockSpec(memory_space=pltpu.VMEM)
     residual, sent = pl.pallas_call(
         norm_kernel,
@@ -370,7 +369,8 @@
         choices,
     )
 
-    pool = [sent] + [shift(sent, NEAR, by) for by in range(1, near)]
+    places = sorted(range(1, near), key=lambda by: min(by, near - by))
+    pool = [sent] + [shift(sent, NEAR, by) for by in places]
     outgoing, scaled = pick_rows(pool, width, top_k)
     incoming = swap(outgoing.reshape(far, SLOTS, width), FAR).reshape(far * SLOTS, width)
     half_out = expert_rows(incoming, expert_gate, expert_up, expert_down)
@@ -379,7 +379,8 @@
         scaled, returned, (((0,), (0,)), ((), ())), preferred_element_type=jnp.float32
     ).astype(jnp.bfloat16)
     parts = [mixed[:tokens]] + [
-        shift(mixed[by * tokens : (by + 1) * tokens], NEAR, -by) for by in range(1, near)
+        shift(mixed[at * tokens : (at + 1) * tokens], NEAR, -places[at - 1])
+        for at in range(near - 1, 0, -1)
     ]
     mixture = sum(part.astype(jnp.float32) for part in parts)
     return (residual + mixture).astype(jnp.bfloat16)

time: 215 us -> 215 us (level)
  blocking collectives: 118 us -> 134 us
  waiting for transfers between devices: 33.6 us -> 22.8 us
  starting transfers between devices: 39.7 us -> 34.3 us
    all_to_all x2 -> x3, blocking collectives: 118 us -> 134 us  [swap(): return lax.all_to_all(blocks, axes, split_axis=0, concat_axis=0, tiled=True)]
    all_to_all x2 -> x1, waiting for transfers between devices: 10.6 us -> 2.49 us  [swap(): return lax.all_to_all(blocks, axes, split_axis=0, concat_axis=0, tiled=True)]
    all_to_all x2 -> x1, starting transfers between devices: 15.7 us -> 9.37 us  [swap(): return lax.all_to_all(blocks, axes, split_axis=0, concat_axis=0, tiled=True)]
    ppermute x14, waiting for transfers between devices: 23 us -> 20.3 us  [shift(): lax.ppermute(block, axis, [(at, (at + by) % count) for at in range(count)])]
  transfers between devices with their start and end apart: 16 -> 15, of which waited for: 11 -> 9; matrix products, arithmetic and copies ran while one was open for 0% -> 1% of each run, Pallas kernels for 2% -> 2%
where the time goes in v6:
time: 215 us; the launch traced here: 214 us
  blocking collectives  134 us (62%)
  starting transfers between devices  34.3 us (16%)
  waiting for transfers between devices  22.8 us (11%)
  Pallas kernels  18.1 us (8%)
  other arithmetic  2.72 us (1%)
    all_to_all x3, blocking collectives, swap(): return lax.all_to_all(blocks, axes, split_axis=0, concat_axis=0, tiled=True)  134 us
    ppermute x14, starting transfers between devices, shift(): lax.ppermute(block, axis, [(at, (at + by) % count) for at in range(count)])  24.9 us
    ppermute x14, waiting for transfers between devices, shift(): lax.ppermute(block, axis, [(at, (at + by) % count) for at in range(count)])  20.3 us
    all_to_all x1, starting transfers between devices, swap(): return lax.all_to_all(blocks, axes, split_axis=0, concat_axis=0, tiled=True)  9.37 us
    pallas_call x1, Pallas kernels, expert_rows(): pl.pallas_call(lambda *refs: ffn_kernel(steps, *refs), out_shape=jax.Shap...  7.12 us
  transfers between devices with their start and end apart: 15, of which 9 were waited for; matrix products, arithmetic and copies ran while one was open for 1% of the time, Pallas kernels for 2%

profile of v6, /device:TPU:1, one launch (start us, length us, event | category | flops | bytes accessed | tf_op | source)
XLA Modules:
  0.0 214.1 jit_solution(5694820185054838293)
XLA Ops:
  1.0 6.5 %collective-permute-start.1 = (bf16[64,2048]{1,0:T(8,128)(2,1)S(1)}, bf16[64,2048]{1,0:T(8,128)(2,1)S(1)}, u32[]{:S(2)}, u32[]{:S(2)}) collective-permute-start(bf16[64,2048]{1,0:T(8,128)(2,1)S(1)} %dynamic-slice_bitcast_fusion.refs_3_), channel_id=1, source_target_pairs={{0,14},{2,0},{4,2},{6,4},{8,6},{10,8},{12,10},{14,12},{1,15},{3,1}... | collective-permute-start | bytes 786440 | tf_op jit(solution)/shard_map/ppermute | solution.py:111
  9.5 3.6 %shard_map.136 = bf16[2,8,16,2048]{3,2,1,0:T(8,128)(2,1)} custom-call(bf16[16,32,128]{2,1,0:T(8,128)(2,1)} %queries_ref.1, bf16[16,256,128]{2,1,0:T(8,128)(2,1)} %bitcast.24, bf16[16,256,128]{2,1,0:T(8,128)(2,1)} %bitcast.25, bf16[16,2,128]{2,1,0:T(2,128)(2,1)} %new_keys_ref.1, bf16[16,2,128]{2,1,0:T(2,128)(2,1)} %new_values_ref.1, s32[16]{0:T(128)S(1)} %copy-done), custom_call_target="tpu_custom_call" | custom-call | tf_op jit(solution)/shard_map/pallas_call | solution.py:80
  13.7 1.8 collective-permute-done.refs_4_
  15.5 2.7 %collective-permute-start.5 = (bf16[64,2048]{1,0:T(8,128)(2,1)S(1)}, bf16[64,2048]{1,0:T(8,128)(2,1)S(1)}, u32[]{:S(2)}, u32[]{:S(2)}) collective-permute-start(bf16[64,2048]{1,0:T(8,128)(2,1)S(1)} %collective-permute-done.1.refs_5_), channel_id=1, source_target_pairs={{0,14},{2,0},{4,2},{6,4},{8,6},{10,8},{12,10},{14,12},{1,15},{3,1}... | collective-permute-start | bytes 786440 | tf_op jit(solution)/shard_map/ppermute | solution.py:111
  18.2 9.4 %all-to-all-start = ((bf16[16,16,2048]{2,1,0:T(8,128)(2,1)}), bf16[16,16,2048]{2,1,0:T(8,128)(2,1)S(1)}, u32[]{:S(2)}, u32[]{:S(2)}) async-start(bf16[16,16,2048]{2,1,0:T(8,128)(2,1)} %bitcast.4), calls=%async_computation | async-start | bytes 2097152 | tf_op jit(solution)/shard_map/all_to_all | solution.py:106
  27.7 2.7 %collective-permute-start.6 = (bf16[64,2048]{1,0:T(8,128)(2,1)S(1)}, bf16[64,2048]{1,0:T(8,128)(2,1)S(1)}, u32[]{:S(2)}, u32[]{:S(2)}) collective-permute-start(bf16[64,2048]{1,0:T(8,128)(2,1)S(1)} %collective-permute-done.5.refs_7_), channel_id=1, source_target_pairs={{0,14},{2,0},{4,2},{6,4},{8,6},{10,8},{12,10},{14,12},{1,15},{3,1}... | collective-permute-start | bytes 786440 | tf_op jit(solution)/shard_map/ppermute | solution.py:111
  30.4 6.4 %collective-permute-done.3.refs_8_ = bf16[64,2048]{1,0:T(8,128)(2,1)S(1)} collective-permute-done((bf16[64,2048]{1,0:T(8,128)(2,1)S(1)}, bf16[64,2048]{1,0:T(8,128)(2,1)S(1)}, u32[]{:S(2)}, u32[]{:S(2)}) %collective-permute-start.3) | collective-permute-done | bytes 262176 | tf_op jit(solution)/shard_map/ppermute | solution.py:111
  36.9 2.7 %collective-permute-start.7 = (bf16[32,2048]{1,0:T(8,128)(2,1)S(1)}, bf16[32,2048]{1,0:T(8,128)(2,1)S(1)}, u32[]{:S(2)}, u32[]{:S(2)}) collective-permute-start(bf16[32,2048]{1,0:T(8,128)(2,1)S(1)} %slice.25), channel_id=1, source_target_pairs={{0,14},{2,0},{4,2},{6,4},{8,6},{10,8},{12,10},{14,12},{1,15},{3,1}... | collective-permute-start | bytes 393224 | tf_op jit(solution)/shard_map/ppermute | solution.py:111
  39.6 2.6 %collective-permute-done.4.top_ref.refs_10_ = bf16[32,2048]{1,0:T(8,128)(2,1)S(1)} collective-permute-done((bf16[32,2048]{1,0:T(8,128)(2,1)S(1)}, bf16[32,2048]{1,0:T(8,128)(2,1)S(1)}, u32[]{:S(2)}, u32[]{:S(2)}) %collective-permute-start.4) | collective-permute-done | bytes 131104 | tf_op jit(solution)/shard_map/ppermute | solution.py:111
  42.8 2.5 %all-to-all-done = bf16[16,16,2048]{2,1,0:T(8,128)(2,1)S(1)} async-done(((bf16[16,16,2048]{2,1,0:T(8,128)(2,1)}), bf16[16,16,2048]{2,1,0:T(8,128)(2,1)S(1)}, u32[]{:S(2)}, u32[]{:S(2)}) %all-to-all-start) | async-done | bytes 1048608 | tf_op jit(solution)/shard_map/all_to_all | solution.py:106
  45.2 1.6 shard_map.138
  46.8 15.1 %all_to_all.20 = bf16[32,8,512]{2,1,0:T(8,128)(2,1)S(1)} all-to-all(bf16[32,8,512]{2,1,0:T(8,128)(2,1)} %bitcast.23), channel_id=1, replica_groups=mesh['role'=2,'xh'=2,'y'=4,'zq'=4,'zp'=2,'head'=2] {'role','xh','y','head'}, dimensions={0} | all-to-all | bytes 524288 | tf_op jit(solution)/shard_map/all_to_all | solution.py:106
  62.0 1.6 shard_map.139
  63.6 1.4 collective-permute-start.10
  65.0 1.3 collective-permute-start.9
  67.4 3.5 %collective-permute-done.10.refs_4_.refs_8_ = bf16[8,4224]{1,0:T(8,128)(2,1)S(1)} collective-permute-done((bf16[8,4224]{1,0:T(8,128)(2,1)}, bf16[8,4224]{1,0:T(8,128)(2,1)S(1)}, u32[]{:S(2)}, u32[]{:S(2)}) %collective-permute-start.10) | collective-permute-done | bytes 67616 | tf_op jit(solution)/shard_map/ppermute | solution.py:111
  70.8 1.3 collective-permute-done.9.refs_3_.refs_7_
  72.5 3.7 %shard_map.140 = (bf16[512,4096]{1,0:T(8,128)(2,1)S(1)}, bf16[512,32]{1,0:T(8,128)(2,1)S(1)}) custom-call(s32[1]{0:T(128)} %bitcast.9.refs_0_, bf16[8,4224]{1,0:T(8,128)(2,1)} %get-tuple-element.18.refs_1_.refs_5_, bf16[8,4224]{1,0:T(8,128)(2,1)S(1)} %collective-permute-done.8.refs_2_.refs_6_, bf16[8,4224]{1,0:T(8,128)(2,1)S(1)} %collective-permute-done.9.refs_3_.refs_7_, ...), custom_call_target="tpu_custom_call" | custom-call | tf_op jit(solution)/shard_map/pallas_call | solution.py:204
  76.1 60.4 %all_to_all.21 = bf16[64,8,4096]{2,1,0:T(8,128)(2,1)S(1)} all-to-all(bf16[64,8,4096]{2,1,0:T(8,128)(2,1)S(1)} %bitcast.19), channel_id=1, replica_groups=mesh['role'=2,'xh'=2,'y'=4,'zq'=4,'zp'=2,'head'=2] {'xh','head','y','zp'..., dimensions={0} | all-to-all | bytes 8388608 | tf_op jit(solution)/shard_map/all_to_all | solution.py:106
  136.5 7.1 %shard_map.141 = bf16[512,4096]{1,0:T(8,128)(2,1)S(1)} custom-call(bf16[512,4096]{1,0:T(8,128)(2,1)S(1)} %bitcast.20, bf16[1,4096,384]{2,1,0:T(8,128)(2,1)S(1)} %copy-done.1, bf16[1,4096,384]{2,1,0:T(8,128)(2,1)S(1)} %copy-done.2, bf16[1,384,4096]{2,1,0:T(8,128)(2,1)} %refs_3_.1), custom_call_target="tpu_custom_call" | custom-call | flops 4831838208 | bytes 17825792 | tf_op jit(solution)/shard_map/pallas_call | solution.py:265
  143.6 58.0 %all_to_all.22 = bf16[64,8,4096]{2,1,0:T(8,128)(2,1)S(1)} all-to-all(bf16[64,8,4096]{2,1,0:T(8,128)(2,1)S(1)} %bitcast.21), channel_id=1, replica_groups=mesh['role'=2,'xh'=2,'y'=4,'zq'=4,'zp'=2,'head'=2] {'xh','head','y','zp'..., dimensions={0} | all-to-all | bytes 8388608 | tf_op jit(solution)/shard_map/all_to_all | solution.py:106
  202.6 4.1 %collective-permute-start.11 = (bf16[8,4096]{1,0:T(8,128)(2,1)S(1)}, bf16[8,4096]{1,0:T(8,128)(2,1)S(1)}, u32[]{:S(2)}, u32[]{:S(2)}) collective-permute-start(bf16[8,4096]{1,0:T(8,128)(2,1)S(1)} %get-tuple-element.21), channel_id=1, source_target_pairs={{0,8},{4,12},{8,0},{12,4},{1,9},{5,13},{9,1},{13,5},{2,10},{6,14},... | collective-permute-start | bytes 196616 | tf_op jit(solution)/shard_map/ppermute | solution.py:111
  206.6 2.4 %collective-permute-start.12 = (bf16[8,4096]{1,0:T(8,128)(2,1)S(1)}, bf16[8,4096]{1,0:T(8,128)(2,1)S(1)}, u32[]{:S(2)}, u32[]{:S(2)}) collective-permute-start(bf16[8,4096]{1,0:T(8,128)(2,1)S(1)} %get-tuple-element.23), channel_id=1, source_target_pairs={{0,4},{4,8},{8,12},{12,0},{1,5},{5,9},{9,13},{13,1},{2,6},{6,10},{... | collective-permute-start | bytes 196616 | tf_op jit(solution)/shard_map/ppermute | solution.py:111
  209.7 3.7 %collective-permute-done.13 = bf16[8,4096]{1,0:T(8,128)(2,1)S(1)} collective-permute-done((bf16[8,4096]{1,0:T(8,128)(2,1)S(1)}, bf16[8,4096]{1,0:T(8,128)(2,1)S(1)}, u32[]{:S(2)}, u32[]{:S(2)}) %collective-permute-start.13) | collective-permute-done | bytes 65568 | tf_op jit(solution)/shard_map/ppermute | solution.py:111
  (32 shorter events, 8.2 us)
Async XLA Ops:
  1.0 12.7 %collective-permute-start.1 = (bf16[64,2048]{1,0:T(8,128)(2,1)S(1)}, bf16[64,2048]{1,0:T(8,128)(2,1)S(1)}, u32[]{:S(2)}, u32[]{:S(2)}) collective-permute-start(bf16[64,2048]{1,0:T(8,128)(2,1)S(1)} %dynamic-slice_bitcast_fusion.refs_3_), channel_id=1, source_target_pairs={{0,14},{2,0},{4,2},{6,4},{8,6},{10,8},{12,10},{14,12},{1,15},{3,1}... | collective-permute-start | bytes 786440 | tf_op jit(solution)/shard_map/ppermute | solution.py:111
  7.5 8.1 %collective-permute-start = (bf16[64,2048]{1,0:T(8,128)(2,1)S(1)}, bf16[64,2048]{1,0:T(8,128)(2,1)S(1)}, u32[]{:S(2)}, u32[]{:S(2)}) collective-permute-start(bf16[64,2048]{1,0:T(8,128)(2,1)S(1)} %dynamic-slice_bitcast_fusion.refs_3_), channel_id=1, source_target_pairs={{0,2},{2,4},{4,6},{6,8},{8,10},{10,12},{12,14},{14,0},{1,3},{3,5},... | collective-permute-start | bytes 786440 | tf_op jit(solution)/shard_map/ppermute | solution.py:111
  8.8 0.7 copy-start
  15.5 12.1 %collective-permute-start.2 = (bf16[64,2048]{1,0:T(8,128)(2,1)S(1)}, bf16[64,2048]{1,0:T(8,128)(2,1)S(1)}, u32[]{:S(2)}, u32[]{:S(2)}) collective-permute-start(bf16[64,2048]{1,0:T(8,128)(2,1)S(1)} %collective-permute-done.refs_4_), channel_id=1, source_target_pairs={{0,2},{2,4},{4,6},{6,8},{8,10},{10,12},{12,14},{14,0},{1,3},{3,5},... | collective-permute-start | bytes 786440 | tf_op jit(solution)/shard_map/ppermute | solution.py:111
  15.5 12.1 %collective-permute-start.5 = (bf16[64,2048]{1,0:T(8,128)(2,1)S(1)}, bf16[64,2048]{1,0:T(8,128)(2,1)S(1)}, u32[]{:S(2)}, u32[]{:S(2)}) collective-permute-start(bf16[64,2048]{1,0:T(8,128)(2,1)S(1)} %collective-permute-done.1.refs_5_), channel_id=1, source_target_pairs={{0,14},{2,0},{4,2},{6,4},{8,6},{10,8},{12,10},{14,12},{1,15},{3,1}... | collective-permute-start | bytes 786440 | tf_op jit(solution)/shard_map/ppermute | solution.py:111
  18.2 27.0 %all-to-all-start = ((bf16[16,16,2048]{2,1,0:T(8,128)(2,1)}), bf16[16,16,2048]{2,1,0:T(8,128)(2,1)S(1)}, u32[]{:S(2)}, u32[]{:S(2)}) async-start(bf16[16,16,2048]{2,1,0:T(8,128)(2,1)} %bitcast.4), calls=%async_computation | async-start | bytes 2097152 | tf_op jit(solution)/shard_map/all_to_all | solution.py:106
  27.6 9.2 %collective-permute-start.3 = (bf16[64,2048]{1,0:T(8,128)(2,1)S(1)}, bf16[64,2048]{1,0:T(8,128)(2,1)S(1)}, u32[]{:S(2)}, u32[]{:S(2)}) collective-permute-start(bf16[64,2048]{1,0:T(8,128)(2,1)S(1)} %collective-permute-done.2.refs_6_), channel_id=1, source_target_pairs={{0,2},{2,4},{4,6},{6,8},{8,10},{10,12},{12,14},{14,0},{1,3},{3,5},... | collective-permute-start | bytes 786440 | tf_op jit(solution)/shard_map/ppermute | solution.py:111
  27.7 9.2 %collective-permute-start.6 = (bf16[64,2048]{1,0:T(8,128)(2,1)S(1)}, bf16[64,2048]{1,0:T(8,128)(2,1)S(1)}, u32[]{:S(2)}, u32[]{:S(2)}) collective-permute-start(bf16[64,2048]{1,0:T(8,128)(2,1)S(1)} %collective-permute-done.5.refs_7_), channel_id=1, source_target_pairs={{0,14},{2,0},{4,2},{6,4},{8,6},{10,8},{12,10},{14,12},{1,15},{3,1}... | collective-permute-start | bytes 786440 | tf_op jit(solution)/shard_map/ppermute | solution.py:111
  36.7 5.4 %collective-permute-start.4 = (bf16[32,2048]{1,0:T(8,128)(2,1)S(1)}, bf16[32,2048]{1,0:T(8,128)(2,1)S(1)}, u32[]{:S(2)}, u32[]{:S(2)}) collective-permute-start(bf16[32,2048]{1,0:T(8,128)(2,1)S(1)} %slice.24), channel_id=1, source_target_pairs={{0,2},{2,4},{4,6},{6,8},{8,10},{10,12},{12,14},{14,0},{1,3},{3,5},... | collective-permute-start | bytes 393224 | tf_op jit(solution)/shard_map/ppermute | solution.py:111
  36.9 5.3 %collective-permute-start.7 = (bf16[32,2048]{1,0:T(8,128)(2,1)S(1)}, bf16[32,2048]{1,0:T(8,128)(2,1)S(1)}, u32[]{:S(2)}, u32[]{:S(2)}) collective-permute-start(bf16[32,2048]{1,0:T(8,128)(2,1)S(1)} %slice.25), channel_id=1, source_target_pairs={{0,14},{2,0},{4,2},{6,4},{8,6},{10,8},{12,10},{14,12},{1,15},{3,1}... | collective-permute-start | bytes 393224 | tf_op jit(solution)/shard_map/ppermute | solution.py:111
  63.6 7.3 %collective-permute-start.10 = (bf16[8,4224]{1,0:T(8,128)(2,1)}, bf16[8,4224]{1,0:T(8,128)(2,1)S(1)}, u32[]{:S(2)}, u32[]{:S(2)}) collective-permute-start(bf16[8,4224]{1,0:T(8,128)(2,1)} %get-tuple-element.18.refs_1_.refs_5_), channel_id=1, source_target_pairs={{0,8},{4,12},{8,0},{12,4},{1,9},{5,13},{9,1},{13,5},{2,10},{6,14},... | collective-permute-start | bytes 202760 | tf_op jit(solution)/shard_map/ppermute | solution.py:111
  65.0 7.1 %collective-permute-start.9 = (bf16[8,4224]{1,0:T(8,128)(2,1)}, bf16[8,4224]{1,0:T(8,128)(2,1)S(1)}, u32[]{:S(2)}, u32[]{:S(2)}) collective-permute-start(bf16[8,4224]{1,0:T(8,128)(2,1)} %get-tuple-element.18.refs_1_.refs_5_), channel_id=1, source_target_pairs={{0,12},{4,0},{8,4},{12,8},{1,13},{5,1},{9,5},{13,9},{2,14},{6,2},{... | collective-permute-start | bytes 202760 | tf_op jit(solution)/shard_map/ppermute | solution.py:111
  66.3 6.2 %collective-permute-start.8 = (bf16[8,4224]{1,0:T(8,128)(2,1)}, bf16[8,4224]{1,0:T(8,128)(2,1)S(1)}, u32[]{:S(2)}, u32[]{:S(2)}) collective-permute-start(bf16[8,4224]{1,0:T(8,128)(2,1)} %get-tuple-element.18.refs_1_.refs_5_), channel_id=1, source_target_pairs={{0,4},{4,8},{8,12},{12,0},{1,5},{5,9},{9,13},{13,1},{2,6},{6,10},{... | collective-permute-start | bytes 202760 | tf_op jit(solution)/shard_map/ppermute | solution.py:111
  76.1 60.4 %copy-start.1 = (bf16[1,4096,384]{2,1,0:T(8,128)(2,1)S(1)}, bf16[1,4096,384]{2,1,0:T(8,128)(2,1)}, u32[]{:S(2)}) copy-start(bf16[1,4096,384]{2,1,0:T(8,128)(2,1)} %refs_1_.1) | copy-start | bytes 9437188
  76.1 60.4 %copy-start.2 = (bf16[1,4096,384]{2,1,0:T(8,128)(2,1)S(1)}, bf16[1,4096,384]{2,1,0:T(8,128)(2,1)}, u32[]{:S(2)}) copy-start(bf16[1,4096,384]{2,1,0:T(8,128)(2,1)} %refs_2_.1) | copy-start | bytes 9437188
  201.7 11.7 %copy-start.3 = (f32[8,4096]{1,0:T(8,128)S(1)}, f32[8,4096]{1,0:T(8,128)}, u32[]{:S(2)}) copy-start(f32[8,4096]{1,0:T(8,128)} %get-tuple-element.17) | copy-start | bytes 393220
  202.6 7.2 %collective-permute-start.11 = (bf16[8,4096]{1,0:T(8,128)(2,1)S(1)}, bf16[8,4096]{1,0:T(8,128)(2,1)S(1)}, u32[]{:S(2)}, u32[]{:S(2)}) collective-permute-start(bf16[8,4096]{1,0:T(8,128)(2,1)S(1)} %get-tuple-element.21), channel_id=1, source_target_pairs={{0,8},{4,12},{8,0},{12,4},{1,9},{5,13},{9,1},{13,5},{2,10},{6,14},... | collective-permute-start | bytes 196616 | tf_op jit(solution)/shard_map/ppermute | solution.py:111
  206.6 6.8 %collective-permute-start.13 = (bf16[8,4096]{1,0:T(8,128)(2,1)S(1)}, bf16[8,4096]{1,0:T(8,128)(2,1)S(1)}, u32[]{:S(2)}, u32[]{:S(2)}) collective-permute-start(bf16[8,4096]{1,0:T(8,128)(2,1)S(1)} %get-tuple-element.22), channel_id=1, source_target_pairs={{0,12},{4,0},{8,4},{12,8},{1,13},{5,1},{9,5},{13,9},{2,14},{6,2},{... | collective-permute-start | bytes 196616 | tf_op jit(solution)/shard_map/ppermute | solution.py:111
  206.6 6.8 %collective-permute-start.12 = (bf16[8,4096]{1,0:T(8,128)(2,1)S(1)}, bf16[8,4096]{1,0:T(8,128)(2,1)S(1)}, u32[]{:S(2)}, u32[]{:S(2)}) collective-permute-start(bf16[8,4096]{1,0:T(8,128)(2,1)S(1)} %get-tuple-element.23), channel_id=1, source_target_pairs={{0,4},{4,8},{8,12},{12,0},{1,5},{5,9},{9,13},{13,1},{2,6},{6,10},{... | collective-permute-start | bytes 196616 | tf_op jit(solution)/shard_map/ppermute | solution.py:111

commit v7 on v6

--- a/solution.py
+++ b/solution.py
@@ -155,13 +155,17 @@
 
 
 def pick_kernel(top_k, blocks, quad_ref, *refs):
-    choices_refs, pool_refs = refs[:blocks], refs[blocks : 2 * blocks]
-    out_ref, scaled_ref, picks = refs[2 * blocks :]
+    pool_refs = refs[:blocks]
+    out_ref, scaled_ref, picks = refs[blocks:]
     count, tokens = picks.shape
+    block = out_ref.shape[1]
+    width = pool_refs[0].shape[1] - LANES
 
     @pl.when(pl.program_id(0) == 0)
     def _():
-        table = jnp.concatenate([ref[...].astype(jnp.float32) for ref in choices_refs], axis=0).T
+        table = jnp.concatenate(
+            [ref[:, width:].astype(jnp.float32) for ref in pool_refs], axis=0
+        ).T
         slot = lax.broadcasted_iota(jnp.int32, (count, tokens), 0)
         token = lax.broadcasted_iota(jnp.int32, (count, tokens), 1)
         far = slot // SLOTS
@@ -189,7 +193,8 @@
         scaled_ref[...] = jnp.where(chosen, share, 0.0).astype(jnp.bfloat16)
         picks[...] = jnp.where(chosen, 1.0, 0.0).astype(jnp.bfloat16)
 
-    pool = jnp.concatenate([ref[...] for ref in pool_refs], axis=0)
+    span = pl.ds(pl.multiple_of(pl.program_id(0) * block, block), block)
+    pool = jnp.concatenate([ref[:, span] for ref in pool_refs], axis=0)
     out_ref[...] = jnp.dot(picks[...], pool, preferred_element_type=jnp.float32).astype(
         jnp.bfloat16
     )
@@ -209,8 +214,7 @@
         ),
         grid=(width // block,),
         in_specs=[pl.BlockSpec(memory_space=pltpu.SMEM)]
-        + [pl.BlockSpec((rows, LANES), lambda s: (0, width // LANES))] * blocks
-        + [pl.BlockSpec((rows, block), lambda s: (0, s))] * blocks,
+        + [pl.BlockSpec(memory_space=pltpu.VMEM)] * blocks,
         out_specs=(
             pl.BlockSpec((count, block), lambda s: (0, s)),
             pl.BlockSpec((count, tokens), lambda s: (0, 0)),
@@ -219,7 +223,7 @@
         compiler_params=pltpu.CompilerParams(
             dimension_semantics=("arbitrary",), vmem_limit_bytes=16 << 20
         ),
-    )(quad, *held(pltpu.HBM, pool[0]), *pool[1:], *held(pltpu.HBM, pool[0]), *pool[1:])
+    )(quad, *held(pltpu.VMEM, *pool))
 
 
 def ffn_kernel(unit_steps, rows_ref, gate_ref, up_ref, down_hbm, out_ref, active, down_ref, arrival):
@@ -259,7 +263,7 @@
 def expert_rows(rows, gate, up, down):
     count, width = rows.shape
     units = gate.shape[2]
-    columns = 1024
+    columns = 2048
     steps = units // LANES
     whole = pl.BlockSpec(memory_space=pltpu.VMEM)
     return pl.pallas_call(

time: 215 us -> 214 us (level)
  no operation moved by 1% of the time
where the time goes in v7:
time: 214 us
  blocking collectives  134 us (63%)
  starting transfers between devices  34.3 us (16%)
  waiting for transfers between devices  22.7 us (11%)
  Pallas kernels  16.8 us (8%)
  other arithmetic  2.7 us (1%)
  local copies, waits for them, and re-layouts  2.56 us (1%)
    all_to_all x3, blocking collectives, swap(): return lax.all_to_all(blocks, axes, split_axis=0, concat_axis=0, tiled=True)  134 us
    ppermute x14, starting transfers between devices, shift(): lax.ppermute(block, axis, [(at, (at + by) % count) for at in range(count)])  24.9 us
    ppermute x14, waiting for transfers between devices, shift(): lax.ppermute(block, axis, [(at, (at + by) % count) for at in range(count)])  20.2 us
    all_to_all x1, starting transfers between devices, swap(): return lax.all_to_all(blocks, axes, split_axis=0, concat_axis=0, tiled=True)  9.37 us
    pallas_call x1, Pallas kernels, expert_rows(): pl.pallas_call(lambda *refs: ffn_kernel(steps, *refs), out_shape=jax.Shap...  6.72 us
  transfers between devices with their start and end apart: 15, of which 9 were waited for; matrix products, arithmetic and copies ran while one was open for 1% of the time, Pallas kernels for 2%

profile of v7, /device:TPU:1, one launch (start us, length us, event | category | flops | bytes accessed | tf_op | source)
XLA Modules:
  0.0 213.5 jit_solution(3934095542091582655)
XLA Ops:
  1.0 6.5 %collective-permute-start.1 = (bf16[64,2048]{1,0:T(8,128)(2,1)S(1)}, bf16[64,2048]{1,0:T(8,128)(2,1)S(1)}, u32[]{:S(2)}, u32[]{:S(2)}) collective-permute-start(bf16[64,2048]{1,0:T(8,128)(2,1)S(1)} %dynamic-slice_bitcast_fusion.refs_3_), channel_id=1, source_target_pairs={{0,14},{2,0},{4,2},{6,4},{8,6},{10,8},{12,10},{14,12},{1,15},{3,1}... | collective-permute-start | bytes 786440 | tf_op jit(solution)/shard_map/ppermute | solution.py:111
  9.5 3.6 %shard_map.136 = bf16[2,8,16,2048]{3,2,1,0:T(8,128)(2,1)} custom-call(bf16[16,32,128]{2,1,0:T(8,128)(2,1)} %queries_ref.1, bf16[16,256,128]{2,1,0:T(8,128)(2,1)} %bitcast.24, bf16[16,256,128]{2,1,0:T(8,128)(2,1)} %bitcast.25, bf16[16,2,128]{2,1,0:T(2,128)(2,1)} %new_keys_ref.1, bf16[16,2,128]{2,1,0:T(2,128)(2,1)} %new_values_ref.1, s32[16]{0:T(128)S(1)} %copy-done.1), custom_call_target="tpu_custom_call" | custom-call | tf_op jit(solution)/shard_map/pallas_call | solution.py:80
  13.7 1.8 collective-permute-done.refs_4_
  15.5 2.7 %collective-permute-start.5 = (bf16[64,2048]{1,0:T(8,128)(2,1)S(1)}, bf16[64,2048]{1,0:T(8,128)(2,1)S(1)}, u32[]{:S(2)}, u32[]{:S(2)}) collective-permute-start(bf16[64,2048]{1,0:T(8,128)(2,1)S(1)} %collective-permute-done.1.refs_5_), channel_id=1, source_target_pairs={{0,14},{2,0},{4,2},{6,4},{8,6},{10,8},{12,10},{14,12},{1,15},{3,1}... | collective-permute-start | bytes 786440 | tf_op jit(solution)/shard_map/ppermute | solution.py:111
  18.2 9.4 %all-to-all-start = ((bf16[16,16,2048]{2,1,0:T(8,128)(2,1)}), bf16[16,16,2048]{2,1,0:T(8,128)(2,1)S(1)}, u32[]{:S(2)}, u32[]{:S(2)}) async-start(bf16[16,16,2048]{2,1,0:T(8,128)(2,1)} %bitcast.4), calls=%async_computation | async-start | bytes 2097152 | tf_op jit(solution)/shard_map/all_to_all | solution.py:106
  27.7 2.7 %collective-permute-start.6 = (bf16[64,2048]{1,0:T(8,128)(2,1)S(1)}, bf16[64,2048]{1,0:T(8,128)(2,1)S(1)}, u32[]{:S(2)}, u32[]{:S(2)}) collective-permute-start(bf16[64,2048]{1,0:T(8,128)(2,1)S(1)} %collective-permute-done.5.refs_7_), channel_id=1, source_target_pairs={{0,14},{2,0},{4,2},{6,4},{8,6},{10,8},{12,10},{14,12},{1,15},{3,1}... | collective-permute-start | bytes 786440 | tf_op jit(solution)/shard_map/ppermute | solution.py:111
  30.4 6.4 %collective-permute-done.3.refs_8_ = bf16[64,2048]{1,0:T(8,128)(2,1)S(1)} collective-permute-done((bf16[64,2048]{1,0:T(8,128)(2,1)S(1)}, bf16[64,2048]{1,0:T(8,128)(2,1)S(1)}, u32[]{:S(2)}, u32[]{:S(2)}) %collective-permute-start.3) | collective-permute-done | bytes 262176 | tf_op jit(solution)/shard_map/ppermute | solution.py:111
  36.9 2.7 %collective-permute-start.7 = (bf16[32,2048]{1,0:T(8,128)(2,1)S(1)}, bf16[32,2048]{1,0:T(8,128)(2,1)S(1)}, u32[]{:S(2)}, u32[]{:S(2)}) collective-permute-start(bf16[32,2048]{1,0:T(8,128)(2,1)S(1)} %slice.25), channel_id=1, source_target_pairs={{0,14},{2,0},{4,2},{6,4},{8,6},{10,8},{12,10},{14,12},{1,15},{3,1}... | collective-permute-start | bytes 393224 | tf_op jit(solution)/shard_map/ppermute | solution.py:111
  39.6 2.6 %collective-permute-done.4.top_ref.refs_10_ = bf16[32,2048]{1,0:T(8,128)(2,1)S(1)} collective-permute-done((bf16[32,2048]{1,0:T(8,128)(2,1)S(1)}, bf16[32,2048]{1,0:T(8,128)(2,1)S(1)}, u32[]{:S(2)}, u32[]{:S(2)}) %collective-permute-start.4) | collective-permute-done | bytes 131104 | tf_op jit(solution)/shard_map/ppermute | solution.py:111
  42.8 2.5 %all-to-all-done = bf16[16,16,2048]{2,1,0:T(8,128)(2,1)S(1)} async-done(((bf16[16,16,2048]{2,1,0:T(8,128)(2,1)}), bf16[16,16,2048]{2,1,0:T(8,128)(2,1)S(1)}, u32[]{:S(2)}, u32[]{:S(2)}) %all-to-all-start) | async-done | bytes 1048608 | tf_op jit(solution)/shard_map/all_to_all | solution.py:106
  45.2 1.6 shard_map.138
  46.8 15.1 %all_to_all.20 = bf16[32,8,512]{2,1,0:T(8,128)(2,1)S(1)} all-to-all(bf16[32,8,512]{2,1,0:T(8,128)(2,1)} %bitcast.23), channel_id=1, replica_groups=mesh['role'=2,'xh'=2,'y'=4,'zq'=4,'zp'=2,'head'=2] {'role','xh','y','head'}, dimensions={0} | all-to-all | bytes 524288 | tf_op jit(solution)/shard_map/all_to_all | solution.py:106
  62.0 1.6 shard_map.139
  63.6 1.4 collective-permute-start.10
  65.0 1.3 collective-permute-start.9
  67.4 3.5 %collective-permute-done.10.refs_4_ = bf16[8,4224]{1,0:T(8,128)(2,1)S(1)} collective-permute-done((bf16[8,4224]{1,0:T(8,128)(2,1)}, bf16[8,4224]{1,0:T(8,128)(2,1)S(1)}, u32[]{:S(2)}, u32[]{:S(2)}) %collective-permute-start.10) | collective-permute-done | bytes 67616 | tf_op jit(solution)/shard_map/ppermute | solution.py:111
  70.9 1.3 collective-permute-done.9.refs_3_
  73.4 2.7 %shard_map.140 = (bf16[512,4096]{1,0:T(8,128)(2,1)S(1)}, bf16[512,32]{1,0:T(8,128)(2,1)S(1)}) custom-call(s32[1]{0:T(128)} %bitcast.9.refs_0_, bf16[8,4224]{1,0:T(8,128)(2,1)S(1)} %copy-done, bf16[8,4224]{1,0:T(8,128)(2,1)S(1)} %collective-permute-done.8.refs_2_, bf16[8,4224]{1,0:T(8,128)(2,1)S(1)} %collective-permute-done.9.refs_3_, ...), custom_call_target="tpu_custom_call" | custom-call | tf_op jit(solution)/shard_map/pallas_call | solution.py:209
  76.1 60.4 %all_to_all.21 = bf16[64,8,4096]{2,1,0:T(8,128)(2,1)S(1)} all-to-all(bf16[64,8,4096]{2,1,0:T(8,128)(2,1)S(1)} %bitcast.19), channel_id=1, replica_groups=mesh['role'=2,'xh'=2,'y'=4,'zq'=4,'zp'=2,'head'=2] {'xh','head','y','zp'..., dimensions={0} | all-to-all | bytes 8388608 | tf_op jit(solution)/shard_map/all_to_all | solution.py:106
  136.4 6.7 %shard_map.141 = bf16[512,4096]{1,0:T(8,128)(2,1)S(1)} custom-call(bf16[512,4096]{1,0:T(8,128)(2,1)S(1)} %bitcast.20, bf16[1,4096,384]{2,1,0:T(8,128)(2,1)S(1)} %copy-done.2, bf16[1,4096,384]{2,1,0:T(8,128)(2,1)S(1)} %copy-done.3, bf16[1,384,4096]{2,1,0:T(8,128)(2,1)} %refs_3_.1), custom_call_target="tpu_custom_call" | custom-call | flops 4831838208 | bytes 17825792 | tf_op jit(solution)/shard_map/pallas_call | solution.py:269
  143.2 58.0 %all_to_all.22 = bf16[64,8,4096]{2,1,0:T(8,128)(2,1)S(1)} all-to-all(bf16[64,8,4096]{2,1,0:T(8,128)(2,1)S(1)} %bitcast.21), channel_id=1, replica_groups=mesh['role'=2,'xh'=2,'y'=4,'zq'=4,'zp'=2,'head'=2] {'xh','head','y','zp'..., dimensions={0} | all-to-all | bytes 8388608 | tf_op jit(solution)/shard_map/all_to_all | solution.py:106
  202.1 4.0 %collective-permute-start.11 = (bf16[8,4096]{1,0:T(8,128)(2,1)S(1)}, bf16[8,4096]{1,0:T(8,128)(2,1)S(1)}, u32[]{:S(2)}, u32[]{:S(2)}) collective-permute-start(bf16[8,4096]{1,0:T(8,128)(2,1)S(1)} %get-tuple-element.21), channel_id=1, source_target_pairs={{0,8},{4,12},{8,0},{12,4},{1,9},{5,13},{9,1},{13,5},{2,10},{6,14},... | collective-permute-start | bytes 196616 | tf_op jit(solution)/shard_map/ppermute | solution.py:111
  206.1 2.4 %collective-permute-start.12 = (bf16[8,4096]{1,0:T(8,128)(2,1)S(1)}, bf16[8,4096]{1,0:T(8,128)(2,1)S(1)}, u32[]{:S(2)}, u32[]{:S(2)}) collective-permute-start(bf16[8,4096]{1,0:T(8,128)(2,1)S(1)} %get-tuple-element.23), channel_id=1, source_target_pairs={{0,4},{4,8},{8,12},{12,0},{1,5},{5,9},{9,13},{13,1},{2,6},{6,10},{... | collective-permute-start | bytes 196616 | tf_op jit(solution)/shard_map/ppermute | solution.py:111
  209.3 3.6 %collective-permute-done.13 = bf16[8,4096]{1,0:T(8,128)(2,1)S(1)} collective-permute-done((bf16[8,4096]{1,0:T(8,128)(2,1)S(1)}, bf16[8,4096]{1,0:T(8,128)(2,1)S(1)}, u32[]{:S(2)}, u32[]{:S(2)}) %collective-permute-start.13) | collective-permute-done | bytes 65568 | tf_op jit(solution)/shard_map/ppermute | solution.py:111
  (34 shorter events, 9.1 us)
Async XLA Ops:
  1.0 12.7 %collective-permute-start.1 = (bf16[64,2048]{1,0:T(8,128)(2,1)S(1)}, bf16[64,2048]{1,0:T(8,128)(2,1)S(1)}, u32[]{:S(2)}, u32[]{:S(2)}) collective-permute-start(bf16[64,2048]{1,0:T(8,128)(2,1)S(1)} %dynamic-slice_bitcast_fusion.refs_3_), channel_id=1, source_target_pairs={{0,14},{2,0},{4,2},{6,4},{8,6},{10,8},{12,10},{14,12},{1,15},{3,1}... | collective-permute-start | bytes 786440 | tf_op jit(solution)/shard_map/ppermute | solution.py:111
  7.5 8.1 %collective-permute-start = (bf16[64,2048]{1,0:T(8,128)(2,1)S(1)}, bf16[64,2048]{1,0:T(8,128)(2,1)S(1)}, u32[]{:S(2)}, u32[]{:S(2)}) collective-permute-start(bf16[64,2048]{1,0:T(8,128)(2,1)S(1)} %dynamic-slice_bitcast_fusion.refs_3_), channel_id=1, source_target_pairs={{0,2},{2,4},{4,6},{6,8},{8,10},{10,12},{12,14},{14,0},{1,3},{3,5},... | collective-permute-start | bytes 786440 | tf_op jit(solution)/shard_map/ppermute | solution.py:111
  8.8 0.7 copy-start.1
  15.5 12.1 %collective-permute-start.2 = (bf16[64,2048]{1,0:T(8,128)(2,1)S(1)}, bf16[64,2048]{1,0:T(8,128)(2,1)S(1)}, u32[]{:S(2)}, u32[]{:S(2)}) collective-permute-start(bf16[64,2048]{1,0:T(8,128)(2,1)S(1)} %collective-permute-done.refs_4_), channel_id=1, source_target_pairs={{0,2},{2,4},{4,6},{6,8},{8,10},{10,12},{12,14},{14,0},{1,3},{3,5},... | collective-permute-start | bytes 786440 | tf_op jit(solution)/shard_map/ppermute | solution.py:111
  15.5 12.1 %collective-permute-start.5 = (bf16[64,2048]{1,0:T(8,128)(2,1)S(1)}, bf16[64,2048]{1,0:T(8,128)(2,1)S(1)}, u32[]{:S(2)}, u32[]{:S(2)}) collective-permute-start(bf16[64,2048]{1,0:T(8,128)(2,1)S(1)} %collective-permute-done.1.refs_5_), channel_id=1, source_target_pairs={{0,14},{2,0},{4,2},{6,4},{8,6},{10,8},{12,10},{14,12},{1,15},{3,1}... | collective-permute-start | bytes 786440 | tf_op jit(solution)/shard_map/ppermute | solution.py:111
  18.2 27.0 %all-to-all-start = ((bf16[16,16,2048]{2,1,0:T(8,128)(2,1)}), bf16[16,16,2048]{2,1,0:T(8,128)(2,1)S(1)}, u32[]{:S(2)}, u32[]{:S(2)}) async-start(bf16[16,16,2048]{2,1,0:T(8,128)(2,1)} %bitcast.4), calls=%async_computation | async-start | bytes 2097152 | tf_op jit(solution)/shard_map/all_to_all | solution.py:106
  27.6 9.2 %collective-permute-start.3 = (bf16[64,2048]{1,0:T(8,128)(2,1)S(1)}, bf16[64,2048]{1,0:T(8,128)(2,1)S(1)}, u32[]{:S(2)}, u32[]{:S(2)}) collective-permute-start(bf16[64,2048]{1,0:T(8,128)(2,1)S(1)} %collective-permute-done.2.refs_6_), channel_id=1, source_target_pairs={{0,2},{2,4},{4,6},{6,8},{8,10},{10,12},{12,14},{14,0},{1,3},{3,5},... | collective-permute-start | bytes 786440 | tf_op jit(solution)/shard_map/ppermute | solution.py:111
  27.7 9.2 %collective-permute-start.6 = (bf16[64,2048]{1,0:T(8,128)(2,1)S(1)}, bf16[64,2048]{1,0:T(8,128)(2,1)S(1)}, u32[]{:S(2)}, u32[]{:S(2)}) collective-permute-start(bf16[64,2048]{1,0:T(8,128)(2,1)S(1)} %collective-permute-done.5.refs_7_), channel_id=1, source_target_pairs={{0,14},{2,0},{4,2},{6,4},{8,6},{10,8},{12,10},{14,12},{1,15},{3,1}... | collective-permute-start | bytes 786440 | tf_op jit(solution)/shard_map/ppermute | solution.py:111
  36.7 5.4 %collective-permute-start.4 = (bf16[32,2048]{1,0:T(8,128)(2,1)S(1)}, bf16[32,2048]{1,0:T(8,128)(2,1)S(1)}, u32[]{:S(2)}, u32[]{:S(2)}) collective-permute-start(bf16[32,2048]{1,0:T(8,128)(2,1)S(1)} %slice.24), channel_id=1, source_target_pairs={{0,2},{2,4},{4,6},{6,8},{8,10},{10,12},{12,14},{14,0},{1,3},{3,5},... | collective-permute-start | bytes 393224 | tf_op jit(solution)/shard_map/ppermute | solution.py:111
  36.9 5.3 %collective-permute-start.7 = (bf16[32,2048]{1,0:T(8,128)(2,1)S(1)}, bf16[32,2048]{1,0:T(8,128)(2,1)S(1)}, u32[]{:S(2)}, u32[]{:S(2)}) collective-permute-start(bf16[32,2048]{1,0:T(8,128)(2,1)S(1)} %slice.25), channel_id=1, source_target_pairs={{0,14},{2,0},{4,2},{6,4},{8,6},{10,8},{12,10},{14,12},{1,15},{3,1}... | collective-permute-start | bytes 393224 | tf_op jit(solution)/shard_map/ppermute | solution.py:111
  63.6 7.3 %collective-permute-start.10 = (bf16[8,4224]{1,0:T(8,128)(2,1)}, bf16[8,4224]{1,0:T(8,128)(2,1)S(1)}, u32[]{:S(2)}, u32[]{:S(2)}) collective-permute-start(bf16[8,4224]{1,0:T(8,128)(2,1)} %get-tuple-element.18.refs_1_), channel_id=1, source_target_pairs={{0,8},{4,12},{8,0},{12,4},{1,9},{5,13},{9,1},{13,5},{2,10},{6,14},... | collective-permute-start | bytes 202760 | tf_op jit(solution)/shard_map/ppermute | solution.py:111
  65.0 7.1 %collective-permute-start.9 = (bf16[8,4224]{1,0:T(8,128)(2,1)}, bf16[8,4224]{1,0:T(8,128)(2,1)S(1)}, u32[]{:S(2)}, u32[]{:S(2)}) collective-permute-start(bf16[8,4224]{1,0:T(8,128)(2,1)} %get-tuple-element.18.refs_1_), channel_id=1, source_target_pairs={{0,12},{4,0},{8,4},{12,8},{1,13},{5,1},{9,5},{13,9},{2,14},{6,2},{... | collective-permute-start | bytes 202760 | tf_op jit(solution)/shard_map/ppermute | solution.py:111
  66.3 6.2 %collective-permute-start.8 = (bf16[8,4224]{1,0:T(8,128)(2,1)}, bf16[8,4224]{1,0:T(8,128)(2,1)S(1)}, u32[]{:S(2)}, u32[]{:S(2)}) collective-permute-start(bf16[8,4224]{1,0:T(8,128)(2,1)} %get-tuple-element.18.refs_1_), channel_id=1, source_target_pairs={{0,4},{4,8},{8,12},{12,0},{1,5},{5,9},{9,13},{13,1},{2,6},{6,10},{... | collective-permute-start | bytes 202760 | tf_op jit(solution)/shard_map/ppermute | solution.py:111
  72.5 0.9 copy-start
  76.1 60.4 %copy-start.2 = (bf16[1,4096,384]{2,1,0:T(8,128)(2,1)S(1)}, bf16[1,4096,384]{2,1,0:T(8,128)(2,1)}, u32[]{:S(2)}) copy-start(bf16[1,4096,384]{2,1,0:T(8,128)(2,1)} %refs_1_.1) | copy-start | bytes 9437188
  76.1 60.4 %copy-start.3 = (bf16[1,4096,384]{2,1,0:T(8,128)(2,1)S(1)}, bf16[1,4096,384]{2,1,0:T(8,128)(2,1)}, u32[]{:S(2)}) copy-start(bf16[1,4096,384]{2,1,0:T(8,128)(2,1)} %refs_2_.1) | copy-start | bytes 9437188
  201.2 11.7 %copy-start.4 = (f32[8,4096]{1,0:T(8,128)S(1)}, f32[8,4096]{1,0:T(8,128)}, u32[]{:S(2)}) copy-start(f32[8,4096]{1,0:T(8,128)} %get-tuple-element.17) | copy-start | bytes 393220
  202.1 7.2 %collective-permute-start.11 = (bf16[8,4096]{1,0:T(8,128)(2,1)S(1)}, bf16[8,4096]{1,0:T(8,128)(2,1)S(1)}, u32[]{:S(2)}, u32[]{:S(2)}) collective-permute-start(bf16[8,4096]{1,0:T(8,128)(2,1)S(1)} %get-tuple-element.21), channel_id=1, source_target_pairs={{0,8},{4,12},{8,0},{12,4},{1,9},{5,13},{9,1},{13,5},{2,10},{6,14},... | collective-permute-start | bytes 196616 | tf_op jit(solution)/shard_map/ppermute | solution.py:111
  206.1 6.7 %collective-permute-start.13 = (bf16[8,4096]{1,0:T(8,128)(2,1)S(1)}, bf16[8,4096]{1,0:T(8,128)(2,1)S(1)}, u32[]{:S(2)}, u32[]{:S(2)}) collective-permute-start(bf16[8,4096]{1,0:T(8,128)(2,1)S(1)} %get-tuple-element.22), channel_id=1, source_target_pairs={{0,12},{4,0},{8,4},{12,8},{1,13},{5,1},{9,5},{13,9},{2,14},{6,2},{... | collective-permute-start | bytes 196616 | tf_op jit(solution)/shard_map/ppermute | solution.py:111
  206.1 6.7 %collective-permute-start.12 = (bf16[8,4096]{1,0:T(8,128)(2,1)S(1)}, bf16[8,4096]{1,0:T(8,128)(2,1)S(1)}, u32[]{:S(2)}, u32[]{:S(2)}) collective-permute-start(bf16[8,4096]{1,0:T(8,128)(2,1)S(1)} %get-tuple-element.23), channel_id=1, source_target_pairs={{0,4},{4,8},{8,12},{12,0},{1,5},{5,9},{9,13},{13,1},{2,6},{6,10},{... | collective-permute-start | bytes 196616 | tf_op jit(solution)/shard_map/ppermute | solution.py:111
